TPU v7x, 32 devices: a whole 2x2x4 slice. The times are simulated.
32 devices in a mesh: dp: 2 (over x), seq: 4 (over y, core), tensor: 4 (over z).
Axes of the slice: x: 2, y: 2, z: 4, core: 2. Of those that a mesh axis runs over, the one named last changes fastest.
Arguments:
- inputs: bfloat16 [4, 2048, 1024], P('dp', ('seq', 'tensor')), may hold values from -6 to 6
- seg_starts: int32 [4, 4], P('dp', 'seq'), may hold values from 0 to 256, as said below
- lengths: int32 [4], P('dp'), may hold values from 512 to 2048, as said below
- init_state: float32 [512, 1024], P('tensor'), may hold values from -6 to 6
- attn_gain: float32 [1024], replicated, may hold values from 0.5 to 1.5
- state_gain: float32 [1024], replicated, may hold values from 0.5 to 1.5
- mlp_gain: float32 [1024], replicated, may hold values from 0.5 to 1.5
- w_query: bfloat16 [1024, 1024], P(None, 'tensor'), may hold values from -0.1875 to 0.1875
- w_key: bfloat16 [1024, 1024], P(None, 'tensor'), may hold values from -0.1875 to 0.1875
- w_value: bfloat16 [1024, 1024], P(None, 'tensor'), may hold values from -0.1875 to 0.1875
- w_out: bfloat16 [1024, 1024], P('tensor'), may hold values from -4 to 4
- w_squery: bfloat16 [1024, 1024], P(None, 'tensor'), may hold values from -0.1875 to 0.1875
- w_sout: bfloat16 [1024, 1024], P('tensor'), may hold values from -4 to 4
- w_up: bfloat16 [1024, 4096], P(None, 'tensor'), may hold values from -0.1875 to 0.1875
- w_down: bfloat16 [4096, 1024], P('tensor'), may hold values from -0.125 to 0.125
- rel_bias: float32 [32, 8], P(None, 'tensor'), may hold values from -4 to 4
- gate_bias: float32 [1024], replicated, may hold values from -3 to 3
- out_cot: bfloat16 [4, 2048, 1024], P('dp', ('seq', 'tensor')), may hold values from -6 to 6
- state_cot: bfloat16 [4, 4, 512, 1024], P('dp', 'seq', 'tensor'), may hold values from -6 to 6
Outputs:
- tokens_out: bfloat16 [4, 2048, 1024], P('dp', ('seq', 'tensor'))
- states_out: float32 [4, 4, 512, 1024], P('dp', 'seq', 'tensor')
- inputs_grad: float32 [4, 2048, 1024], P('dp', ('seq', 'tensor'))
- state_grad: float32 [512, 1024], P('tensor')
- attn_gain_grad: float32 [1024], replicated
- state_gain_grad: float32 [1024], replicated
- mlp_gain_grad: float32 [1024], replicated
- query_grad: float32 [1024, 1024], P(None, 'tensor')
- key_grad: float32 [1024, 1024], P(None, 'tensor')
- value_grad: float32 [1024, 1024], P(None, 'tensor')
- out_grad: float32 [1024, 1024], P('tensor')
- squery_grad: float32 [1024, 1024], P(None, 'tensor')
- sout_grad: float32 [1024, 1024], P('tensor')
- up_grad: float32 [1024, 4096], P(None, 'tensor')
- down_grad: float32 [4096, 1024], P('tensor')
- bias_grad: float32 [32, 8], P(None, 'tensor')
- gate_grad: float32 [1024], replicated
Inputs may be any that keep to these rules, and one draw needn't show every extreme that they name: `seg_starts`: each block's bidirectional segment starts at this offset inside the block and covers 256 tokens. `lengths`: tokens at or past a sequence's length are padding that no key may show.
All inputs are finite; a program needn't handle non-finite values.
Results may differ from a plain program's by a relative error of at most 0.025.
Values may be sent and summed in bfloat16 or wider, within the bound.
A program may use at most 192 MiB of HBM per device.

v0:
```python
import jax
import jax.numpy as jnp
from jax import lax
from jax.sharding import PartitionSpec as P

D = 1024
HEAD_DIM = 128
STATES = 512
BLOCK = 512
SEG = 256
BUCKETS = 32


norm_eps = 1e-06
masked_score = -1e30
bucket_edges = (12, 16, 23, 32, 46, 64, 91)


def passed_along(value, axis, steps):
    count = lax.axis_size(axis)
    leading, last = (max(0, -steps), min(count, count - steps))
    return lax.ppermute(value, axis, [(source, source + steps) for source in range(leading, last)])


def bucket_of(relative):
    distance = jnp.abs(relative)
    far_bucket = 8 + sum(((distance >= boundary).astype(jnp.int32) for boundary in bucket_edges))
    near_far = jnp.where(distance < 8, distance, far_bucket)
    return near_far + 16 * (relative > 0).astype(jnp.int32)


def token_mask(seg_start, seq_length, block_index):
    positions = jnp.arange(BLOCK)
    offset = block_index * BLOCK
    prev_valid = (block_index > 0) & (offset - BLOCK + positions < seq_length)
    cur_valid = offset + positions < seq_length
    inside = (positions >= seg_start) & (positions < seg_start + SEG)
    prev_mask = (positions[None, :] > positions[:, None]) & prev_valid[None, :]
    cur_mask = (
        (positions[None, :] <= positions[:, None]) | inside[None, :] & inside[:, None]
    ) & cur_valid[None, :]
    state_mask = jnp.ones((BLOCK, STATES), jnp.bool_)
    return jnp.concatenate([prev_mask, cur_mask, state_mask], axis=1)


def state_mask_of(valid_blk):
    batch_count = valid_blk.shape[0]
    block_part = jnp.broadcast_to(valid_blk[:, None, :], (batch_count, STATES, BLOCK))
    return jnp.concatenate([block_part, jnp.ones((batch_count, STATES, STATES), jnp.bool_)], axis=2)


def layer_norm(values, gain_vec):
    centered = values - jnp.mean(values, axis=-1, keepdims=True)
    spread = jnp.mean(centered * centered, axis=-1, keepdims=True)
    return centered * lax.rsqrt(spread + norm_eps) * gain_vec


def norm_back(values, gain_vec, grad_out):
    _, pullback = jax.vjp(layer_norm, values, gain_vec)
    return pullback(grad_out)


def gelu_back(pre_act, grad_out):
    _, pullback = jax.vjp(jax.nn.gelu, pre_act)
    return pullback(grad_out)[0]


def to_low(array_in):
    return array_in.astype(jnp.bfloat16)


def matmul(left, right):
    return jnp.einsum("...k,kn->...n", left, right, preferred_element_type=jnp.float32)


def matmul_t(left, right):
    return jnp.einsum("...n,kn->...k", left, right, preferred_element_type=jnp.float32)


def outer_sum(left, right):
    left_flat = left.reshape(-1, left.shape[-1])
    right_flat = right.reshape(-1, right.shape[-1])
    return lax.dot_general(
        left_flat, right_flat, (((0,), (0,)), ((), ())), preferred_element_type=jnp.float32
    )


def gather_rows(values):
    return lax.all_gather(values, "tensor", axis=1, tiled=True)


def sum_rows(terms):
    return lax.psum_scatter(
        terms.astype(jnp.bfloat16), "tensor", scatter_dimension=1, tiled=True
    ).astype(jnp.float32)


def pass_state(rows_now):
    return passed_along(rows_now.astype(jnp.bfloat16), "seq", 1).astype(rows_now.dtype)


def pass_back(grad_now):
    return passed_along(grad_now.astype(jnp.bfloat16), "seq", -1).astype(grad_now.dtype)


def split_heads(rows_in):
    return rows_in.reshape(rows_in.shape[0], rows_in.shape[1] // HEAD_DIM, HEAD_DIM)


def score_block(query_rows, key_all, bias_all, allowed):
    scores = (
        jnp.einsum(
            "qhd,khd->hqk",
            split_heads(query_rows),
            split_heads(key_all),
            preferred_element_type=jnp.float32,
        )
        * HEAD_DIM ** (-0.5)
        + bias_all
    )
    return jnp.where(allowed[None], scores, masked_score)


def attend_forward(query_rows, key_all, value_all, bias_all, allowed):
    scores = score_block(query_rows, key_all, bias_all, allowed)
    row_max = jnp.max(scores, axis=-1, keepdims=True)
    exp_scores = jnp.exp(scores - row_max)
    row_total = jnp.sum(exp_scores, axis=-1, keepdims=True)
    weight_all = to_low(exp_scores / row_total)
    mixed_out = jnp.einsum(
        "hqk,khd->qhd", weight_all, split_heads(value_all), preferred_element_type=jnp.float32
    )
    return (
        to_low(mixed_out.reshape(query_rows.shape[0], -1)),
        (row_max + jnp.log(row_total))[..., 0],
    )


def attend_back(query_rows, key_all, value_all, bias_all, allowed, log_total, grad_mixed):
    scores = score_block(query_rows, key_all, bias_all, allowed)
    weight_all = jnp.where(allowed[None], jnp.exp(scores - log_total[..., None]), 0.0)
    grad_heads = split_heads(grad_mixed)
    grad_weight = jnp.einsum(
        "qhd,khd->hqk", grad_heads, split_heads(value_all), preferred_element_type=jnp.float32
    )
    row_inner = jnp.sum(weight_all * grad_weight, axis=-1, keepdims=True)
    grad_scores = to_low(weight_all * (grad_weight - row_inner))
    grad_query = jnp.einsum(
        "hqk,khd->qhd", grad_scores, split_heads(key_all), preferred_element_type=jnp.float32
    ) * HEAD_DIM ** (-0.5)
    grad_keys = jnp.einsum(
        "hqk,qhd->khd", grad_scores, split_heads(query_rows), preferred_element_type=jnp.float32
    ) * HEAD_DIM ** (-0.5)
    grad_values = jnp.einsum(
        "hqk,qhd->khd", to_low(weight_all), grad_heads, preferred_element_type=jnp.float32
    )
    return (
        grad_query.reshape(query_rows.shape[0], -1),
        grad_keys.reshape(key_all.shape[0], -1),
        grad_values.reshape(key_all.shape[0], -1),
        grad_scores,
    )


def bias_lookup(rel_bias, rel_table):
    table_heads = jnp.zeros((rel_bias.shape[1],) + rel_table.shape, jnp.float32)
    for bucket_id in range(BUCKETS):
        table_heads = table_heads + jnp.where(
            rel_table[None] == bucket_id, rel_bias[bucket_id][:, None, None], 0.0
        )
    return table_heads


def bias_sums(score_grad, rel_table):
    grad_wide = score_grad.astype(jnp.float32)
    columns = []
    for bucket_id in range(BUCKETS):
        columns.append(
            jnp.sum(jnp.where(rel_table[None, None] == bucket_id, grad_wide, 0.0), axis=(0, 2, 3))
        )
    return jnp.stack(columns, axis=0)


def body(
    inputs,
    seg_starts,
    lengths,
    init_state,
    attn_gain,
    state_gain,
    mlp_gain,
    w_query,
    w_key,
    w_value,
    w_out,
    w_squery,
    w_sout,
    w_up,
    w_down,
    rel_bias,
    gate_bias,
    out_cot,
    state_cot,
):
    seq_count = inputs.shape[0]
    chain_length = lax.axis_size("seq")
    block_index = lax.axis_index("seq")
    is_first = block_index == 0
    width_local = w_query.shape[1]
    head_count = width_local // HEAD_DIM
    gate_value = jax.nn.sigmoid(gate_bias)
    positions = jnp.arange(BLOCK)
    inputs_wide = inputs.astype(jnp.float32)
    tokens_low = gather_rows(to_low(layer_norm(inputs_wide, attn_gain)))
    query_tok = to_low(matmul(tokens_low, w_query))
    key_tok = to_low(matmul(tokens_low, w_key))
    value_tok = to_low(matmul(tokens_low, w_value))
    key_prev, value_prev = passed_along((key_tok, value_tok), "seq", 1)
    valid_keys = (block_index * BLOCK + positions)[None, :] < lengths[:, None]
    batched_attend = jax.vmap(attend_forward, in_axes=(0, 0, 0, None, 0))
    batched_back = jax.vmap(attend_back, in_axes=(0, 0, 0, None, 0, 0, 0))

    def state_forward(state_rows, key_blk, value_blk, valid_blk):
        state_low = lax.all_gather(
            to_low(layer_norm(state_rows, state_gain)), "tensor", axis=1, tiled=True
        )
        query_st = to_low(matmul(state_low, w_squery))
        key_st = to_low(matmul(state_low, w_key))
        value_st = to_low(matmul(state_low, w_value))
        key_all = jnp.concatenate([key_blk, key_st], axis=1)
        value_all = jnp.concatenate([value_blk, value_st], axis=1)
        mixed_st, lse_st = batched_attend(
            query_st, key_all, value_all, 0.0, state_mask_of(valid_blk)
        )
        update = lax.psum_scatter(
            matmul(mixed_st, w_sout).astype(jnp.bfloat16), "tensor", scatter_dimension=1, tiled=True
        ).astype(jnp.float32)
        state_next = gate_value * state_rows + (1.0 - gate_value) * update
        return (state_next, (state_low, query_st, key_st, value_st, mixed_st, lse_st, update))

    def state_backward(
        grad_out, state_rows, kept_one, key_blk, value_blk, valid_blk, extra_key, extra_value
    ):
        state_low, query_st, key_st, value_st, mixed_st, lse_st, update = kept_one
        gate_part = (
            jnp.sum(grad_out * (state_rows - update), axis=(0, 1)) * gate_value * (1.0 - gate_value)
        )
        grad_update = lax.all_gather(
            to_low((1.0 - gate_value) * grad_out), "tensor", axis=1, tiled=True
        )
        grad_mixed_st = to_low(matmul_t(grad_update, w_sout))
        sout_part = outer_sum(mixed_st, grad_update)
        key_all = jnp.concatenate([key_blk, key_st], axis=1)
        value_all = jnp.concatenate([value_blk, value_st], axis=1)
        grad_query_st, grad_keys_st, grad_values_st, _ = batched_back(
            query_st, key_all, value_all, 0.0, state_mask_of(valid_blk), lse_st, grad_mixed_st
        )
        query_low = to_low(grad_query_st)
        key_low = to_low(grad_keys_st[:, BLOCK:] + extra_key)
        value_low = to_low(grad_values_st[:, BLOCK:] + extra_value)
        squery_part = outer_sum(state_low, query_low)
        key_part = outer_sum(state_low, key_low)
        value_part = outer_sum(state_low, value_low)
        terms = (
            matmul_t(query_low, w_squery) + matmul_t(key_low, w_key) + matmul_t(value_low, w_value)
        )
        grad_normed = lax.psum_scatter(
            terms.astype(jnp.bfloat16), "tensor", scatter_dimension=1, tiled=True
        ).astype(jnp.float32)
        grad_rows_norm, gain_part = norm_back(state_rows, state_gain, grad_normed)
        grad_in = gate_value * grad_out + grad_rows_norm
        block_grads = (grad_keys_st[:, :BLOCK], grad_values_st[:, :BLOCK])
        return (
            grad_in,
            block_grads,
            (squery_part, key_part, value_part, sout_part, gain_part, gate_part),
        )

    zeros_rows = jnp.zeros((seq_count,) + init_state.shape, jnp.float32)
    narrow_zero = jnp.zeros((seq_count, STATES, width_local), jnp.bfloat16)
    stored_start = (
        zeros_rows,
        zeros_rows,
        jnp.zeros((seq_count, STATES, D), jnp.bfloat16),
        narrow_zero,
        narrow_zero,
        narrow_zero,
        narrow_zero,
        jnp.zeros((seq_count, head_count, STATES), jnp.float32),
        zeros_rows,
    )

    def forward_turn(turn_index, carry):
        incoming, stored_now = carry
        order_index = turn_index - block_index
        is_live = (order_index >= 0) & (order_index < seq_count)
        picked = jnp.clip(order_index, 0, seq_count - 1)
        rows_now = jnp.where(is_first, init_state[None], incoming)
        key_one = lax.dynamic_slice_in_dim(key_tok, picked, 1, 0)
        value_one = lax.dynamic_slice_in_dim(value_tok, picked, 1, 0)
        valid_one = lax.dynamic_slice_in_dim(valid_keys, picked, 1, 0)
        rows_next, kept_one = state_forward(rows_now, key_one, value_one, valid_one)
        fresh = (rows_now, rows_next) + kept_one
        stored_now = tuple(
            (
                jnp.where(
                    is_live,
                    lax.dynamic_update_slice_in_dim(whole_array, fresh_part, picked, 0),
                    whole_array,
                )
                for whole_array, fresh_part in zip(stored_now, fresh)
            )
        )
        return (pass_state(rows_next), stored_now)

    incoming_start = jnp.zeros((1,) + init_state.shape, jnp.float32)
    _, stored_all = lax.fori_loop(
        0, chain_length + seq_count - 1, forward_turn, (incoming_start, stored_start)
    )
    state_in = stored_all[0]
    state_out = stored_all[1]
    kept = stored_all[2:]
    key_all_tok = jnp.concatenate([key_prev, key_tok, kept[2]], axis=1)
    value_all_tok = jnp.concatenate([value_prev, value_tok, kept[3]], axis=1)
    allowed_tok = jax.vmap(token_mask, in_axes=(0, 0, None))(seg_starts[:, 0], lengths, block_index)
    rel_table = bucket_of((jnp.arange(2 * BLOCK) - BLOCK)[None, :] - positions[:, None])
    full_bias = jnp.concatenate(
        [bias_lookup(rel_bias, rel_table), jnp.zeros((head_count, BLOCK, STATES), jnp.float32)],
        axis=2,
    )
    mixed_tok, lse_tok = batched_attend(
        query_tok, key_all_tok, value_all_tok, full_bias, allowed_tok
    )
    hidden_in = inputs_wide + sum_rows(matmul(mixed_tok, w_out))
    mid_low = gather_rows(to_low(layer_norm(hidden_in, mlp_gain)))
    pre_act = matmul(mid_low, w_up)
    hidden_low = to_low(jax.nn.gelu(pre_act))
    mlp_rows = sum_rows(matmul(hidden_low, w_down))
    tokens_out = (hidden_in + mlp_rows).astype(jnp.bfloat16)
    cot_wide = out_cot.astype(jnp.float32)
    cot_used = gather_rows(out_cot)
    grad_hidden_act = matmul_t(cot_used, w_down)
    down_grad = outer_sum(hidden_low, cot_used)
    grad_pre = to_low(gelu_back(pre_act, grad_hidden_act))
    up_grad = outer_sum(mid_low, grad_pre)
    grad_normed_mid = sum_rows(matmul_t(grad_pre, w_up))
    grad_mid_in, mlp_gain_grad = norm_back(hidden_in, mlp_gain, grad_normed_mid)
    grad_hidden = cot_wide + grad_mid_in
    grad_attn_low = gather_rows(to_low(grad_hidden))
    grad_mixed = to_low(matmul_t(grad_attn_low, w_out))
    out_grad = outer_sum(mixed_tok, grad_attn_low)
    grad_query_tok, grad_keys_tok, grad_values_tok, grad_scores = batched_back(
        query_tok, key_all_tok, value_all_tok, full_bias, allowed_tok, lse_tok, grad_mixed
    )
    bias_grad = bias_sums(grad_scores[..., : 2 * BLOCK], rel_table)
    grad_key_next, grad_value_next = (
        passed_along(grad_keys_tok[:, :BLOCK].astype(jnp.bfloat16), "seq", -1).astype(jnp.float32),
        passed_along(grad_values_tok[:, :BLOCK].astype(jnp.bfloat16), "seq", -1).astype(
            jnp.float32
        ),
    )
    grad_key_own = grad_keys_tok[:, BLOCK : 2 * BLOCK] + grad_key_next
    grad_value_own = grad_values_tok[:, BLOCK : 2 * BLOCK] + grad_value_next
    grad_key_st_tok = grad_keys_tok[:, 2 * BLOCK :]
    grad_value_st_tok = grad_values_tok[:, 2 * BLOCK :]
    cot_rows = state_cot[:, 0].astype(jnp.float32)
    wide_zero = jnp.zeros((seq_count, BLOCK, width_local), jnp.float32)
    stored_back = (zeros_rows, wide_zero, wide_zero)
    totals_start = (
        jnp.zeros((D, width_local), jnp.float32),
        jnp.zeros((D, width_local), jnp.float32),
        jnp.zeros((D, width_local), jnp.float32),
        jnp.zeros((width_local, D), jnp.float32),
        jnp.zeros((D,), jnp.float32),
        jnp.zeros((D,), jnp.float32),
    )

    def backward_turn(turn_index, carry):
        incoming, stored_now, totals_now = carry
        order_index = turn_index - (chain_length - 1 - block_index)
        is_live = (order_index >= 0) & (order_index < seq_count)
        picked = jnp.clip(order_index, 0, seq_count - 1)

        def slice_one(whole_array):
            return lax.dynamic_slice_in_dim(whole_array, picked, 1, 0)

        grad_out = slice_one(cot_rows) + incoming
        kept_one = tuple((slice_one(kept_array) for kept_array in kept))
        grad_in, block_one, parts_one = state_backward(
            grad_out,
            slice_one(state_in),
            kept_one,
            slice_one(key_tok),
            slice_one(value_tok),
            slice_one(valid_keys),
            slice_one(grad_key_st_tok),
            slice_one(grad_value_st_tok),
        )
        fresh = (grad_in,) + block_one
        stored_now = tuple(
            (
                jnp.where(
                    is_live,
                    lax.dynamic_update_slice_in_dim(whole_array, fresh_part, picked, 0),
                    whole_array,
                )
                for whole_array, fresh_part in zip(stored_now, fresh)
            )
        )
        totals_now = tuple(
            (
                total_now + jnp.where(is_live, part_now, 0.0)
                for total_now, part_now in zip(totals_now, parts_one)
            )
        )
        return (pass_back(grad_in), stored_now, totals_now)

    incoming_start = jnp.zeros((1,) + init_state.shape, jnp.float32)
    _, stored_done, weight_parts = lax.fori_loop(
        0, chain_length + seq_count - 1, backward_turn, (incoming_start, stored_back, totals_start)
    )
    grad_in_all, grad_key_blk, grad_value_blk = stored_done
    query_low = to_low(grad_query_tok)
    key_low = to_low(grad_key_own + grad_key_blk)
    value_low = to_low(grad_value_own + grad_value_blk)
    query_grad = outer_sum(tokens_low, query_low)
    key_grad = outer_sum(tokens_low, key_low) + weight_parts[1]
    value_grad = outer_sum(tokens_low, value_low) + weight_parts[2]
    grad_tokens = sum_rows(
        matmul_t(query_low, w_query) + matmul_t(key_low, w_key) + matmul_t(value_low, w_value)
    )
    grad_in_norm, attn_gain_grad = norm_back(inputs_wide, attn_gain, grad_tokens)
    inputs_grad = grad_hidden + grad_in_norm
    state_part = jnp.where(is_first, jnp.sum(grad_in_all, axis=0), 0.0)
    gains = lax.psum(
        jnp.stack([attn_gain_grad, weight_parts[4], mlp_gain_grad, weight_parts[5]]), "tensor"
    )
    totals = (
        lax.psum(query_grad.astype(jnp.bfloat16), ("dp", "seq")).astype(jnp.float32),
        lax.psum(key_grad.astype(jnp.bfloat16), ("dp", "seq")).astype(jnp.float32),
        lax.psum(value_grad.astype(jnp.bfloat16), ("dp", "seq")).astype(jnp.float32),
        lax.psum(out_grad.astype(jnp.bfloat16), ("dp", "seq")).astype(jnp.float32),
        lax.psum(weight_parts[0].astype(jnp.bfloat16), ("dp", "seq")).astype(jnp.float32),
        lax.psum(weight_parts[3].astype(jnp.bfloat16), ("dp", "seq")).astype(jnp.float32),
        lax.psum(up_grad.astype(jnp.bfloat16), ("dp", "seq")).astype(jnp.float32),
        lax.psum(down_grad.astype(jnp.bfloat16), ("dp", "seq")).astype(jnp.float32),
        lax.psum(bias_grad.astype(jnp.bfloat16), ("dp", "seq")).astype(jnp.float32),
        lax.psum(state_part.astype(jnp.bfloat16), ("dp", "seq")).astype(jnp.float32),
        lax.psum(gains.astype(jnp.bfloat16), ("dp", "seq")).astype(jnp.float32),
    )
    gain_total = totals[10]
    return (
        tokens_out,
        state_out[:, None],
        inputs_grad,
        totals[9],
        gain_total[0],
        gain_total[1],
        gain_total[2],
        totals[0],
        totals[1],
        totals[2],
        totals[3],
        totals[4],
        totals[5],
        totals[6],
        totals[7],
        totals[8],
        gain_total[3],
    )


def solution(mesh):
    return jax.shard_map(
        body,
        mesh=mesh,
        in_specs=(
            P("dp", ("seq", "tensor"), None),
            P("dp", "seq"),
            P("dp"),
            P("tensor", None),
            P(),
            P(),
            P(),
            P(None, "tensor"),
            P(None, "tensor"),
            P(None, "tensor"),
            P("tensor", None),
            P(None, "tensor"),
            P("tensor", None),
            P(None, "tensor"),
            P("tensor", None),
            P(None, "tensor"),
            P(),
            P("dp", ("seq", "tensor"), None),
            P("dp", "seq", "tensor", None),
        ),
        out_specs=(
            P("dp", ("seq", "tensor"), None),
            P("dp", "seq", "tensor", None),
            P("dp", ("seq", "tensor"), None),
            P("tensor", None),
            P(),
            P(),
            P(),
            P(None, "tensor"),
            P(None, "tensor"),
            P(None, "tensor"),
            P("tensor", None),
            P(None, "tensor"),
            P("tensor", None),
            P(None, "tensor"),
            P("tensor", None),
            P(None, "tensor"),
            P(),
        ),
        check_vma=False,
    )
```

profile of v0, /device:TPU:0, one launch (start us, length us, event | category | flops | bytes accessed | tf_op | source)
XLA Modules:
  0.0 1462.0 jit_solution(14470292739887533268)
XLA Ops:
  16.7 14.6 broadcast_compare_fusion.27
  31.6 17.1 %select_add_fusion.3 = f32[2,512,1024]{2,1,0:T(8,128)} fusion(f32[2]{0:T(128)S(1)} %get-tuple-element.1549, f32[2]{0:T(128)S(1)} %get-tuple-element.1550, f32[2]{0:T(128)S(1)} %get-tuple-element.1520, f32[2]{0:T(128)S(1)} %get-tuple-element.1521, f32[2]{0:T(128)S(1)} %get-tuple-element.1522, f32[2]{0:T(128)S(1)} %get-tuple-element.1523, ...), kind=kLoop, calls=%fused_computation.223 | loop fusion | flops 66060288 | bytes 20971776 | tf_op jit(solution)/shard_map/add | solution.py:168
  49.1 5.6 concatenate.67
  57.7 4.4 all-gather.7.cloned.1.call-done
  62.1 3.2 convolution_convert_fusion.8
  69.8 3.2 convolution_convert_fusion.9
  75.0 3.9 collective-permute-start.2
  87.2 409.5 %while.66 = (s32[]{:T(128)}, f32[1,128,1024]{2,1,0:T(8,128)S(1)}, f32[2,128,1024]{2,1,0:T(8,128)}, f32[2,128,1024]{2,1,0:T(8,128)}, bf16[2,512,1024]{2,1,0:T(8,1...) while((s32[]{:T(128)}, f32[1,128,1024]{2,1,0:T(8,128)S(1)}, ...), condition=%wide.region_8.9_spmd.clone, body=%wide.region_2.8_spmd.clone.sunk | while | flops 1629881472 | bytes 53808180 | solution.py:317
  92.6 23.9 %all-gather.15.cloned.1.call-done = bf16[1,512,1024]{2,1,0:T(8,128)(2,1)} async-done(((bf16[1,128,1024]{2,1,0:T(8,128)(2,1)}), bf16[1,512,1024]{2,1,0:T(8,128)(2,1)}) %all-gather.15.cloned.1.call-update) | async-done | bytes 1048592 | tf_op jit(solution)/shard_map/while/body/eval_jaxpr/all_gather | solution.py:224
  133.6 25.0 %reduce-scatter.15.cloned.1.call-done = bf16[1,128,1024]{2,1,0:T(8,128)(2,1)} async-done(((bf16[1,512,1024]{2,1,0:T(8,128)(2,1)}), bf16[1,128,1024]{2,1,0:T(8,128)(2,1)}) %reduce-scatter.15.cloned.1.call-update) | async-done | bytes 262160 | tf_op jit(solution)/shard_map/while/body/eval_jaxpr/reduce_scatter | solution.py:235
  171.0 28.2 %all-gather.15.cloned.1.call-done = bf16[1,512,1024]{2,1,0:T(8,128)(2,1)} async-done(((bf16[1,128,1024]{2,1,0:T(8,128)(2,1)}), bf16[1,512,1024]{2,1,0:T(8,128)(2,1)}) %all-gather.15.cloned.1.call-update) | async-done | bytes 1048592 | tf_op jit(solution)/shard_map/while/body/eval_jaxpr/all_gather | solution.py:224
  216.5 25.0 %reduce-scatter.15.cloned.1.call-done = bf16[1,128,1024]{2,1,0:T(8,128)(2,1)} async-done(((bf16[1,512,1024]{2,1,0:T(8,128)(2,1)}), bf16[1,128,1024]{2,1,0:T(8,128)(2,1)}) %reduce-scatter.15.cloned.1.call-update) | async-done | bytes 262160 | tf_op jit(solution)/shard_map/while/body/eval_jaxpr/reduce_scatter | solution.py:235
  253.8 28.2 %all-gather.15.cloned.1.call-done = bf16[1,512,1024]{2,1,0:T(8,128)(2,1)} async-done(((bf16[1,128,1024]{2,1,0:T(8,128)(2,1)}), bf16[1,512,1024]{2,1,0:T(8,128)(2,1)}) %all-gather.15.cloned.1.call-update) | async-done | bytes 1048592 | tf_op jit(solution)/shard_map/while/body/eval_jaxpr/all_gather | solution.py:224
  299.2 25.0 %reduce-scatter.15.cloned.1.call-done = bf16[1,128,1024]{2,1,0:T(8,128)(2,1)} async-done(((bf16[1,512,1024]{2,1,0:T(8,128)(2,1)}), bf16[1,128,1024]{2,1,0:T(8,128)(2,1)}) %reduce-scatter.15.cloned.1.call-update) | async-done | bytes 262160 | tf_op jit(solution)/shard_map/while/body/eval_jaxpr/reduce_scatter | solution.py:235
  336.5 28.2 %all-gather.15.cloned.1.call-done = bf16[1,512,1024]{2,1,0:T(8,128)(2,1)} async-done(((bf16[1,128,1024]{2,1,0:T(8,128)(2,1)}), bf16[1,512,1024]{2,1,0:T(8,128)(2,1)}) %all-gather.15.cloned.1.call-update) | async-done | bytes 1048592 | tf_op jit(solution)/shard_map/while/body/eval_jaxpr/all_gather | solution.py:224
  382.0 25.0 %reduce-scatter.15.cloned.1.call-done = bf16[1,128,1024]{2,1,0:T(8,128)(2,1)} async-done(((bf16[1,512,1024]{2,1,0:T(8,128)(2,1)}), bf16[1,128,1024]{2,1,0:T(8,128)(2,1)}) %reduce-scatter.15.cloned.1.call-update) | async-done | bytes 262160 | tf_op jit(solution)/shard_map/while/body/eval_jaxpr/reduce_scatter | solution.py:235
  419.3 28.2 %all-gather.15.cloned.1.call-done = bf16[1,512,1024]{2,1,0:T(8,128)(2,1)} async-done(((bf16[1,128,1024]{2,1,0:T(8,128)(2,1)}), bf16[1,512,1024]{2,1,0:T(8,128)(2,1)}) %all-gather.15.cloned.1.call-update) | async-done | bytes 1048592 | tf_op jit(solution)/shard_map/while/body/eval_jaxpr/all_gather | solution.py:224
  464.8 25.0 %reduce-scatter.15.cloned.1.call-done = bf16[1,128,1024]{2,1,0:T(8,128)(2,1)} async-done(((bf16[1,512,1024]{2,1,0:T(8,128)(2,1)}), bf16[1,128,1024]{2,1,0:T(8,128)(2,1)}) %reduce-scatter.15.cloned.1.call-update) | async-done | bytes 262160 | tf_op jit(solution)/shard_map/while/body/eval_jaxpr/reduce_scatter | solution.py:235
  502.9 2.8 pad_maximum_fusion.2
  508.3 6.3 fusion.182
  519.2 4.7 fusion.145
  526.9 46.1 %reduce-scatter.7.cloned.1.call-done = bf16[2,128,1024]{2,1,0:T(8,128)(2,1)} async-done(((bf16[2,512,1024]{2,1,0:T(8,128)(2,1)}), bf16[2,128,1024]{2,1,0:T(8,128)(2,1)}) %reduce-scatter.7.cloned.1.call-update) | async-done | bytes 524304 | tf_op jit(solution)/shard_map/reduce_scatter | solution.py:93
  578.9 44.3 %all-gather.9.cloned.1.call-done = bf16[2,512,1024]{2,1,0:T(8,128)(2,1)} async-done(((bf16[2,128,1024]{2,1,0:T(8,128)(2,1)}), bf16[2,512,1024]{2,1,0:T(8,128)(2,1)}) %all-gather.9.cloned.1.call-update) | async-done | bytes 2097168 | tf_op jit(solution)/shard_map/all_gather | solution.py:89
  623.2 5.9 fusion.112
  629.1 40.3 %all-gather.11.cloned.1.call-done = bf16[2,512,1024]{2,1,0:T(8,128)(2,1)} async-done(((bf16[2,128,1024]{2,1,0:T(8,128)(2,1)}), bf16[2,512,1024]{2,1,0:T(8,128)(2,1)}) %all-gather.11.cloned.1.call-update) | async-done | bytes 2097168 | tf_op jit(solution)/shard_map/all_gather | solution.py:89
  669.3 7.9 fusion.105
  678.7 3.7 fusion.123
  682.6 42.5 %reduce-scatter.11.cloned.1.call-done = bf16[2,128,1024]{2,1,0:T(8,128)(2,1)} async-done(((bf16[2,512,1024]{2,1,0:T(8,128)(2,1)}), bf16[2,128,1024]{2,1,0:T(8,128)(2,1)}) %reduce-scatter.11.cloned.1.call-update) | async-done | bytes 524304 | tf_op jit(solution)/shard_map/reduce_scatter | solution.py:93
  732.4 6.1 bitcast_convert_fusion.1
  738.6 4.1 bitcast_convert_fusion
  742.7 33.9 %all-gather.13.cloned.1.call-done = bf16[2,512,1024]{2,1,0:T(8,128)(2,1)} async-done(((bf16[2,128,1024]{2,1,0:T(8,128)(2,1)}), bf16[2,512,1024]{2,1,0:T(8,128)(2,1)}) %all-gather.13.cloned.1.call-update) | async-done | bytes 2097168 | tf_op jit(solution)/shard_map/all_gather | solution.py:89
  779.2 6.6 fusion.93
  788.8 8.7 multiply_reduce_fusion.4
  797.5 6.9 multiply_convert_fusion.3
  808.6 3.0 fusion.140
  817.4 400.5 %while.67 = (s32[]{:T(128)}, f32[1,128,1024]{2,1,0:T(8,128)}, f32[2,128,1024]{2,1,0:T(8,128)}, f32[2,512,256]{1,2,0:T(8,128)}, f32[2,512,256]{1,2,0:T(8,128)}, /...) while((s32[]{:T(128)}, f32[1,128,1024]{2,1,0:T(8,128)}, ...), condition=%wide.region_28.29_spmd.clone, body=%wide.region_19.28_spmd.clone.sunk | while | flops 3512737536 | bytes 166820528 | solution.py:419
  825.2 24.0 %all-gather.17.cloned.1.call-done = bf16[1,512,1024]{2,1,0:T(8,128)(2,1)} async-done(((bf16[1,128,1024]{2,1,0:T(8,128)(2,1)}), bf16[1,512,1024]{2,1,0:T(8,128)(2,1)}) %all-gather.17.cloned.1.call-update) | async-done | bytes 1048592 | tf_op jit(solution)/shard_map/while/body/eval_jaxpr/all_gather | solution.py:248
  870.8 19.3 %reduce-scatter.17.cloned.1.call-done = bf16[1,128,1024]{2,1,0:T(8,128)(2,1)} async-done(((bf16[1,512,1024]{2,1,0:T(8,128)(2,1)}), bf16[1,128,1024]{2,1,0:T(8,128)(2,1)}) %reduce-scatter.17.cloned.1.call-update) | async-done | bytes 262160 | tf_op jit(solution)/shard_map/while/body/eval_jaxpr/reduce_scatter | solution.py:267
  904.8 24.6 %all-gather.17.cloned.1.call-done = bf16[1,512,1024]{2,1,0:T(8,128)(2,1)} async-done(((bf16[1,128,1024]{2,1,0:T(8,128)(2,1)}), bf16[1,512,1024]{2,1,0:T(8,128)(2,1)}) %all-gather.17.cloned.1.call-update) | async-done | bytes 1048592 | tf_op jit(solution)/shard_map/while/body/eval_jaxpr/all_gather | solution.py:248
  943.8 3.0 fusion.346
  952.7 17.6 %reduce-scatter.17.cloned.1.call-done = bf16[1,128,1024]{2,1,0:T(8,128)(2,1)} async-done(((bf16[1,512,1024]{2,1,0:T(8,128)(2,1)}), bf16[1,128,1024]{2,1,0:T(8,128)(2,1)}) %reduce-scatter.17.cloned.1.call-update) | async-done | bytes 262160 | tf_op jit(solution)/shard_map/while/body/eval_jaxpr/reduce_scatter | solution.py:267
  985.0 24.5 %all-gather.17.cloned.1.call-done = bf16[1,512,1024]{2,1,0:T(8,128)(2,1)} async-done(((bf16[1,128,1024]{2,1,0:T(8,128)(2,1)}), bf16[1,512,1024]{2,1,0:T(8,128)(2,1)}) %all-gather.17.cloned.1.call-update) | async-done | bytes 1048592 | tf_op jit(solution)/shard_map/while/body/eval_jaxpr/all_gather | solution.py:248
  1024.0 3.0 fusion.346
  1032.8 17.6 %reduce-scatter.17.cloned.1.call-done = bf16[1,128,1024]{2,1,0:T(8,128)(2,1)} async-done(((bf16[1,512,1024]{2,1,0:T(8,128)(2,1)}), bf16[1,128,1024]{2,1,0:T(8,128)(2,1)}) %reduce-scatter.17.cloned.1.call-update) | async-done | bytes 262160 | tf_op jit(solution)/shard_map/while/body/eval_jaxpr/reduce_scatter | solution.py:267
  1065.0 24.6 %all-gather.17.cloned.1.call-done = bf16[1,512,1024]{2,1,0:T(8,128)(2,1)} async-done(((bf16[1,128,1024]{2,1,0:T(8,128)(2,1)}), bf16[1,512,1024]{2,1,0:T(8,128)(2,1)}) %all-gather.17.cloned.1.call-update) | async-done | bytes 1048592 | tf_op jit(solution)/shard_map/while/body/eval_jaxpr/all_gather | solution.py:248
  1104.1 3.0 fusion.346
  1112.9 17.6 %reduce-scatter.17.cloned.1.call-done = bf16[1,128,1024]{2,1,0:T(8,128)(2,1)} async-done(((bf16[1,512,1024]{2,1,0:T(8,128)(2,1)}), bf16[1,128,1024]{2,1,0:T(8,128)(2,1)}) %reduce-scatter.17.cloned.1.call-update) | async-done | bytes 262160 | tf_op jit(solution)/shard_map/while/body/eval_jaxpr/reduce_scatter | solution.py:267
  1145.2 24.6 %all-gather.17.cloned.1.call-done = bf16[1,512,1024]{2,1,0:T(8,128)(2,1)} async-done(((bf16[1,128,1024]{2,1,0:T(8,128)(2,1)}), bf16[1,512,1024]{2,1,0:T(8,128)(2,1)}) %all-gather.17.cloned.1.call-update) | async-done | bytes 1048592 | tf_op jit(solution)/shard_map/while/body/eval_jaxpr/all_gather | solution.py:248
  1184.2 3.0 fusion.346
  1193.0 17.6 %reduce-scatter.17.cloned.1.call-done = bf16[1,128,1024]{2,1,0:T(8,128)(2,1)} async-done(((bf16[1,512,1024]{2,1,0:T(8,128)(2,1)}), bf16[1,128,1024]{2,1,0:T(8,128)(2,1)}) %reduce-scatter.17.cloned.1.call-update) | async-done | bytes 262160 | tf_op jit(solution)/shard_map/while/body/eval_jaxpr/reduce_scatter | solution.py:267
  1223.7 3.2 fusion.142
  1227.6 3.3 fusion.141
  1241.1 3.1 add_convert_fusion.1
  1244.3 8.1 fusion.126
  1252.6 10.7 fusion.82
  1263.4 10.9 fusion.73
  1276.2 15.4 %fusion.91 = (bf16[2]{0:T(256)(128)(2,1)S(1)}, bf16[2]{0:T(256)(128)(2,1)S(1)}, bf16[2]{0:T(256)(128)(2,1)S(1)}, bf16[2]{0:T(256)(128)(2,1)S(1)}, bf16[2]{0:T(25...) fusion(pred[512,1024]{1,0:T(8,128)(4,1)} %copy-done.60, ...), kind=kLoop, calls=%fused_computation.201 | loop fusion | flops 60817392 | bytes 11534392 | tf_op jit(solution)/shard_map/reduce_sum | solution.py:179
  1293.3 66.3 %all-reduce.7.cloned.1.call-done = (bf16[128,1024]{1,0:T(8,128)(2,1)}, bf16[1024,256]{1,0:T(8,128)(2,1)}, bf16[1024,256]{1,0:T(8,128)(2,1)}, bf16[1024,256]{1,0:...) async-done(((bf16[128,1024]{1,0:T(8,128)(2,1)}, ...) | async-done | bytes 7602192 | tf_op jit(solution)/shard_map/psum | solution.py:448
  1359.6 4.2 convert_element_type.2728
  1373.6 32.3 %reduce-scatter.13.cloned.1.call-done = bf16[2,128,1024]{2,1,0:T(8,128)(2,1)} async-done(((bf16[2,512,1024]{2,1,0:T(8,128)(2,1)}), bf16[2,128,1024]{2,1,0:T(8,128)(2,1)}) %reduce-scatter.13.cloned.1.call-update) | async-done | bytes 524304 | tf_op jit(solution)/shard_map/reduce_scatter | solution.py:93
  1409.0 17.3 %psum.85 = bf16[4,1024]{1,0:T(4,128)(2,1)S(1)} all-reduce(f32[4,1024]{1,0:T(4,128)S(1)} %pad_maximum_fusion.3), channel_id=1, replica_groups=mesh['dp'=2,'seq'=4,'tensor'=4] {'tensor'}, use_global_device_ids=true, to_apply=%region_36.37 | all-reduce | flops 4096 | bytes 24576 | tf_op jit(solution)/shard_map/psum | solution.py:435
  1426.3 13.1 all-reduce.3
  1440.6 11.2 reduce-scatter.9.cloned.1.call-done
  1451.8 3.5 add_add_fusion.5
  (999 shorter events, 429.1 us)
Async XLA Ops:
  7.2 616.0 %copy-start = (bf16[1024,1024]{1,0:T(8,128)(2,1)S(1)}, bf16[1024,1024]{1,0:T(8,128)(2,1)}, u32[]{:S(2)}) copy-start(bf16[1024,1024]{1,0:T(8,128)(2,1)} %param.36) | copy-start | bytes 6291460
  7.2 54.9 %all-gather.7.cloned.1.call-start = ((), (), s32[]{:S(2)}) async-start(), calls=%async_computation.6 | async-start | bytes 2621440 | tf_op jit(solution)/shard_map/all_gather | solution.py:89
  67.3 435.6 %collective-permute-start.3 = (bf16[2,512,256]{2,1,0:T(8,128)(2,1)}, bf16[2,512,256]{2,1,0:T(8,128)(2,1)}, u32[]{:S(2)}, u32[]{:S(2)}) collective-permute-start(bf16[2,512,256]{2,1,0:T(8,128)(2,1)} %convolution_convert_fusion.8), channel_id=1, source_target_pairs={{0,4},{4,8},{8,12},{1,5},{5,9},{9,13},{2,6},{6,10},{10,14},{3,7},{... | collective-permute-start | bytes 1572872 | tf_op jit(solution)/shard_map/ppermute | solution.py:22
  75.0 441.5 %collective-permute-start.2 = (bf16[2,512,256]{2,1,0:T(8,128)(2,1)}, bf16[2,512,256]{2,1,0:T(8,128)(2,1)}, u32[]{:S(2)}, u32[]{:S(2)}) collective-permute-start(bf16[2,512,256]{2,1,0:T(8,128)(2,1)} %convolution_convert_fusion.9), channel_id=1, source_target_pairs={{0,4},{4,8},{8,12},{1,5},{5,9},{9,13},{2,6},{6,10},{10,14},{3,7},{... | collective-permute-start | bytes 1572872 | tf_op jit(solution)/shard_map/ppermute | solution.py:22
  87.2 29.3 %all-gather.15.cloned.1.call-start = ((), (), s32[]{:S(2)}) async-start(), calls=%async_computation.15 | async-start | bytes 1310720 | tf_op jit(solution)/shard_map/while/body/eval_jaxpr/all_gather | solution.py:224
  90.6 68.1 %reduce-scatter.15.cloned.1.call-start = ((), (), s32[]{:S(2)}) async-start(), calls=%async_computation.16 | async-start | bytes 1310720 | tf_op jit(solution)/shard_map/while/body/eval_jaxpr/reduce_scatter | solution.py:235
  161.3 4.2 collective-permute-start
  165.6 33.6 %all-gather.15.cloned.1.call-start = ((), (), s32[]{:S(2)}) async-start(), calls=%async_computation.15 | async-start | bytes 1310720 | tf_op jit(solution)/shard_map/while/body/eval_jaxpr/all_gather | solution.py:224
  169.0 72.5 %reduce-scatter.15.cloned.1.call-start = ((), (), s32[]{:S(2)}) async-start(), calls=%async_computation.16 | async-start | bytes 1310720 | tf_op jit(solution)/shard_map/while/body/eval_jaxpr/reduce_scatter | solution.py:235
  244.1 4.2 collective-permute-start
  248.4 33.6 %all-gather.15.cloned.1.call-start = ((), (), s32[]{:S(2)}) async-start(), calls=%async_computation.15 | async-start | bytes 1310720 | tf_op jit(solution)/shard_map/while/body/eval_jaxpr/all_gather | solution.py:224
  251.8 72.5 %reduce-scatter.15.cloned.1.call-start = ((), (), s32[]{:S(2)}) async-start(), calls=%async_computation.16 | async-start | bytes 1310720 | tf_op jit(solution)/shard_map/while/body/eval_jaxpr/reduce_scatter | solution.py:235
  326.9 4.2 collective-permute-start
  331.1 33.6 %all-gather.15.cloned.1.call-start = ((), (), s32[]{:S(2)}) async-start(), calls=%async_computation.15 | async-start | bytes 1310720 | tf_op jit(solution)/shard_map/while/body/eval_jaxpr/all_gather | solution.py:224
  334.5 72.5 %reduce-scatter.15.cloned.1.call-start = ((), (), s32[]{:S(2)}) async-start(), calls=%async_computation.16 | async-start | bytes 1310720 | tf_op jit(solution)/shard_map/while/body/eval_jaxpr/reduce_scatter | solution.py:235
  409.6 4.2 collective-permute-start
  413.9 33.6 %all-gather.15.cloned.1.call-start = ((), (), s32[]{:S(2)}) async-start(), calls=%async_computation.15 | async-start | bytes 1310720 | tf_op jit(solution)/shard_map/while/body/eval_jaxpr/all_gather | solution.py:224
  417.3 72.5 %reduce-scatter.15.cloned.1.call-start = ((), (), s32[]{:S(2)}) async-start(), calls=%async_computation.16 | async-start | bytes 1310720 | tf_op jit(solution)/shard_map/while/body/eval_jaxpr/reduce_scatter | solution.py:235
  492.4 4.2 collective-permute-start
  496.7 76.4 %reduce-scatter.7.cloned.1.call-start = ((), (), s32[]{:S(2)}) async-start(), calls=%async_computation.7 | async-start | bytes 2621440 | tf_op jit(solution)/shard_map/reduce_scatter | solution.py:93
  524.0 49.1 %copy-start.9 = (bf16[2,128,1024]{2,1,0:T(8,128)(2,1)S(1)}, bf16[2,128,1024]{2,1,0:T(8,128)(2,1)}, u32[]{:S(2)}) copy-start(bf16[2,128,1024]{2,1,0:T(8,128)(2,1)} %param.23) | copy-start | bytes 1572868
  524.0 51.7 %copy-start.115 = (f32[1024]{0:T(1024)S(1)}, f32[1024]{0:T(1024)}, u32[]{:S(2)}) copy-start(f32[1024]{0:T(1024)} %param.29) | copy-start | bytes 12292
  526.8 96.3 %all-gather.9.cloned.1.call-start = ((), (), s32[]{:S(2)}) async-start(), calls=%async_computation.8 | async-start | bytes 2621440 | tf_op jit(solution)/shard_map/all_gather | solution.py:89
  574.3 154.6 %copy-start.118 = (f32[2,128]{1,0:T(2,128)}, f32[2,128]{1,0:T(2,128)S(1)}, u32[]{:S(2)}) copy-start(f32[2,128]{1,0:T(2,128)S(1)} %broadcast_multiply_fusion.2) | copy-start | bytes 3076
  575.6 153.2 %copy-start.122 = (f32[2,128]{1,0:T(2,128)}, f32[2,128]{1,0:T(2,128)S(1)}, u32[]{:S(2)}) copy-start(f32[2,128]{1,0:T(2,128)S(1)} %fusion.177) | copy-start | bytes 3076
  577.8 91.6 %all-gather.11.cloned.1.call-start = ((), (), s32[]{:S(2)}) async-start(), calls=%async_computation.10 | async-start | bytes 2621440 | tf_op jit(solution)/shard_map/all_gather | solution.py:89
  578.3 146.8 %reduce-scatter.11.cloned.1.call-start = ((), (), s32[]{:S(2)}) async-start(), calls=%async_computation.11 | async-start | bytes 2621440 | tf_op jit(solution)/shard_map/reduce_scatter | solution.py:93
  678.7 46.5 %copy-start.24 = (bf16[2,128,1024]{2,1,0:T(8,128)(2,1)S(1)}, bf16[2,128,1024]{2,1,0:T(8,128)(2,1)}, u32[]{:S(2)}) copy-start(bf16[2,128,1024]{2,1,0:T(8,128)(2,1)} %reduce-scatter.7.cloned.1.call-done) | copy-start | bytes 1572868
  682.4 46.5 %copy-start.94 = (bf16[2,128,1024]{2,1,0:T(8,128)(2,1)S(1)}, bf16[2,128,1024]{2,1,0:T(8,128)(2,1)}, u32[]{:S(2)}) copy-start(bf16[2,128,1024]{2,1,0:T(8,128)(2,1)} %param.40) | copy-start | bytes 1572868
  682.4 48.9 %copy-start.102 = (bf16[2,1,128,1024]{3,2,1,0:T(8,128)(2,1)S(1)}, bf16[2,1,128,1024]{3,2,1,0:T(8,128)(2,1)}, u32[]{:S(2)}) copy-start(bf16[2,1,128,1024]{3,2,1,0:T(8,128)(2,1)} %param.41) | copy-start | bytes 1572868
  682.4 94.3 %all-gather.13.cloned.1.call-start = ((), (), s32[]{:S(2)}) async-start(), calls=%async_computation.12 | async-start | bytes 2621440 | tf_op jit(solution)/shard_map/all_gather | solution.py:89
  738.6 40.6 %copy-start.16 = (pred[2,512,1536]{2,1,0:T(8,128)(4,1)S(1)}, pred[2,512,1536]{2,1,0:T(8,128)(4,1)}, u32[]{:S(2)}) copy-start(pred[2,512,1536]{2,1,0:T(8,128)(4,1)} %add_add_fusion.2) | copy-start | bytes 4718596
  811.5 419.4 %collective-permute-start.5 = (bf16[2,512,256]{1,2,0:T(8,128)(2,1)}, bf16[2,512,256]{1,2,0:T(8,128)(2,1)}, u32[]{:S(2)}, u32[]{:S(2)}) collective-permute-start(bf16[2,512,256]{1,2,0:T(8,128)(2,1)} %slice.321), channel_id=1, source_target_pairs={{4,0},{8,4},{12,8},{5,1},{9,5},{13,9},{6,2},{10,6},{14,10},{7,3},{... | collective-permute-start | bytes 1572872 | tf_op jit(solution)/shard_map/ppermute | solution.py:22
  812.8 421.4 %collective-permute-start.4 = (bf16[2,512,256]{1,2,0:T(8,128)(2,1)}, bf16[2,512,256]{1,2,0:T(8,128)(2,1)}, u32[]{:S(2)}, u32[]{:S(2)}) collective-permute-start(bf16[2,512,256]{1,2,0:T(8,128)(2,1)} %slice.322), channel_id=1, source_target_pairs={{4,0},{8,4},{12,8},{5,1},{9,5},{13,9},{6,2},{10,6},{14,10},{7,3},{... | collective-permute-start | bytes 1572872 | tf_op jit(solution)/shard_map/ppermute | solution.py:22
  817.8 31.4 %all-gather.17.cloned.1.call-start = ((), (), s32[]{:S(2)}) async-start(), calls=%async_computation.17 | async-start | bytes 1310720 | tf_op jit(solution)/shard_map/while/body/eval_jaxpr/all_gather | solution.py:248
  820.0 70.1 %reduce-scatter.17.cloned.1.call-start = ((), (), s32[]{:S(2)}) async-start(), calls=%async_computation.18 | async-start | bytes 1310720 | tf_op jit(solution)/shard_map/while/body/eval_jaxpr/reduce_scatter | solution.py:267
  893.1 3.4 collective-permute-start.1
  897.4 32.0 %all-gather.17.cloned.1.call-start = ((), (), s32[]{:S(2)}) async-start(), calls=%async_computation.17 | async-start | bytes 1310720 | tf_op jit(solution)/shard_map/while/body/eval_jaxpr/all_gather | solution.py:248
  899.6 70.6 %reduce-scatter.17.cloned.1.call-start = ((), (), s32[]{:S(2)}) async-start(), calls=%async_computation.18 | async-start | bytes 1310720 | tf_op jit(solution)/shard_map/while/body/eval_jaxpr/reduce_scatter | solution.py:267
  973.3 3.4 collective-permute-start.1
  977.6 31.9 %all-gather.17.cloned.1.call-start = ((), (), s32[]{:S(2)}) async-start(), calls=%async_computation.17 | async-start | bytes 1310720 | tf_op jit(solution)/shard_map/while/body/eval_jaxpr/all_gather | solution.py:248
  979.8 70.5 %reduce-scatter.17.cloned.1.call-start = ((), (), s32[]{:S(2)}) async-start(), calls=%async_computation.18 | async-start | bytes 1310720 | tf_op jit(solution)/shard_map/while/body/eval_jaxpr/reduce_scatter | solution.py:267
  1053.4 3.4 collective-permute-start.1
  1057.7 31.9 %all-gather.17.cloned.1.call-start = ((), (), s32[]{:S(2)}) async-start(), calls=%async_computation.17 | async-start | bytes 1310720 | tf_op jit(solution)/shard_map/while/body/eval_jaxpr/all_gather | solution.py:248
  1059.9 70.6 %reduce-scatter.17.cloned.1.call-start = ((), (), s32[]{:S(2)}) async-start(), calls=%async_computation.18 | async-start | bytes 1310720 | tf_op jit(solution)/shard_map/while/body/eval_jaxpr/reduce_scatter | solution.py:267
  1133.5 3.4 collective-permute-start.1
  1137.8 32.0 %all-gather.17.cloned.1.call-start = ((), (), s32[]{:S(2)}) async-start(), calls=%async_computation.17 | async-start | bytes 1310720 | tf_op jit(solution)/shard_map/while/body/eval_jaxpr/all_gather | solution.py:248
  1140.0 70.6 %reduce-scatter.17.cloned.1.call-start = ((), (), s32[]{:S(2)}) async-start(), calls=%async_computation.18 | async-start | bytes 1310720 | tf_op jit(solution)/shard_map/while/body/eval_jaxpr/reduce_scatter | solution.py:267
  1213.6 3.4 collective-permute-start.1
  1217.9 141.7 %all-reduce.7.cloned.1.call-start = ((), (), s32[]{:S(2)}) async-start(), calls=%async_computation.14 | async-start | bytes 15204352 | tf_op jit(solution)/shard_map/psum | solution.py:448
  1237.5 168.4 %reduce-scatter.13.cloned.1.call-start = ((), (), s32[]{:S(2)}) async-start(), calls=%async_computation.13 | async-start | bytes 2621440 | tf_op jit(solution)/shard_map/reduce_scatter | solution.py:93
  1244.3 207.5 %reduce-scatter.9.cloned.1.call-start = ((), (), s32[]{:S(2)}) async-start(), calls=%async_computation.9 | async-start | bytes 2621440 | tf_op jit(solution)/shard_map/reduce_scatter | solution.py:93
  1367.4 38.6 %copy-start.10 = (bf16[2,128,1024]{2,1,0:T(8,128)(2,1)S(1)}, bf16[2,128,1024]{2,1,0:T(8,128)(2,1)}, u32[]{:S(2)}) copy-start(bf16[2,128,1024]{2,1,0:T(8,128)(2,1)} %param.23) | copy-start | bytes 1572868
  1367.4 38.6 %copy-start.117 = (f32[1024]{0:T(1024)S(1)}, f32[1024]{0:T(1024)}, u32[]{:S(2)}) copy-start(f32[1024]{0:T(1024)} %param.27) | copy-start | bytes 12292
  1368.4 38.9 %copy-start.132 = (f32[2,128]{1,0:T(2,128)S(1)}, f32[2,128]{1,0:T(2,128)}, u32[]{:S(2)}) copy-start(f32[2,128]{1,0:T(2,128)} %copy-done.131) | copy-start | bytes 3076
  1368.4 38.9 %copy-start.128 = (f32[2,128]{1,0:T(2,128)S(1)}, f32[2,128]{1,0:T(2,128)}, u32[]{:S(2)}) copy-start(f32[2,128]{1,0:T(2,128)} %copy-done.127) | copy-start | bytes 3076
  1369.5 39.5 %copy-start.126 = (f32[1024]{0:T(1024)S(1)}, f32[1024]{0:T(1024)}, u32[]{:S(2)}) copy-start(f32[1024]{0:T(1024)} %get-tuple-element.1515) | copy-start | bytes 12292
  1369.5 82.3 %copy-start.25 = (bf16[2,128,1024]{2,1,0:T(8,128)(2,1)S(1)}, bf16[2,128,1024]{2,1,0:T(8,128)(2,1)}, u32[]{:S(2)}) copy-start(bf16[2,128,1024]{2,1,0:T(8,128)(2,1)} %reduce-scatter.7.cloned.1.call-done) | copy-start | bytes 1572868
  1369.5 82.3 %copy-start.116 = (f32[1024]{0:T(1024)S(1)}, f32[1024]{0:T(1024)}, u32[]{:S(2)}) copy-start(f32[1024]{0:T(1024)} %param.29) | copy-start | bytes 12292
  1369.5 82.3 %copy-start.119 = (f32[2,128]{1,0:T(2,128)S(1)}, f32[2,128]{1,0:T(2,128)}, u32[]{:S(2)}) copy-start(f32[2,128]{1,0:T(2,128)} %copy-done.118) | copy-start | bytes 3076
  1369.5 82.3 %copy-start.123 = (f32[2,128]{1,0:T(2,128)S(1)}, f32[2,128]{1,0:T(2,128)}, u32[]{:S(2)}) copy-start(f32[2,128]{1,0:T(2,128)} %copy-done.122) | copy-start | bytes 3076
  1369.5 82.3 %copy-start.125 = (f32[2,128]{1,0:T(2,128)S(1)}, f32[2,128]{1,0:T(2,128)}, u32[]{:S(2)}) copy-start(f32[2,128]{1,0:T(2,128)} %copy-done.124) | copy-start | bytes 3076
  1369.5 82.3 %copy-start.130 = (f32[2,128]{1,0:T(2,128)S(1)}, f32[2,128]{1,0:T(2,128)}, u32[]{:S(2)}) copy-start(f32[2,128]{1,0:T(2,128)} %copy-done.129) | copy-start | bytes 3076
  1371.7 83.6 %copy-start.1 = (bf16[1024,1024]{1,0:T(8,128)(2,1)S(1)}, bf16[1024,1024]{1,0:T(8,128)(2,1)}, u32[]{:S(2)}) copy-start(bf16[1024,1024]{1,0:T(8,128)(2,1)} %param.36) | copy-start | bytes 6291460
  (218 other events, 1945.5 us)
Sparse Core Ops, SparseCore 0:
  13.3 48.6 all-gather.6
  90.7 25.7 all-gather.14
  132.0 26.6 reduce-scatter.14
  169.1 30.0 all-gather.14
  214.8 26.6 reduce-scatter.14
  251.9 30.0 all-gather.14
  297.5 26.6 reduce-scatter.14
  334.6 30.0 all-gather.14
  380.3 26.6 reduce-scatter.14
  417.4 30.0 all-gather.14
  463.1 26.6 reduce-scatter.14
  526.9 46.0 reduce-scatter.6
  577.9 45.2 all-gather.8
  624.7 44.6 all-gather.10
  682.5 42.5 reduce-scatter.10
  731.4 45.2 all-gather.12
  820.1 29.0 all-gather.16
  863.4 26.6 reduce-scatter.16
  899.9 29.4 all-gather.16
  943.6 26.6 reduce-scatter.16
  980.0 29.4 all-gather.16
  1023.7 26.5 reduce-scatter.16
  1060.1 29.4 all-gather.16
  1103.8 26.6 reduce-scatter.16
  1140.3 29.4 all-gather.16
  1183.9 26.6 reduce-scatter.16
  1237.6 121.9 all-reduce.6
  1361.9 44.0 reduce-scatter.12
  1408.3 43.3 reduce-scatter.8
where the time goes:
time: 1470 us; the launch traced here: 1460 us
  waiting for transfers between devices  806 us (55%)
  matrix products  260 us (18%)
  other arithmetic  224 us (15%)
  local copies, waits for them, and re-layouts  96.2 us (7%)
  blocking collectives  30.3 us (2%)
  starting transfers between devices  25.4 us (2%)
  between operations  15.7 us (1%)
    all_gather x5, waiting for transfers between devices, state_forward(): lax.all_gather(to_low(layer_norm(state_rows, state_gain)), 'tensor', axis...  137 us
    reduce_scatter x4, waiting for transfers between devices, sum_rows(): lax.psum_scatter(terms.astype(jnp.bfloat16), 'tensor', scatter_dimension=...  132 us
    reduce_scatter x5, waiting for transfers between devices, state_forward(): lax.psum_scatter(matmul(mixed_st, w_sout).astype(jnp.bfloat16), 'tensor',...  125 us
    all_gather x4, waiting for transfers between devices, gather_rows(): return lax.all_gather(values, 'tensor', axis=1, tiled=True)  123 us
    all_gather x5, waiting for transfers between devices, state_backward(): lax.all_gather(to_low((1.0 - gate_value) * grad_out), 'tensor', axis=1, t...  122 us
    reduce_scatter x5, waiting for transfers between devices, state_backward(): lax.psum_scatter(terms.astype(jnp.bfloat16), 'tensor', scatter_dimension=...  89.6 us
    dot_general x26, matrix products, matmul(): jnp.einsum('...k,kn->...n', left, right, preferred_element_type=jnp.float32)  75 us
    psum x1, waiting for transfers between devices, body(): lax.psum(state_part.astype(jnp.bfloat16), ('dp', 'seq')).astype(jnp.float32)  66.3 us
  transfers between devices with their start and end apart: 43, of which 34 were waited for; matrix products, arithmetic and copies ran while one was open for 33% of the time, Pallas kernels for 0%

commit v1 on v0

--- a/solution.py
+++ b/solution.py
@@ -1,6 +1,8 @@
 import jax
 import jax.numpy as jnp
 from jax import lax
+from jax.experimental import pallas as pl
+from jax.experimental.pallas import tpu as pltpu
 from jax.sharding import PartitionSpec as P
 
 D = 1024
@@ -470,9 +472,658 @@
     )
 
 
+def chosen_body(mesh):
+    if mesh.shape["seq"] == 4 and mesh.shape["tensor"] == 4:
+        return line_body
+    return body
+
+
+MESH_ID = pl.DeviceIdType.MESH
+ROWS = 128
+CHUNKS = BLOCK // ROWS
+LINE = 8
+SCALE = HEAD_DIM ** (-0.5)
+VMEM_LIMIT = 60 * 1024 * 1024
+
+
+def dot_nn(left, right):
+    return lax.dot_general(left, right, (((1,), (0,)), ((), ())), preferred_element_type=jnp.float32)
+
+
+def dot_nt(left, right):
+    return lax.dot_general(left, right, (((1,), (1,)), ((), ())), preferred_element_type=jnp.float32)
+
+
+def dot_tn(left, right):
+    return lax.dot_general(left, right, (((0,), (0,)), ((), ())), preferred_element_type=jnp.float32)
+
+
+def line_place():
+    place = lax.axis_index("seq")
+    half = lax.rem(place, 2)
+    rank = lax.axis_index("tensor")
+    return place, half, rank
+
+
+def span(index, size):
+    return pl.ds(pl.multiple_of(index * size, size), size)
+
+
+def norm_parts(rows):
+    centered = rows - jnp.mean(rows, axis=-1, keepdims=True)
+    spread = jnp.mean(centered * centered, axis=-1, keepdims=True)
+    return centered, lax.rsqrt(spread + norm_eps)
+
+
+def token_masks(scal, block_id, first_row):
+    length = scal[0]
+    start = scal[1 + block_id]
+    row = lax.broadcasted_iota(jnp.int32, (ROWS, BLOCK), 0) + first_row
+    col = lax.broadcasted_iota(jnp.int32, (ROWS, BLOCK), 1)
+    prev_limit = jnp.where(block_id > 0, length - (block_id - 1) * BLOCK, 0)
+    prev_ok = (col > row) & (col < prev_limit)
+    row_in = (row >= start) & (row < start + SEG)
+    col_in = (col >= start) & (col < start + SEG)
+    cur_ok = ((col <= row) | (row_in & col_in)) & (col < length - block_id * BLOCK)
+    return prev_ok, cur_ok
+
+
+def state_block_mask(scal, block_id):
+    col = lax.broadcasted_iota(jnp.int32, (ROWS, BLOCK), 1)
+    return col < scal[0] - block_id * BLOCK
+
+
+def softmax_of(score_parts):
+    top = jnp.max(score_parts[0], axis=-1, keepdims=True)
+    for part in score_parts[1:]:
+        top = jnp.maximum(top, jnp.max(part, axis=-1, keepdims=True))
+    raised = [jnp.exp(part - top) for part in score_parts]
+    total = jnp.sum(raised[0], axis=-1, keepdims=True)
+    for part in raised[1:]:
+        total = total + jnp.sum(part, axis=-1, keepdims=True)
+    inverse = 1.0 / total
+    return [to_low(part * inverse) for part in raised], top + jnp.log(total)
+
+
+def token_scores(scal, qkv, qkvst, bias, block_id, chunk):
+    rows = span(chunk, ROWS)
+    prev_id = jnp.maximum(block_id - 1, 0)
+    query = qkv[block_id, rows, 0:128]
+    prev_ok, cur_ok = token_masks(scal, block_id, chunk * ROWS)
+    prev = dot_nt(query, qkv[prev_id, :, 128:256]) * SCALE + bias[rows, 0:BLOCK]
+    cur = dot_nt(query, qkv[block_id, :, 128:256]) * SCALE + bias[rows, BLOCK : 2 * BLOCK]
+    stt = dot_nt(query, qkvst[block_id, :, 128:256]) * SCALE
+    prev = jnp.where(prev_ok, prev, masked_score)
+    cur = jnp.where(cur_ok, cur, masked_score)
+    return query, (prev, cur, stt)
+
+
+def state_scores(scal, qkv, qkvst, block_id, chunk):
+    query = qkvst[block_id, span(chunk, ROWS), 0:128]
+    tok = dot_nt(query, qkv[block_id, :, 128:256]) * SCALE
+    tok = jnp.where(state_block_mask(scal, block_id), tok, masked_score)
+    stt = dot_nt(query, qkvst[block_id, :, 128:256]) * SCALE
+    return query, (tok, stt)
+
+
+def forward_kernel(
+    scal, qkv, start, w_state, w_sout, vecs, bias,
+    o_out, lse_out, state_rows, state_low, qkvst, lse_st, os_rows,
+    held, os_all, send_sem, pass_sem, recv_sem,
+):
+    place, half, rank = line_place()
+    partner = place + 1 - 2 * half
+    head = 2 * rank + half
+    peers = [lax.rem(rank + step, 4) for step in (1, 2, 3)]
+    barrier = pltpu.get_barrier_semaphore()
+    for peer in peers:
+        pl.semaphore_signal(
+            barrier, inc=1, device_id={"seq": place, "tensor": peer}, device_id_type=MESH_ID
+        )
+    pl.semaphore_signal(
+        barrier, inc=1, device_id={"seq": partner, "tensor": rank}, device_id_type=MESH_ID
+    )
+    held[...] = start[...].astype(jnp.float32)
+    gain = vecs[0:1, :]
+    gate = vecs[1:2, :]
+    pl.semaphore_wait(barrier, 4)
+
+    def carry_copy(block_id, which, sem, seq_to, rank_to):
+        part = os_all.at[block_id, :, span(which, 128)]
+        return pltpu.make_async_remote_copy(
+            src_ref=part,
+            dst_ref=part,
+            send_sem=sem,
+            recv_sem=recv_sem.at[block_id, which],
+            device_id={"seq": seq_to, "tensor": rank_to},
+            device_id_type=MESH_ID,
+        )
+
+    def one_block(block_id, _):
+        def project(chunk, _):
+            rows = span(chunk, ROWS)
+            centered, scale = norm_parts(held[rows, :])
+            low = to_low(centered * scale * gain)
+            state_low[block_id, rows, :] = low
+            qkvst[block_id, rows, :] = to_low(dot_nn(low, w_state[...]))
+            return 0
+
+        lax.fori_loop(0, CHUNKS, project, 0)
+
+        def attend_state(chunk, _):
+            rows = span(chunk, ROWS)
+            _, parts = state_scores(scal, qkv, qkvst, block_id, chunk)
+            (w_tok, w_stt), total = softmax_of(parts)
+            mixed = dot_nn(w_tok, qkv[block_id, :, 256:384]) + dot_nn(
+                w_stt, qkvst[block_id, :, 256:384]
+            )
+            os_all[block_id, rows, span(head, 128)] = to_low(mixed)
+            lse_st[block_id, rows, :] = total
+            return 0
+
+        lax.fori_loop(0, CHUNKS, attend_state, 0)
+        for slot, peer in enumerate(peers):
+            carry_copy(block_id, head, send_sem.at[block_id, slot], place, peer).start()
+        carry_copy(block_id, head, send_sem.at[block_id, 3], partner, rank).start()
+
+        def attend_token(chunk, _):
+            rows = span(chunk, ROWS)
+            _, parts = token_scores(scal, qkv, qkvst, bias, block_id, chunk)
+            weights, total = softmax_of(parts)
+            prev_id = jnp.maximum(block_id - 1, 0)
+            mixed = (
+                dot_nn(weights[0], qkv[prev_id, :, 256:384])
+                + dot_nn(weights[1], qkv[block_id, :, 256:384])
+                + dot_nn(weights[2], qkvst[block_id, :, 256:384])
+            )
+            o_out[block_id, rows, :] = to_low(mixed)
+            lse_out[block_id, rows, :] = total
+            return 0
+
+        lax.fori_loop(0, CHUNKS, attend_token, 0)
+        for slot, peer in enumerate(peers):
+            other = 2 * peer + half
+            carry_copy(block_id, other, send_sem.at[block_id, slot], place, peer).wait_recv()
+            carry_copy(block_id, other, pass_sem.at[block_id, slot], partner, rank).start()
+        for other_rank in range(4):
+            carry_copy(
+                block_id, 2 * other_rank + 1 - half, send_sem.at[block_id, 3], partner, rank
+            ).wait_recv()
+
+        def update(chunk, _):
+            rows = span(chunk, ROWS)
+            change = dot_nn(os_all[block_id, rows, :], w_sout[...])
+            held[rows, :] = gate * held[rows, :] + (1.0 - gate) * change
+            return 0
+
+        lax.fori_loop(0, CHUNKS, update, 0)
+        state_rows[block_id] = held[span(rank, 128), :]
+        os_rows[block_id] = os_all[block_id, span(head, 64), :]
+        return 0
+
+    lax.fori_loop(0, 4, one_block, 0)
+
+    def drain(block_id, _):
+        for slot, peer in enumerate(peers):
+            carry_copy(block_id, head, send_sem.at[block_id, slot], place, peer).wait_send()
+            other = 2 * peer + half
+            carry_copy(block_id, other, pass_sem.at[block_id, slot], partner, rank).wait_send()
+        carry_copy(block_id, head, send_sem.at[block_id, 3], partner, rank).wait_send()
+        return 0
+
+    lax.fori_loop(0, 4, drain, 0)
+
+
+def vmem_specs(count):
+    return [pl.BlockSpec(memory_space=pltpu.VMEM)] * count
+
+
+def forward_chain(scal, qkv, start, w_state, w_sout, vecs, bias):
+    low, wide = jnp.bfloat16, jnp.float32
+    shapes = (
+        ((4, BLOCK, 128), low),
+        ((4, BLOCK, 1), wide),
+        ((4, 128, D), wide),
+        ((4, STATES, D), low),
+        ((4, STATES, 384), low),
+        ((4, STATES, 1), wide),
+        ((4, 64, D), low),
+    )
+    return pl.pallas_call(
+        forward_kernel,
+        out_shape=[jax.ShapeDtypeStruct(*one) for one in shapes],
+        in_specs=[pl.BlockSpec(memory_space=pltpu.SMEM)] + vmem_specs(6),
+        out_specs=vmem_specs(7),
+        scratch_shapes=[
+            pltpu.VMEM((STATES, D), wide),
+            pltpu.VMEM((4, STATES, D), low),
+            pltpu.SemaphoreType.DMA((4, 4)),
+            pltpu.SemaphoreType.DMA((4, 3)),
+            pltpu.SemaphoreType.DMA((4, 8)),
+        ],
+        compiler_params=pltpu.CompilerParams(
+            collective_id=1, has_side_effects=True, vmem_limit_bytes=VMEM_LIMIT
+        ),
+        cost_estimate=pl.CostEstimate(flops=20000000000, bytes_accessed=20000000, transcendentals=0),
+        name="forward_chain",
+    )(scal, qkv, start, w_state, w_sout, vecs, bias)
+
+
+def backward_kernel(
+    scal, qkv, d_o, lse_tok, qkvst, lse_st, states, cots, w_back, w_sout, vecs, bias,
+    d_qkv, d_qkvst, du_rows, d_start, sums, dz_sum,
+    key_acc, value_acc, st_key, st_value, dos_rows, dos_got, d_got, grad_in,
+    send_sem, recv_sem,
+):
+    place, half, rank = line_place()
+    head = 2 * rank + half
+    peers = []
+    for step in range(1, LINE):
+        other = lax.rem(head + step, LINE)
+        peers.append((other, place - half + lax.rem(other, 2), other // 2))
+    barrier = pltpu.get_barrier_semaphore()
+    for _, seq_to, rank_to in peers:
+        pl.semaphore_signal(
+            barrier, inc=1, device_id={"seq": seq_to, "tensor": rank_to}, device_id_type=MESH_ID
+        )
+    gain = vecs[0:1, :]
+    gate = vecs[1:2, :]
+    key_acc[...] = jnp.zeros_like(key_acc)
+    value_acc[...] = jnp.zeros_like(value_acc)
+    dz_sum[...] = jnp.zeros_like(dz_sum)
+    sums[...] = jnp.zeros_like(sums)
+    grad_in[...] = jnp.zeros_like(grad_in)
+
+    def back_parts(parts, total, grad, values):
+        weights = [jnp.exp(part - total) for part in parts]
+        d_weights = [dot_nt(grad, value) for value in values]
+        inner = jnp.sum(weights[0] * d_weights[0], axis=-1, keepdims=True)
+        for one, other in zip(weights[1:], d_weights[1:]):
+            inner = inner + jnp.sum(one * other, axis=-1, keepdims=True)
+        d_scores = [to_low(one * (other - inner)) for one, other in zip(weights, d_weights)]
+        return [to_low(one) for one in weights], d_scores
+
+    def token_back(block_id):
+        prev_id = jnp.maximum(block_id - 1, 0)
+        st_key[...] = jnp.zeros_like(st_key)
+        st_value[...] = jnp.zeros_like(st_value)
+
+        def one_chunk(chunk, _):
+            rows = span(chunk, ROWS)
+            query, parts = token_scores(scal, qkv, qkvst, bias, block_id, chunk)
+            grad = d_o[block_id, rows, :]
+            keys = (qkv[prev_id, :, 128:256], qkv[block_id, :, 128:256], qkvst[block_id, :, 128:256])
+            values = (
+                qkv[prev_id, :, 256:384], qkv[block_id, :, 256:384], qkvst[block_id, :, 256:384]
+            )
+            weights, d_scores = back_parts(parts, lse_tok[block_id, rows, :], grad, values)
+            d_query = dot_nn(d_scores[0], keys[0])
+            d_query = d_query + dot_nn(d_scores[1], keys[1]) + dot_nn(d_scores[2], keys[2])
+            d_qkv[block_id, rows, 0:128] = to_low(d_query * SCALE)
+            key_acc[prev_id] += dot_tn(d_scores[0], query) * SCALE
+            value_acc[prev_id] += dot_tn(weights[0], grad)
+            key_acc[block_id] += dot_tn(d_scores[1], query) * SCALE
+            value_acc[block_id] += dot_tn(weights[1], grad)
+            st_key[...] += dot_tn(d_scores[2], query) * SCALE
+            st_value[...] += dot_tn(weights[2], grad)
+            dz_sum[rows, 0:BLOCK] += d_scores[0].astype(jnp.float32)
+            dz_sum[rows, BLOCK : 2 * BLOCK] += d_scores[1].astype(jnp.float32)
+            return 0
+
+        lax.fori_loop(0, CHUNKS, one_chunk, 0)
+
+    token_back(3)
+    pl.semaphore_wait(barrier, LINE - 1)
+
+    def mixed_copy(block_id, slot, sender, other, seq_to, rank_to):
+        return pltpu.make_async_remote_copy(
+            src_ref=dos_rows.at[block_id, :, span(other, 128)],
+            dst_ref=dos_got.at[block_id, span(sender, 64), :],
+            send_sem=send_sem.at[0, block_id, slot],
+            recv_sem=recv_sem.at[0, block_id, sender],
+            device_id={"seq": seq_to, "tensor": rank_to},
+            device_id_type=MESH_ID,
+        )
+
+    def grads_copy(block_id, slot, sender, other, seq_to, rank_to):
+        return pltpu.make_async_remote_copy(
+            src_ref=d_qkvst.at[block_id, span(other, 64), :],
+            dst_ref=d_got.at[block_id, sender],
+            send_sem=send_sem.at[1, block_id, slot],
+            recv_sem=recv_sem.at[1, block_id, sender],
+            device_id={"seq": seq_to, "tensor": rank_to},
+            device_id_type=MESH_ID,
+        )
+
+    def one_block(turn, _):
+        block_id = 3 - turn
+        grad_out = grad_in[...] + cots[block_id].astype(jnp.float32)
+        sums[0:1, :] += jnp.sum(
+            grad_out * (states[block_id] - states[block_id + 1]), axis=0, keepdims=True
+        ) * gate
+        change = to_low((1.0 - gate) * grad_out)
+        du_rows[block_id] = change
+        dos_rows[block_id] = to_low(dot_nt(change, w_sout[...]))
+        for slot, (other, seq_to, rank_to) in enumerate(peers):
+            mixed_copy(block_id, slot, head, other, seq_to, rank_to).start()
+        dos_got[block_id, span(head, 64), :] = dos_rows[block_id, :, span(head, 128)]
+        for slot, (other, seq_to, rank_to) in enumerate(peers):
+            mixed_copy(block_id, slot, other, other, seq_to, rank_to).wait_recv()
+
+        def one_chunk(chunk, _):
+            rows = span(chunk, ROWS)
+            query, parts = state_scores(scal, qkv, qkvst, block_id, chunk)
+            grad = dos_got[block_id, rows, :]
+            keys = (qkv[block_id, :, 128:256], qkvst[block_id, :, 128:256])
+            values = (qkv[block_id, :, 256:384], qkvst[block_id, :, 256:384])
+            weights, d_scores = back_parts(parts, lse_st[block_id, rows, :], grad, values)
+            d_query = dot_nn(d_scores[0], keys[0]) + dot_nn(d_scores[1], keys[1])
+            d_qkvst[block_id, rows, 0:128] = to_low(d_query * SCALE)
+            key_acc[block_id] += dot_tn(d_scores[0], query) * SCALE
+            value_acc[block_id] += dot_tn(weights[0], grad)
+            st_key[...] += dot_tn(d_scores[1], query) * SCALE
+            st_value[...] += dot_tn(weights[1], grad)
+            return 0
+
+        lax.fori_loop(0, CHUNKS, one_chunk, 0)
+        d_qkvst[block_id, :, 128:256] = to_low(st_key[...])
+        d_qkvst[block_id, :, 256:384] = to_low(st_value[...])
+        for slot, (other, seq_to, rank_to) in enumerate(peers):
+            grads_copy(block_id, slot, head, other, seq_to, rank_to).start()
+        d_got[block_id, head] = d_qkvst[block_id, span(head, 64), :]
+
+        @pl.when(turn < 3)
+        def _():
+            token_back(block_id - 1)
+
+        d_qkv[block_id, :, 128:256] = to_low(key_acc[block_id])
+        d_qkv[block_id, :, 256:384] = to_low(value_acc[block_id])
+        for slot, (other, seq_to, rank_to) in enumerate(peers):
+            grads_copy(block_id, slot, other, other, seq_to, rank_to).wait_recv()
+        d_low = dot_nn(d_got[block_id, 0], w_back[0])
+        for other in range(1, LINE):
+            d_low = d_low + dot_nn(d_got[block_id, other], w_back[other])
+        centered, scale = norm_parts(states[block_id])
+        normed = centered * scale
+        sums[1:2, :] += jnp.sum(d_low * normed, axis=0, keepdims=True)
+        lifted = d_low * gain
+        grad_in[...] = gate * grad_out + scale * (
+            lifted
+            - jnp.mean(lifted, axis=-1, keepdims=True)
+            - normed * jnp.mean(lifted * normed, axis=-1, keepdims=True)
+        )
+        return 0
+
+    lax.fori_loop(0, 4, one_block, 0)
+    d_start[...] = grad_in[...]
+
+    def drain(block_id, _):
+        for slot, (other, seq_to, rank_to) in enumerate(peers):
+            mixed_copy(block_id, slot, head, other, seq_to, rank_to).wait_send()
+            grads_copy(block_id, slot, head, other, seq_to, rank_to).wait_send()
+        return 0
+
+    lax.fori_loop(0, 4, drain, 0)
+
+
+def backward_chain(scal, qkv, d_o, lse_tok, qkvst, lse_st, states, cots, w_back, w_sout, vecs, bias):
+    low, wide = jnp.bfloat16, jnp.float32
+    shapes = (
+        ((4, BLOCK, 384), low),
+        ((4, STATES, 384), low),
+        ((4, 64, D), low),
+        ((64, D), wide),
+        ((8, D), wide),
+        ((BLOCK, 2 * BLOCK), wide),
+    )
+    return pl.pallas_call(
+        backward_kernel,
+        out_shape=[jax.ShapeDtypeStruct(*one) for one in shapes],
+        in_specs=[pl.BlockSpec(memory_space=pltpu.SMEM)] + vmem_specs(11),
+        out_specs=vmem_specs(6),
+        scratch_shapes=[
+            pltpu.VMEM((4, BLOCK, 128), wide),
+            pltpu.VMEM((4, BLOCK, 128), wide),
+            pltpu.VMEM((STATES, 128), wide),
+            pltpu.VMEM((STATES, 128), wide),
+            pltpu.VMEM((4, 64, D), low),
+            pltpu.VMEM((4, STATES, 128), low),
+            pltpu.VMEM((4, LINE, 64, 384), low),
+            pltpu.VMEM((64, D), wide),
+            pltpu.SemaphoreType.DMA((2, 4, LINE - 1)),
+            pltpu.SemaphoreType.DMA((2, 4, LINE)),
+        ],
+        compiler_params=pltpu.CompilerParams(
+            collective_id=2, has_side_effects=True, vmem_limit_bytes=VMEM_LIMIT
+        ),
+        cost_estimate=pl.CostEstimate(flops=40000000000, bytes_accessed=40000000, transcendentals=0),
+        name="backward_chain",
+    )(scal, qkv, d_o, lse_tok, qkvst, lse_st, states, cots, w_back, w_sout, vecs, bias)
+
+
+WIDE = 2048
+
+
+def bias_kernel(line, table):
+    first = line[...]
+    row = lax.broadcasted_iota(jnp.int32, (8, WIDE), 0)
+    for step in (1, 2, 4):
+        first = jnp.where(row // step % 2 == 1, pltpu.roll(first, step, 1), first)
+
+    def one(group, _):
+        table[span(group, 8), :] = pltpu.roll(first, 8 * group, 1)[:, 0 : 2 * BLOCK]
+        return 0
+
+    lax.fori_loop(0, BLOCK // 8, one, 0)
+
+
+def bias_table(line):
+    return pl.pallas_call(
+        bias_kernel,
+        out_shape=jax.ShapeDtypeStruct((BLOCK, 2 * BLOCK), jnp.float32),
+        in_specs=vmem_specs(1),
+        out_specs=pl.BlockSpec(memory_space=pltpu.VMEM),
+        compiler_params=pltpu.CompilerParams(vmem_limit_bytes=VMEM_LIMIT),
+        name="bias_table",
+    )(line)
+
+
+def diagonal_kernel(table, out, acc):
+    acc[...] = jnp.zeros_like(acc)
+
+    def one(group, _):
+        rows = table[span(group, 8), :]
+        wide = jnp.concatenate([rows, jnp.zeros((8, WIDE - 2 * BLOCK), jnp.float32)], axis=1)
+        acc[...] += pltpu.roll(wide, lax.rem(WIDE - 8 * group, WIDE), 1)
+        return 0
+
+    lax.fori_loop(0, BLOCK // 8, one, 0)
+    total = acc[...]
+    row = lax.broadcasted_iota(jnp.int32, (8, WIDE), 0)
+    for step in (1, 2, 4):
+        total = jnp.where(row // step % 2 == 1, pltpu.roll(total, WIDE - step, 1), total)
+    out[...] = jnp.broadcast_to(jnp.sum(total, axis=0, keepdims=True), (8, WIDE))
+
+
+def diagonal_sums(table):
+    return pl.pallas_call(
+        diagonal_kernel,
+        out_shape=jax.ShapeDtypeStruct((8, WIDE), jnp.float32),
+        in_specs=vmem_specs(1),
+        out_specs=pl.BlockSpec(memory_space=pltpu.VMEM),
+        scratch_shapes=[pltpu.VMEM((8, WIDE), jnp.float32)],
+        compiler_params=pltpu.CompilerParams(vmem_limit_bytes=VMEM_LIMIT),
+        name="diagonal_sums",
+    )(table)
+
+
+def own_half(part, half, axis):
+    empty = jnp.zeros_like(part)
+    return jnp.where(
+        half == 0,
+        jnp.concatenate([part, empty], axis=axis),
+        jnp.concatenate([empty, part], axis=axis),
+    )
+
+
+def swap_seq(value):
+    return lax.all_to_all(value, "seq", 0, 0, tiled=False)
+
+
+def line_body(
+    inputs,
+    seg_starts,
+    lengths,
+    init_state,
+    attn_gain,
+    state_gain,
+    mlp_gain,
+    w_query,
+    w_key,
+    w_value,
+    w_out,
+    w_squery,
+    w_sout,
+    w_up,
+    w_down,
+    rel_bias,
+    gate_bias,
+    out_cot,
+    state_cot,
+):
+    low, wide = jnp.bfloat16, jnp.float32
+    place = lax.axis_index("seq")
+    half = lax.rem(place, 2)
+    mine = place // 2
+    head_of = lambda weight: lax.dynamic_slice_in_dim(weight, half * 128, 128, 1)
+    gate_value = jax.nn.sigmoid(gate_bias)
+    vecs = jnp.stack([state_gain, gate_value] + [jnp.zeros_like(gate_value)] * 6)
+    offsets = lax.rem(jnp.arange(WIDE) + WIDE - BLOCK, WIDE)
+    offsets = jnp.arange(WIDE) - BLOCK
+    offsets = jnp.where(offsets >= WIDE - 2 * BLOCK, offsets - WIDE, offsets)
+    bucket_ids = bucket_of(offsets)
+    one_hot = (bucket_ids[:, None] == jnp.arange(BUCKETS)[None, :]).astype(wide)
+    my_bias = jnp.where(half == 0, rel_bias[:, 0], rel_bias[:, 1])
+    bias_line = jnp.sum(one_hot * my_bias[None, :], axis=1)
+    bias = bias_table(jnp.broadcast_to(bias_line[None, :], (8, WIDE)))
+    segs = lax.all_gather(seg_starts[:, 0], "seq", axis=1, tiled=False)
+    scal = jnp.concatenate(
+        [lax.dynamic_slice_in_dim(lengths, mine, 1, 0), lax.dynamic_slice_in_dim(segs, mine, 1, 0)[0]]
+    )
+
+    inputs_wide = inputs.astype(wide)
+    tokens_low = gather_rows(to_low(layer_norm(inputs_wide, attn_gain)))
+    w_qkv = jnp.stack(
+        [w.reshape(D, 2, 128) for w in (w_query, w_key, w_value)], axis=2
+    ).reshape(D, 2, 384)
+    qkv_native = to_low(
+        jnp.einsum("sqd,dhe->shqe", tokens_low, w_qkv, preferred_element_type=wide)
+    )
+    qkv = swap_seq(qkv_native.reshape(4, BLOCK, 384))
+    start_all = lax.all_gather(to_low(init_state), "tensor", axis=0, tiled=True)
+    w_sout_all = lax.all_gather(w_sout, "tensor", axis=0, tiled=True)
+    w_state = jnp.concatenate([head_of(w_squery), head_of(w_key), head_of(w_value)], axis=1)
+    mixed, lse_tok, state_rows, state_low, qkvst, lse_st, os_rows = forward_chain(
+        scal, qkv, start_all, w_state, w_sout_all, vecs, bias
+    )
+    other_block = lax.rem(place + 2, 4)
+    sent = lax.dynamic_slice_in_dim(state_rows, other_block, 1, 0)[0].astype(low)
+    came = lax.ppermute(sent, "seq", [(source, (source + 2) % 4) for source in range(4)])
+    kept = lax.dynamic_slice_in_dim(state_rows, place, 1, 0)[0]
+    state_out = jnp.where(
+        mine == 0, jnp.stack([kept, came.astype(wide)]), jnp.stack([came.astype(wide), kept])
+    )
+
+    mixed_native = swap_seq(mixed).reshape(2, 2, BLOCK, 128)
+    w_out_heads = w_out.reshape(2, 128, D)
+    hidden_in = inputs_wide + sum_rows(
+        jnp.einsum("shqe,hed->sqd", mixed_native, w_out_heads, preferred_element_type=wide)
+    )
+    mid_low = gather_rows(to_low(layer_norm(hidden_in, mlp_gain)))
+    pre_act = matmul(mid_low, w_up)
+    hidden_low = to_low(jax.nn.gelu(pre_act))
+    mlp_rows = sum_rows(matmul(hidden_low, w_down))
+    tokens_out = (hidden_in + mlp_rows).astype(low)
+    cot_wide = out_cot.astype(wide)
+    cot_used = gather_rows(out_cot)
+    grad_hidden_act = matmul_t(cot_used, w_down)
+    down_grad = outer_sum(hidden_low, cot_used)
+    grad_pre = to_low(gelu_back(pre_act, grad_hidden_act))
+    up_grad = outer_sum(mid_low, grad_pre)
+    grad_normed_mid = sum_rows(matmul_t(grad_pre, w_up))
+    grad_mid_in, mlp_gain_grad = norm_back(hidden_in, mlp_gain, grad_normed_mid)
+    grad_hidden = cot_wide + grad_mid_in
+    grad_attn_low = gather_rows(to_low(grad_hidden))
+    d_mixed_native = to_low(
+        jnp.einsum("sqd,hed->shqe", grad_attn_low, w_out_heads, preferred_element_type=wide)
+    )
+    out_grad = jnp.einsum(
+        "shqe,sqd->hed", mixed_native, grad_attn_low, preferred_element_type=wide
+    ).reshape(256, D)
+    d_mixed = swap_seq(d_mixed_native.reshape(4, BLOCK, 128))
+
+    cots = swap_seq(state_cot.reshape(4, 64, D))
+    w_back_own = jnp.concatenate(
+        [w.T.reshape(2, 128, D) for w in (w_squery, w_key, w_value)], axis=1
+    )
+    w_back = lax.all_gather(w_back_own, "tensor", axis=0, tiled=True)
+    start_half = lax.dynamic_slice_in_dim(to_low(init_state).astype(wide), half * 64, 64, 0)
+    states = jnp.concatenate(
+        [start_half[None], lax.dynamic_slice_in_dim(state_rows, half * 64, 64, 1)], axis=0
+    )
+    d_qkv, d_qkvst, du_rows, d_start, sums, dz_sum = backward_chain(
+        scal, qkv, d_mixed, lse_tok, qkvst, lse_st, states, cots, w_back, w_sout_all, vecs, bias
+    )
+    diag = diagonal_sums(dz_sum)[0]
+    bias_grad = own_half(
+        jnp.sum(one_hot * diag[:, None], axis=0)[:, None], half, 1
+    )
+    d_native = swap_seq(d_qkv).reshape(2, 2, BLOCK, 384)
+    grad_tokens = sum_rows(
+        jnp.einsum("shqe,dhe->sqd", d_native, w_qkv, preferred_element_type=wide)
+    )
+    grad_in_norm, attn_gain_grad = norm_back(inputs_wide, attn_gain, grad_tokens)
+    inputs_grad = grad_hidden + grad_in_norm
+    tok_grads = jnp.einsum("sqd,shqe->dhe", tokens_low, d_native, preferred_element_type=wide)
+    st_grads = outer_sum(state_low, d_qkvst)
+    query_grad = tok_grads[:, :, 0:128].reshape(D, 256)
+    key_grad = tok_grads[:, :, 128:256].reshape(D, 256) + own_half(st_grads[:, 128:256], half, 1)
+    value_grad = tok_grads[:, :, 256:384].reshape(D, 256) + own_half(st_grads[:, 256:384], half, 1)
+    squery_grad = own_half(st_grads[:, 0:128], half, 1)
+    sout_part = lax.psum_scatter(
+        outer_sum(os_rows, du_rows).astype(low), "tensor", scatter_dimension=0, tiled=True
+    )
+    state_part = own_half(d_start, half, 0)
+    gains = lax.psum(jnp.stack([attn_gain_grad, sums[1], mlp_gain_grad, sums[0]]), "tensor")
+
+    def total(part):
+        return lax.psum(part.astype(low), ("dp", "seq")).astype(wide)
+
+    gain_total = total(gains)
+    return (
+        tokens_out,
+        state_out[:, None],
+        inputs_grad,
+        total(state_part),
+        gain_total[0],
+        gain_total[1],
+        gain_total[2],
+        total(query_grad),
+        total(key_grad),
+        total(value_grad),
+        total(out_grad),
+        total(squery_grad),
+        total(sout_part),
+        total(up_grad),
+        total(down_grad),
+        total(bias_grad),
+        gain_total[3],
+    )
+
+
 def solution(mesh):
     return jax.shard_map(
-        body,
+        chosen_body(mesh),
         mesh=mesh,
         in_specs=(
             P("dp", ("seq", "tensor"), None),

time: 1470 us -> 986 us (0.67)
  waiting for transfers between devices: 806 us -> 530 us
  matrix products: 260 us -> 58.3 us
  Pallas kernels: 0 us -> 192 us
  other arithmetic: 224 us -> 51.7 us
  local copies, waits for them, and re-layouts: 96.2 us -> 30 us
  blocking collectives: 30.3 us -> 87.6 us
    reduce_scatter x10 -> x1, waiting for transfers between devices: 215 us -> 0.01 us  [line_body(): lax.psum_scatter(outer_sum(os_rows, du_rows).astype(low), 'tensor', scatt...]
    pallas_call x0 -> x4, Pallas kernels: none -> 192 us  [the longest x1 89.3 us: backward_chain(): pl.pallas_call(backward_kernel, out_shape=[jax.ShapeDtypeStruct(*one) for...]
    all_gather x10 -> x3, waiting for transfers between devices: 259 us -> 134 us  [the longest x1 105 us: line_body(): w_back = lax.all_gather(w_back_own, 'tensor', axis=0, tiled=True)]
    dot_general x26 -> x2, matrix products: 75 us -> 12.8 us  [matmul(): jnp.einsum('...k,kn->...n', left, right, preferred_element_type=jnp.float32)]
    psum x1, waiting for transfers between devices: 66.3 us -> 123 us  [total(): return lax.psum(part.astype(low), ('dp', 'seq')).astype(wide)]
    dot_general x41 -> x6, matrix products: 68.9 us -> 18.1 us  [the longest x1 5.04 us: line_body(): jnp.einsum('sqd,dhe->shqe', tokens_low, w_qkv, preferred_element_type=wide)]
    dot_general x26 -> x2, matrix products: 59.5 us -> 11.6 us  [matmul_t(): jnp.einsum('...n,kn->...k', left, right, preferred_element_type=jnp.float32)]
    select_n x35 -> x2, other arithmetic: 48.6 us -> 1.1 us  [the longest x1 1.09 us: line_body(): jnp.where(mine == 0, jnp.stack([kept, came.astype(wide)]), jnp.stack([cam...]
  transfers between devices with their start and end apart: 43 -> 17, of which waited for: 34 -> 12; matrix products, arithmetic and copies ran while one was open for 33% -> 9% of each run, Pallas kernels for 0% -> 2%
where the time goes in v1:
time: 986 us; the launch traced here: 978 us
  waiting for transfers between devices  530 us (54%)
  Pallas kernels  192 us (19%)
  blocking collectives  87.6 us (9%)
  matrix products  58.3 us (6%)
  other arithmetic  51.7 us (5%)
  local copies, waits for them, and re-layouts  30 us (3%)
  between operations  14.9 us (2%)
  starting transfers between devices  13.4 us (1%)
    all_gather x4, waiting for transfers between devices, gather_rows(): return lax.all_gather(values, 'tensor', axis=1, tiled=True)  160 us
    psum x1, waiting for transfers between devices, total(): return lax.psum(part.astype(low), ('dp', 'seq')).astype(wide)  123 us
    all_gather x1, waiting for transfers between devices, line_body(): w_back = lax.all_gather(w_back_own, 'tensor', axis=0, tiled=True)  105 us
    reduce_scatter x4, waiting for transfers between devices, sum_rows(): lax.psum_scatter(terms.astype(jnp.bfloat16), 'tensor', scatter_dimension=...  104 us
    pallas_call x1, Pallas kernels, backward_chain(): pl.pallas_call(backward_kernel, out_shape=[jax.ShapeDtypeStruct(*one) for...  89.3 us
    pallas_call x1, Pallas kernels, forward_chain(): pl.pallas_call(forward_kernel, out_shape=[jax.ShapeDtypeStruct(*one) for...  86.2 us
    all_to_all x2, blocking collectives, swap_seq(): return lax.all_to_all(value, 'seq', 0, 0, tiled=False)  36.4 us
    all_gather x1, waiting for transfers between devices, line_body(): w_sout_all = lax.all_gather(w_sout, 'tensor', axis=0, tiled=True)  28.8 us
  transfers between devices with their start and end apart: 17, of which 12 were waited for; matrix products, arithmetic and copies ran while one was open for 9% of the time, Pallas kernels for 2%

profile of v1, /device:TPU:0, one launch (start us, length us, event | category | flops | bytes accessed | tf_op | source)
XLA Modules:
  0.0 978.3 jit_solution(11123076409730474310)
XLA Ops:
  7.3 1.3 convert_reduce_fusion
  8.6 1.3 fusion.51
  9.9 2.2 fusion.47
  12.2 1.8 convert_element_type.211
  14.8 2.0 copy.109
  18.9 2.7 pad_maximum_fusion
  21.6 39.4 %all-gather.9.cloned.1.call-done = bf16[2,512,1024]{2,1,0:T(8,128)(2,1)} async-done(((bf16[2,128,1024]{2,1,0:T(8,128)(2,1)}), bf16[2,512,1024]{2,1,0:T(8,128)(2,1)}) %all-gather.9.cloned.1.call-update) | async-done | bytes 2097168 | tf_op jit(solution)/shard_map/all_gather | solution.py:91
  61.0 5.0 fusion.36
  66.0 2.6 copy.86
  68.6 4.5 all-to-all-start
  73.2 20.9 %all-gather = s32[4,1,2]{2,1,0:T(1,128)S(1)} all-gather(s32[1,1,2]{2,1,0:T(1,128)S(1)} %bitcast.164), channel_id=1, replica_groups=mesh['dp'=2,'seq'=4,'tensor'=4] {'seq'}, dimensions={0}, use_global_device_ids=true | all-gather | bytes 40 | tf_op jit(solution)/shard_map/all_gather | solution.py:1009
  95.0 8.1 bias_table.1.bias
  107.9 28.8 %all-gather.13.cloned.1.call-done.w_sout = bf16[1024,1024]{1,0:T(8,128)(2,1)} async-done(((bf16[256,1024]{1,0:T(8,128)(2,1)}), bf16[1024,1024]{1,0:T(8,128)(2,1)}) %all-gather.13.cloned.1.call-update) | async-done | bytes 2097168 | tf_op jit(solution)/shard_map/all_gather | solution.py:1024
  136.7 86.2 %forward_chain.1 = (bf16[4,512,128]{2,1,0:T(8,128)(2,1)}, f32[4,512,1]{2,1,0:T(8,128)}, f32[4,128,1024]{2,1,0:T(8,128)}, bf16[4,512,1024]{2,1,0:T(8,128)(2,1)}, ...) custom-call(s32[5]{0:T(128)} %pad_add_fusion.scal, ...), custom_call_target="tpu_custom_call" | custom-call | flops 20000000000 | bytes 20000000 | tf_op jit(solution)/shard_map/forward_chain/pallas_call | solution.py:692
  223.0 12.3 %all_to_all.25 = bf16[4,512,128]{2,1,0:T(8,128)(2,1)S(1)} all-to-all(bf16[4,512,128]{2,1,0:T(8,128)(2,1)} %get-tuple-element.30), channel_id=1, replica_groups=mesh['dp'=2,'seq'=4,'tensor'=4] {'seq'}, dimensions={0} | all-to-all | bytes 1048576 | tf_op jit(solution)/shard_map/all_to_all | solution.py:970
  235.3 3.3 bitcast_convert_fusion.4
  238.6 45.5 %reduce-scatter.6.cloned.1.call-done = bf16[2,128,1024]{2,1,0:T(8,128)(2,1)} async-done(((bf16[2,512,1024]{2,1,0:T(8,128)(2,1)}), bf16[2,128,1024]{2,1,0:T(8,128)(2,1)}) %reduce-scatter.6.cloned.1.call-update) | async-done | bytes 524304 | tf_op jit(solution)/shard_map/reduce_scatter | solution.py:95
  284.2 1.3 fusion.56
  285.5 1.3 multiply_reduce_fusion
  288.7 44.6 %all-gather.15.cloned.1.call-done = bf16[2,512,1024]{2,1,0:T(8,128)(2,1)} async-done(((bf16[2,128,1024]{2,1,0:T(8,128)(2,1)}), bf16[2,512,1024]{2,1,0:T(8,128)(2,1)}) %all-gather.15.cloned.1.call-update) | async-done | bytes 2097168 | tf_op jit(solution)/shard_map/all_gather | solution.py:91
  333.3 5.9 fusion.16
  339.3 40.3 %all-gather.17.cloned.1.call-done = bf16[2,512,1024]{2,1,0:T(8,128)(2,1)} async-done(((bf16[2,128,1024]{2,1,0:T(8,128)(2,1)}), bf16[2,512,1024]{2,1,0:T(8,128)(2,1)}) %all-gather.17.cloned.1.call-update) | async-done | bytes 2097168 | tf_op jit(solution)/shard_map/all_gather | solution.py:91
  379.5 7.9 fusion.6
  387.5 1.4 copy-done.43
  388.9 3.7 fusion.20
  392.6 42.7 %reduce-scatter.10.cloned.1.call-done = bf16[2,128,1024]{2,1,0:T(8,128)(2,1)} async-done(((bf16[2,512,1024]{2,1,0:T(8,128)(2,1)}), bf16[2,128,1024]{2,1,0:T(8,128)(2,1)}) %reduce-scatter.10.cloned.1.call-update) | async-done | bytes 524304 | tf_op jit(solution)/shard_map/reduce_scatter | solution.py:95
  435.3 1.5 fusion.48
  436.9 1.7 fusion.49
  438.6 1.3 fusion.58
  443.3 2.3 pad_maximum_fusion.1
  445.6 3.5 all-to-all-start.3
  449.1 36.2 %all-gather.19.cloned.1.call-done = bf16[2,512,1024]{2,1,0:T(8,128)(2,1)} async-done(((bf16[2,128,1024]{2,1,0:T(8,128)(2,1)}), bf16[2,512,1024]{2,1,0:T(8,128)(2,1)}) %all-gather.19.cloned.1.call-update) | async-done | bytes 2097168 | tf_op jit(solution)/shard_map/all_gather | solution.py:91
  485.3 3.2 fusion.40
  488.6 4.2 all-to-all-start.2
  493.0 1.5 constant_dynamic-slice_fusion
  495.7 105.3 %all-gather.21.cloned.1.call-done.w_back = bf16[8,384,1024]{2,1,0:T(8,128)(2,1)} async-done(((bf16[2,384,1024]{2,1,0:T(8,128)(2,1)}), bf16[8,384,1024]{2,1,0:T(8,128)(2,1)}) %all-gather.21.cloned.1.call-update) | async-done | bytes 6291472 | tf_op jit(solution)/shard_map/all_gather | solution.py:1069
  601.0 89.3 %backward_chain.1 = (bf16[4,512,384]{2,1,0:T(8,128)(2,1)}, bf16[4,512,384]{2,1,0:T(8,128)(2,1)}, bf16[4,64,1024]{2,1,0:T(8,128)(2,1)}, f32[64,1024]{1,0:T(8,128)...) custom-call(s32[5]{0:T(128)} %pad_add_fusion.scal, bf16[4,512,384]{2,1,0:T(8,128)(2,1)} %all-to-all-done.qkv, ...), custom_call_target="tpu_custom_call" | custom-call | flops 40000000000 | bytes 40000000 | tf_op jit(solution)/shard_map/backward_chain/pallas_call | solution.py:879
  690.4 3.1 bitcast_convert_fusion.2
  693.6 24.1 %all_to_all.26 = bf16[4,512,384]{2,1,0:T(8,128)(2,1)S(1)} all-to-all(bf16[4,512,384]{2,1,0:T(8,128)(2,1)} %get-tuple-element.35), channel_id=1, replica_groups=mesh['dp'=2,'seq'=4,'tensor'=4] {'seq'}, dimensions={0} | all-to-all | bytes 3145728 | tf_op jit(solution)/shard_map/all_to_all | solution.py:970
  718.9 3.1 bitcast_convert_fusion.3
  722.1 6.9 fusion.23
  730.2 6.2 bitcast_convert_fusion.1
  736.4 4.1 bitcast_convert_fusion
  740.5 1.5 fusion.39
  742.1 2.4 convolution_bitcast_fusion
  747.2 1.9 fusion.26
  751.1 1.3 copy.95
  752.4 1.6 copy.94
  754.0 2.1 copy.92
  756.0 2.5 add_convert_fusion
  761.8 7.1 collective-permute-done
  770.1 8.6 diagonal_sums.1
  780.5 4.9 reduce-scatter.12.cloned.1.call-done
  785.4 1.4 fusion.52
  786.8 1.7 fusion.50
  788.5 17.2 %psum.85 = bf16[4,1024]{1,0:T(4,128)(2,1)S(1)} all-reduce(f32[4,1024]{1,0:T(4,128)S(1)} %pad_maximum_fusion.4), channel_id=1, replica_groups=mesh['dp'=2,'seq'=4,'tensor'=4] {'tensor'}, use_global_device_ids=true, to_apply=%region_16.17 | all-reduce | flops 4096 | bytes 24576 | tf_op jit(solution)/shard_map/psum | solution.py:1097
  805.7 13.1 %all-reduce.9 = (bf16[4,1024]{1,0:T(4,128)(2,1)S(1)}, bf16[32,2]{0,1:T(2,128)(2,1)S(1)}) all-reduce(bf16[4,1024]{1,0:T(4,128)(2,1)S(1)} %psum.85, bf16[32,2]{0,1:T(2,128)(2,1)S(1)} %select_convert_fusion.1), channel_id=1, replica_groups=mesh['dp'=2,'seq'=4,'tensor'=4] {'dp','seq'}, use_global_device_ids=true, to_apply=%region_17.18 | all-reduce | flops 4160 | bytes 16640 | tf_op jit(solution)/shard_map/psum | solution.py:1100
  820.0 11.0 %reduce-scatter.8.cloned.1.call-done = bf16[2,128,1024]{2,1,0:T(8,128)(2,1)} async-done(((bf16[2,512,1024]{2,1,0:T(8,128)(2,1)}), bf16[2,128,1024]{2,1,0:T(8,128)(2,1)}) %reduce-scatter.8.cloned.1.call-update) | async-done | bytes 524304 | tf_op jit(solution)/shard_map/reduce_scatter | solution.py:95
  831.0 3.0 add_add_fusion.2
  834.0 123.0 %all-reduce.13.cloned.1.call-done = (bf16[128,1024]{1,0:T(8,128)(2,1)}, bf16[1024,256]{1,0:T(8,128)(2,1)}, bf16[1024,256]{1,0:T(8,128)(2,1)}, bf16[1024,256]{1,0...) async-done(((bf16[128,1024]{1,0:T(8,128)(2,1)}, ...) | async-done | bytes 7602192 | tf_op jit(solution)/shard_map/psum | solution.py:1100
  957.0 1.9 convert_element_type.239
  958.9 2.1 convert_element_type.243
  966.3 2.5 convert_element_type.255
  968.8 2.5 convert_element_type.257
  (175 shorter events, 35.5 us)
Async XLA Ops:
  7.2 326.2 %copy-start = (bf16[1024,1024]{1,0:T(8,128)(2,1)S(1)}, bf16[1024,1024]{1,0:T(8,128)(2,1)}, u32[]{:S(2)}) copy-start(bf16[1024,1024]{1,0:T(8,128)(2,1)} %param.32) | copy-start | bytes 6291460
  7.2 53.8 %all-gather.9.cloned.1.call-start = ((), (), s32[]{:S(2)}) async-start(), calls=%async_computation.10 | async-start | bytes 2621440 | tf_op jit(solution)/shard_map/all_gather | solution.py:91
  9.9 6.9 copy-start.11
  12.1 5.7 copy-start.9
  12.2 95.7 %all-gather.11.cloned.1.call-start = ((), (), s32[]{:S(2)}) async-start(), calls=%async_computation.11 | async-start | bytes 1310720 | tf_op jit(solution)/shard_map/all_gather | solution.py:1023
  14.1 122.6 %all-gather.13.cloned.1.call-start = ((), (), s32[]{:S(2)}) async-start(), calls=%async_computation.12 | async-start | bytes 2621440 | tf_op jit(solution)/shard_map/all_gather | solution.py:1024
  68.6 4.6 copy-start.32
  68.6 4.6 copy-start.34
  68.6 34.5 %copy-start.38 = (s32[2]{0:T(128)S(1)}, s32[2]{0:T(128)}, u32[]{:S(2)}) copy-start(s32[2]{0:T(128)} %param.21) | copy-start | bytes 28
  68.6 68.1 %all-to-all-start = ((bf16[4,512,384]{2,1,0:T(8,128)(2,1)}), bf16[4,512,384]{2,1,0:T(8,128)(2,1)}, u32[]{:S(2)}, u32[]{:S(2)}) async-start(bf16[4,512,384]{2,1,0:T(8,128)(2,1)} %bitcast.131), calls=%async_computation | async-start | bytes 3145728 | tf_op jit(solution)/shard_map/all_to_all | solution.py:970
  73.1 211.1 %reduce-scatter.6.cloned.1.call-start = ((), (), s32[]{:S(2)}) async-start(), calls=%async_computation.13 | async-start | bytes 2621440 | tf_op jit(solution)/shard_map/reduce_scatter | solution.py:95
  103.1 4.1 copy-start.30
  103.1 4.1 copy-start.31
  235.3 3.3 copy-start.7
  235.3 48.9 %copy-start.2 = (bf16[2,128,1024]{2,1,0:T(8,128)(2,1)S(1)}, bf16[2,128,1024]{2,1,0:T(8,128)(2,1)}, u32[]{:S(2)}) copy-start(bf16[2,128,1024]{2,1,0:T(8,128)(2,1)} %param.19) | copy-start | bytes 1572868
  238.6 48.3 %copy-start.28 = (f32[1024]{0:T(1024)S(1)}, f32[1024]{0:T(1024)}, u32[]{:S(2)}) copy-start(f32[1024]{0:T(1024)} %param.25) | copy-start | bytes 12292
  238.6 94.8 %all-gather.15.cloned.1.call-start = ((), (), s32[]{:S(2)}) async-start(), calls=%async_computation.14 | async-start | bytes 2621440 | tf_op jit(solution)/shard_map/all_gather | solution.py:91
  284.2 2.7 copy-start.3
  287.9 91.6 %all-gather.17.cloned.1.call-start = ((), (), s32[]{:S(2)}) async-start(), calls=%async_computation.16 | async-start | bytes 2621440 | tf_op jit(solution)/shard_map/all_gather | solution.py:91
  288.5 146.8 %reduce-scatter.10.cloned.1.call-start = ((), (), s32[]{:S(2)}) async-start(), calls=%async_computation.17 | async-start | bytes 2621440 | tf_op jit(solution)/shard_map/reduce_scatter | solution.py:95
  387.5 1.4 copy-start.43
  392.6 46.0 %copy-start.5 = (bf16[2,128,1024]{2,1,0:T(8,128)(2,1)S(1)}, bf16[2,128,1024]{2,1,0:T(8,128)(2,1)}, u32[]{:S(2)}) copy-start(bf16[2,128,1024]{2,1,0:T(8,128)(2,1)} %param.36) | copy-start | bytes 1572868
  392.6 92.7 %all-gather.19.cloned.1.call-start = ((), (), s32[]{:S(2)}) async-start(), calls=%async_computation.18 | async-start | bytes 2621440 | tf_op jit(solution)/shard_map/all_gather | solution.py:91
  435.3 3.3 copy-start.4
  436.8 3.1 copy-start.10
  438.6 2.4 copy-start.12
  439.9 161.1 %all-gather.21.cloned.1.call-start = ((), (), s32[]{:S(2)}) async-start(), calls=%async_computation.19 | async-start | bytes 7864320 | tf_op jit(solution)/shard_map/all_gather | solution.py:1069
  441.0 2.3 copy-start.16
  445.6 42.9 %all-to-all-start.3 = ((bf16[4,64,1024]{2,1,0:T(8,128)(2,1)}), bf16[4,64,1024]{2,1,0:T(8,128)(2,1)S(1)}, u32[]{:S(2)}, u32[]{:S(2)}) async-start(bf16[4,64,1024]{2,1,0:T(8,128)(2,1)} %bitcast.150), calls=%async_computation.6 | async-start | bytes 1048576 | tf_op jit(solution)/shard_map/all_to_all | solution.py:970
  449.1 43.8 %copy-start.17 = (bf16[128,1024]{1,0:T(8,128)(2,1)S(1)}, bf16[128,1024]{1,0:T(8,128)(2,1)}, u32[]{:S(2)}) copy-start(bf16[128,1024]{1,0:T(8,128)(2,1)} %convert_element_type.211) | copy-start | bytes 786436
  488.6 4.5 copy-start.26
  488.6 112.5 %all-to-all-start.2 = ((bf16[4,512,128]{2,1,0:T(8,128)(2,1)}), bf16[4,512,128]{2,1,0:T(8,128)(2,1)}, u32[]{:S(2)}, u32[]{:S(2)}) async-start(bf16[4,512,128]{2,1,0:T(8,128)(2,1)} %bitcast.151), calls=%async_computation.5 | async-start | bytes 1048576 | tf_op jit(solution)/shard_map/all_to_all | solution.py:970
  492.7 266.8 %reduce-scatter.14.cloned.1.call-start = ((), (), s32[]{:S(2)}) async-start(), calls=%async_computation.21 | async-start | bytes 2621440 | tf_op jit(solution)/shard_map/reduce_scatter | solution.py:1093
  601.0 89.3 %copy-start.41 = (bf16[4,64,1024]{2,1,0:T(8,128)(2,1)S(1)}, bf16[4,64,1024]{2,1,0:T(8,128)(2,1)}, u32[]{:S(2)}) copy-start(bf16[4,64,1024]{2,1,0:T(8,128)(2,1)} %get-tuple-element.40) | copy-start | bytes 1572868
  693.5 91.9 %reduce-scatter.12.cloned.1.call-start = ((), (), s32[]{:S(2)}) async-start(), calls=%async_computation.20 | async-start | bytes 2621440 | tf_op jit(solution)/shard_map/reduce_scatter | solution.py:95
  693.6 25.3 %copy-start.18 = (bf16[1024,2,3,128]{0,3,2,1:T(8,128)(2,1)S(1)}, bf16[1024,2,3,128]{0,3,2,1:T(8,128)(2,1)}, u32[]{:S(2)}) copy-start(bf16[1024,2,3,128]{0,3,2,1:T(8,128)(2,1)} %pad_maximum_fusion) | copy-start | bytes 4718596
  717.7 1.2 copy-start.19
  722.0 108.9 %reduce-scatter.8.cloned.1.call-start = ((), (), s32[]{:S(2)}) async-start(), calls=%async_computation.15 | async-start | bytes 2621440 | tf_op jit(solution)/shard_map/reduce_scatter | solution.py:95
  729.0 1.0 copy-start.8
  729.0 228.0 %all-reduce.13.cloned.1.call-start = ((), (), s32[]{:S(2)}) async-start(), calls=%async_computation.22 | async-start | bytes 15204352 | tf_op jit(solution)/shard_map/psum | solution.py:1100
  730.2 6.2 copy-start.36
  730.2 6.2 copy-start.42
  736.4 4.1 copy-start.37
  736.4 5.6 copy-start.39
  740.5 1.6 copy-start.40
  742.1 2.5 copy-start.27
  744.4 1.9 copy-start.33
  744.5 2.7 copy-start.20
  744.5 2.7 copy-start.35
  756.0 2.5 copy-start.15
  760.6 8.3 collective-permute-start
  769.0 16.4 %copy-start.29 = (f32[1024]{0:T(1024)S(1)}, f32[1024]{0:T(1024)}, u32[]{:S(2)}) copy-start(f32[1024]{0:T(1024)} %param.23) | copy-start | bytes 12292
  785.4 45.6 %copy-start.6 = (bf16[2,128,1024]{2,1,0:T(8,128)(2,1)S(1)}, bf16[2,128,1024]{2,1,0:T(8,128)(2,1)}, u32[]{:S(2)}) copy-start(bf16[2,128,1024]{2,1,0:T(8,128)(2,1)} %reduce-scatter.12.cloned.1.call-done) | copy-start | bytes 1572868
  957.0 4.0 copy-start.25
  957.0 5.1 copy-start.24
  958.9 4.3 copy-start.23
  961.0 3.2 copy-start.22
  962.1 3.2 copy-start.21
  963.1 3.2 copy-start.14
  966.3 2.5 copy-start.13
  968.8 2.5 copy-start.1
Sparse Core Ops, SparseCore 0:
  12.3 48.6 all-gather.8
  63.1 26.6 all-gather.10
  91.4 45.3 all-gather.12
  238.7 45.4 reduce-scatter.5
  288.0 45.2 all-gather.14
  334.9 44.6 all-gather.16
  392.7 42.5 reduce-scatter.9
  440.1 45.2 all-gather.18
  486.9 114.0 all-gather.20
  693.6 45.4 reduce-scatter.13
  742.1 43.1 reduce-scatter.11
  787.5 43.3 reduce-scatter.7
  837.2 119.7 all-reduce.12

commit v2 on v1

--- a/solution.py
+++ b/solution.py
@@ -901,6 +901,336 @@
     )(scal, qkv, d_o, lse_tok, qkvst, lse_st, states, cots, w_back, w_sout, vecs, bias)
 
 
+def plane_place():
+    place, half, rank = line_place()
+    side = lax.axis_index("dp")
+    return side, place, half, rank
+
+
+def plane_index(side, place):
+    return 4 * side + place
+
+
+def plane_gather(buf, rows, send_sem, recv_sem):
+    side, place, half, rank = plane_place()
+    across, beside = 1 - side, lax.rem(place + 2, 4)
+    core = place + 1 - 2 * half
+    me = plane_index(side, place)
+    at_x, at_y = plane_index(across, place), plane_index(side, beside)
+    at_d = plane_index(across, beside)
+    to_x = {"dp": across}
+    to_y = {"seq": beside}
+    to_c = {"seq": core}
+    size = rows // 2
+
+    def piece(owner, part, slot, target):
+        view = buf.at[owner, pl.ds(part * size, size), :]
+        return pltpu.make_async_remote_copy(
+            src_ref=view,
+            dst_ref=view,
+            send_sem=send_sem.at[slot],
+            recv_sem=recv_sem.at[owner, part],
+            device_id=target,
+            device_id_type=MESH_ID,
+        )
+
+    sent = []
+
+    def send(owner, part, target):
+        one = piece(owner, part, len(sent), target)
+        sent.append(one)
+        one.start()
+
+    def arrived(owner, part):
+        piece(owner, part, 0, to_c).wait_recv()
+
+    send(me, 0, to_x)
+    send(me, 1, to_y)
+    send(me, 1, to_x)
+    send(me, 0, to_y)
+    send(me, 0, to_c)
+    send(me, 1, to_c)
+    arrived(at_x, 0)
+    send(at_x, 0, to_y)
+    arrived(at_y, 1)
+    send(at_y, 1, to_x)
+    send(at_x, 0, to_c)
+    send(at_y, 1, to_c)
+    arrived(at_x, 1)
+    send(at_x, 1, to_c)
+    arrived(at_y, 0)
+    send(at_y, 0, to_c)
+    arrived(at_d, 0)
+    send(at_d, 0, to_c)
+    arrived(at_d, 1)
+    send(at_d, 1, to_c)
+    for owner in (
+        plane_index(side, core),
+        plane_index(across, core),
+        plane_index(side, lax.rem(core + 2, 4)),
+        plane_index(across, lax.rem(core + 2, 4)),
+    ):
+        arrived(owner, 0)
+        arrived(owner, 1)
+    for one in sent:
+        one.wait_send()
+
+
+def plane_scatter(part, core_got, near_got, far_got, total, rows, send_sem, recv_sem):
+    side, place, half, rank = plane_place()
+    across, beside = 1 - side, lax.rem(place + 2, 4)
+    core = place + 1 - 2 * half
+    me = plane_index(side, place)
+    at_x, at_y = plane_index(across, place), plane_index(side, beside)
+    at_d = plane_index(across, beside)
+    size = rows // 2
+    halves = (pl.ds(0, size), pl.ds(size, size))
+
+    def moved(source, target_ref, slot, target):
+        return pltpu.make_async_remote_copy(
+            src_ref=source,
+            dst_ref=target_ref,
+            send_sem=send_sem.at[slot],
+            recv_sem=recv_sem.at[slot],
+            device_id=target,
+            device_id_type=MESH_ID,
+        )
+
+    order = (at_d, at_x, at_y, me)
+    swapped = (
+        plane_index(across, lax.rem(core + 2, 4)),
+        plane_index(across, core),
+        plane_index(side, lax.rem(core + 2, 4)),
+        plane_index(side, core),
+    )
+    first = [
+        moved(part.at[owner], core_got.at[slot], slot, {"seq": core})
+        for slot, owner in enumerate(swapped)
+    ]
+    for one in first:
+        one.start()
+
+    def add_into(owner, view, other):
+        part[owner, view, :] = to_low(
+            part[owner, view, :].astype(jnp.float32) + other.astype(jnp.float32)
+        )
+
+    near = [
+        moved(part.at[at_d, halves[0], :], near_got.at[0], 4, {"dp": across}),
+        moved(part.at[at_d, halves[1], :], near_got.at[1], 5, {"seq": beside}),
+        moved(part.at[at_x, halves[0], :], near_got.at[2], 6, {"dp": across}),
+        moved(part.at[at_y, halves[1], :], near_got.at[3], 7, {"seq": beside}),
+    ]
+    for slot, owner in enumerate(order):
+        first[slot].wait_recv()
+        for view in halves:
+            add_into(owner, view, core_got[slot, view, :])
+        if slot == 0:
+            near[0].start()
+            near[1].start()
+        if slot == 1:
+            near[2].start()
+        if slot == 2:
+            near[3].start()
+    near[0].wait_recv()
+    add_into(at_y, halves[0], near_got[0])
+    far = [
+        moved(part.at[at_y, halves[0], :], far_got.at[0], 8, {"seq": beside}),
+        moved(part.at[at_x, halves[1], :], far_got.at[1], 9, {"dp": across}),
+    ]
+    far[0].start()
+    near[1].wait_recv()
+    add_into(at_x, halves[1], near_got[1])
+    far[1].start()
+    near[2].wait_recv()
+    add_into(me, halves[0], near_got[2])
+    near[3].wait_recv()
+    add_into(me, halves[1], near_got[3])
+    for slot, view in enumerate(halves):
+        far[slot].wait_recv()
+        total[view, :] = part[me, view, :].astype(jnp.float32) + far_got[slot].astype(jnp.float32)
+    for one in first + near + far:
+        one.wait_send()
+
+
+def group_peers():
+    place, half, rank = line_place()
+    here = 4 * place + rank
+    peers = []
+    for step in range(1, 16):
+        other = lax.rem(here + step, 16)
+        peers.append((other, other // 4, lax.rem(other, 4)))
+    return here, peers
+
+
+def greet(peers):
+    side = lax.axis_index("dp")
+    barrier = pltpu.get_barrier_semaphore()
+    for _, seq_to, rank_to in peers:
+        pl.semaphore_signal(
+            barrier, inc=1, device_id={"seq": seq_to, "tensor": rank_to}, device_id_type=MESH_ID
+        )
+    pl.semaphore_signal(barrier, inc=1, device_id={"dp": 1 - side}, device_id_type=MESH_ID)
+    pl.semaphore_wait(barrier, len(peers) + 1)
+
+
+def middle_forward_kernel(
+    mixed, tokens, w_out, vecs,
+    hidden, mixed_rows, mid_all,
+    send_sem, recv_sem, ring_send, ring_recv,
+):
+    side, place, half, rank = plane_place()
+    mine = place // 2
+    head = 2 * rank + half
+    here, peers = group_peers()
+    greet(peers)
+
+    def rows_copy(slot, sender, seq_from, rank_from, seq_to, rank_to):
+        return pltpu.make_async_remote_copy(
+            src_ref=mixed.at[seq_to, span(rank_to, 128), :],
+            dst_ref=mixed_rows.at[
+                seq_from // 2, :, span(2 * rank_from + lax.rem(seq_from, 2), 128)
+            ],
+            send_sem=send_sem.at[slot],
+            recv_sem=recv_sem.at[sender],
+            device_id={"seq": seq_to, "tensor": rank_to},
+            device_id_type=MESH_ID,
+        )
+
+    for slot, (_, seq_to, rank_to) in enumerate(peers):
+        rows_copy(slot, here, place, rank, seq_to, rank_to).start()
+    mixed_rows[mine, :, span(head, 128)] = mixed[place, span(rank, 128), :]
+    for slot, (other, seq_to, rank_to) in enumerate(peers):
+        rows_copy(slot, other, seq_to, rank_to, seq_to, rank_to).wait_recv()
+    me = plane_index(side, place)
+    gain = vecs[2:3, :]
+
+    def one(which, _):
+        added = dot_nn(mixed_rows[which], w_out[...]) + tokens[which].astype(jnp.float32)
+        hidden[which] = added
+        centered, scale = norm_parts(added)
+        mid_all[me, span(which, 128), :] = to_low(centered * scale * gain)
+        return 0
+
+    lax.fori_loop(0, 2, one, 0)
+    plane_gather(mid_all, 256, ring_send, ring_recv)
+    for slot, (_, seq_to, rank_to) in enumerate(peers):
+        rows_copy(slot, here, place, rank, seq_to, rank_to).wait_send()
+
+
+def middle_forward(mixed, tokens, w_out, vecs):
+    low, wide = jnp.bfloat16, jnp.float32
+    shapes = (((2, 128, D), wide), ((2, 128, D), low), ((8, 256, D), low))
+    return pl.pallas_call(
+        middle_forward_kernel,
+        out_shape=[jax.ShapeDtypeStruct(*one) for one in shapes],
+        in_specs=vmem_specs(4),
+        out_specs=vmem_specs(3),
+        scratch_shapes=[
+            pltpu.SemaphoreType.DMA((15,)),
+            pltpu.SemaphoreType.DMA((16,)),
+            pltpu.SemaphoreType.DMA((16,)),
+            pltpu.SemaphoreType.DMA((8, 2)),
+        ],
+        compiler_params=pltpu.CompilerParams(
+            collective_id=3, has_side_effects=True, vmem_limit_bytes=VMEM_LIMIT
+        ),
+        cost_estimate=pl.CostEstimate(
+            flops=30000000000, bytes_accessed=30000000, transcendentals=0
+        ),
+        name="middle_forward",
+    )(mixed, tokens, w_out, vecs)
+
+
+def middle_backward_kernel(
+    part, hidden, cots, w_out, vecs,
+    d_hidden, d_low, d_line, sums,
+    work, core_got, near_got, far_got, total, d_rows,
+    ring_send, ring_recv, send_sem, recv_sem,
+):
+    side, place, half, rank = plane_place()
+    mine = place // 2
+    head = 2 * rank + half
+    here, peers = group_peers()
+
+    def keep(owner, _):
+        work[owner] = part[owner]
+        return 0
+
+    lax.fori_loop(0, 8, keep, 0)
+    greet(peers)
+    plane_scatter(work, core_got, near_got, far_got, total, 256, ring_send, ring_recv)
+    gain = vecs[2:3, :]
+    sums[...] = jnp.zeros_like(sums)
+
+    def one(which, _):
+        rows = span(which, 128)
+        grad = total[rows, :]
+        centered, scale = norm_parts(hidden[which])
+        normed = centered * scale
+        sums[0:1, :] += jnp.sum(grad * normed, axis=0, keepdims=True)
+        lifted = grad * gain
+        back = cots[which].astype(jnp.float32) + scale * (
+            lifted
+            - jnp.mean(lifted, axis=-1, keepdims=True)
+            - normed * jnp.mean(lifted * normed, axis=-1, keepdims=True)
+        )
+        d_hidden[which] = back
+        d_low[which] = to_low(back)
+        d_rows[which] = to_low(dot_nt(to_low(back), w_out[...]))
+        return 0
+
+    lax.fori_loop(0, 2, one, 0)
+
+    def line_copy(slot, sender, seq_from, rank_from, seq_to, rank_to):
+        return pltpu.make_async_remote_copy(
+            src_ref=d_rows.at[seq_to // 2, :, span(2 * rank_to + lax.rem(seq_to, 2), 128)],
+            dst_ref=d_line.at[seq_from, span(rank_from, 128), :],
+            send_sem=send_sem.at[slot],
+            recv_sem=recv_sem.at[sender],
+            device_id={"seq": seq_to, "tensor": rank_to},
+            device_id_type=MESH_ID,
+        )
+
+    for slot, (_, seq_to, rank_to) in enumerate(peers):
+        line_copy(slot, here, place, rank, seq_to, rank_to).start()
+    d_line[place, span(rank, 128), :] = d_rows[mine, :, span(head, 128)]
+    for slot, (other, seq_to, rank_to) in enumerate(peers):
+        line_copy(slot, other, seq_to, rank_to, seq_to, rank_to).wait_recv()
+    for slot, (_, seq_to, rank_to) in enumerate(peers):
+        line_copy(slot, here, place, rank, seq_to, rank_to).wait_send()
+
+
+def middle_backward(part, hidden, cots, w_out, vecs):
+    low, wide = jnp.bfloat16, jnp.float32
+    shapes = (((2, 128, D), wide), ((2, 128, D), low), ((4, BLOCK, 128), low), ((8, D), wide))
+    return pl.pallas_call(
+        middle_backward_kernel,
+        out_shape=[jax.ShapeDtypeStruct(*one) for one in shapes],
+        in_specs=vmem_specs(5),
+        out_specs=vmem_specs(4),
+        scratch_shapes=[
+            pltpu.VMEM((8, 256, D), low),
+            pltpu.VMEM((4, 256, D), low),
+            pltpu.VMEM((4, 128, D), low),
+            pltpu.VMEM((2, 128, D), low),
+            pltpu.VMEM((256, D), wide),
+            pltpu.VMEM((2, 128, D), low),
+            pltpu.SemaphoreType.DMA((10,)),
+            pltpu.SemaphoreType.DMA((10,)),
+            pltpu.SemaphoreType.DMA((15,)),
+            pltpu.SemaphoreType.DMA((16,)),
+        ],
+        compiler_params=pltpu.CompilerParams(
+            collective_id=4, has_side_effects=True, vmem_limit_bytes=VMEM_LIMIT
+        ),
+        cost_estimate=pl.CostEstimate(
+            flops=30000000000, bytes_accessed=30000000, transcendentals=0
+        ),
+        name="middle_backward",
+    )(part, hidden, cots, w_out, vecs)
+
+
 WIDE = 2048
 
 
@@ -997,8 +1327,7 @@
     mine = place // 2
     head_of = lambda weight: lax.dynamic_slice_in_dim(weight, half * 128, 128, 1)
     gate_value = jax.nn.sigmoid(gate_bias)
-    vecs = jnp.stack([state_gain, gate_value] + [jnp.zeros_like(gate_value)] * 6)
-    offsets = lax.rem(jnp.arange(WIDE) + WIDE - BLOCK, WIDE)
+    vecs = jnp.stack([state_gain, gate_value, mlp_gain] + [jnp.zeros_like(gate_value)] * 5)
     offsets = jnp.arange(WIDE) - BLOCK
     offsets = jnp.where(offsets >= WIDE - 2 * BLOCK, offsets - WIDE, offsets)
     bucket_ids = bucket_of(offsets)
@@ -1006,10 +1335,9 @@
     my_bias = jnp.where(half == 0, rel_bias[:, 0], rel_bias[:, 1])
     bias_line = jnp.sum(one_hot * my_bias[None, :], axis=1)
     bias = bias_table(jnp.broadcast_to(bias_line[None, :], (8, WIDE)))
-    segs = lax.all_gather(seg_starts[:, 0], "seq", axis=1, tiled=False)
-    scal = jnp.concatenate(
-        [lax.dynamic_slice_in_dim(lengths, mine, 1, 0), lax.dynamic_slice_in_dim(segs, mine, 1, 0)[0]]
-    )
+    segs = jnp.broadcast_to(jnp.repeat(seg_starts[:, 0], 2)[:, None, None], (4, 1, 128))
+    segs = swap_seq(segs)[:, 0, 0]
+    scal = jnp.concatenate([lax.dynamic_slice_in_dim(lengths, mine, 1, 0), segs])
 
     inputs_wide = inputs.astype(wide)
     tokens_low = gather_rows(to_low(layer_norm(inputs_wide, attn_gain)))
@@ -1022,6 +1350,28 @@
     qkv = swap_seq(qkv_native.reshape(4, BLOCK, 384))
     start_all = lax.all_gather(to_low(init_state), "tensor", axis=0, tiled=True)
     w_sout_all = lax.all_gather(w_sout, "tensor", axis=0, tiled=True)
+    plane = ("dp", "seq")
+    spot = 4 * lax.axis_index("dp") + place
+    ff_own = w_up.shape[1] // 8
+    ff_slices = jnp.concatenate(
+        [
+            lax.dynamic_slice_in_dim(w_up, spot * ff_own, ff_own, 1).T,
+            lax.dynamic_slice_in_dim(w_down, spot * ff_own, ff_own, 0),
+        ],
+        axis=0,
+    )
+    w_back_own = jnp.concatenate(
+        [w.T.reshape(2, 128, D) for w in (w_squery, w_key, w_value)], axis=1
+    )
+    w_sout_all, w_out_own, ff_slices, cot_own, w_back_own = lax.optimization_barrier(
+        (w_sout_all, w_out, ff_slices, out_cot, w_back_own)
+    )
+    w_out_all = lax.all_gather(w_out_own, "tensor", axis=0, tiled=True)
+    ff_all = lax.all_gather(ff_slices, "tensor", axis=0, tiled=True).reshape(4, 2, ff_own, D)
+    up_rows = ff_all[:, 0].reshape(4 * ff_own, D)
+    down_rows = ff_all[:, 1].reshape(4 * ff_own, D)
+    cot_used = lax.all_gather(cot_own.reshape(256, D), plane, axis=0, tiled=True)
+    w_back = lax.all_gather(w_back_own, "tensor", axis=0, tiled=True)
     w_state = jnp.concatenate([head_of(w_squery), head_of(w_key), head_of(w_value)], axis=1)
     mixed, lse_tok, state_rows, state_low, qkvst, lse_st, os_rows = forward_chain(
         scal, qkv, start_all, w_state, w_sout_all, vecs, bias
@@ -1034,39 +1384,37 @@
         mine == 0, jnp.stack([kept, came.astype(wide)]), jnp.stack([came.astype(wide), kept])
     )
 
-    mixed_native = swap_seq(mixed).reshape(2, 2, BLOCK, 128)
-    w_out_heads = w_out.reshape(2, 128, D)
-    hidden_in = inputs_wide + sum_rows(
-        jnp.einsum("shqe,hed->sqd", mixed_native, w_out_heads, preferred_element_type=wide)
-    )
-    mid_low = gather_rows(to_low(layer_norm(hidden_in, mlp_gain)))
-    pre_act = matmul(mid_low, w_up)
+    hidden_in, mixed_rows, mid_all = middle_forward(mixed, inputs, w_out_all, vecs)
+    mid_low = mid_all.reshape(2048, D)
+    pre_act = matmul_t(mid_low, up_rows)
     hidden_low = to_low(jax.nn.gelu(pre_act))
-    mlp_rows = sum_rows(matmul(hidden_low, w_down))
-    tokens_out = (hidden_in + mlp_rows).astype(low)
-    cot_wide = out_cot.astype(wide)
-    cot_used = gather_rows(out_cot)
-    grad_hidden_act = matmul_t(cot_used, w_down)
-    down_grad = outer_sum(hidden_low, cot_used)
+    mlp_part = to_low(matmul(hidden_low, down_rows))
+    grad_hidden_act = matmul_t(cot_used, down_rows)
     grad_pre = to_low(gelu_back(pre_act, grad_hidden_act))
-    up_grad = outer_sum(mid_low, grad_pre)
-    grad_normed_mid = sum_rows(matmul_t(grad_pre, w_up))
-    grad_mid_in, mlp_gain_grad = norm_back(hidden_in, mlp_gain, grad_normed_mid)
-    grad_hidden = cot_wide + grad_mid_in
-    grad_attn_low = gather_rows(to_low(grad_hidden))
-    d_mixed_native = to_low(
-        jnp.einsum("sqd,hed->shqe", grad_attn_low, w_out_heads, preferred_element_type=wide)
-    )
-    out_grad = jnp.einsum(
-        "shqe,sqd->hed", mixed_native, grad_attn_low, preferred_element_type=wide
-    ).reshape(256, D)
-    d_mixed = swap_seq(d_mixed_native.reshape(4, BLOCK, 128))
+    d_mid_part = to_low(matmul(grad_pre, up_rows))
+    grad_hidden, grad_low, d_mixed, mlp_sums = middle_backward(
+        d_mid_part.reshape(8, 256, D), hidden_in, out_cot, w_out_all, vecs
+    )
+    mlp_rows = lax.psum_scatter(mlp_part, plane, scatter_dimension=0, tiled=True)
+    tokens_out = (hidden_in + mlp_rows.reshape(2, 128, D).astype(wide)).astype(low)
+    ff_grads = jnp.stack(
+        [
+            outer_sum(grad_pre, mid_low).astype(low).reshape(4, ff_own, D),
+            outer_sum(hidden_low, cot_used).astype(low).reshape(4, ff_own, D),
+        ],
+        axis=1,
+    )
+    ff_sum = lax.psum_scatter(
+        ff_grads.reshape(8 * ff_own, D), "tensor", scatter_dimension=0, tiled=True
+    )
+    ff_total = lax.all_gather(ff_sum, plane, axis=0, tiled=True).reshape(8, 2, ff_own, D)
+    up_grad = ff_total[:, 0].reshape(8 * ff_own, D).T.astype(wide)
+    down_grad = ff_total[:, 1].reshape(8 * ff_own, D).astype(wide)
+    out_part = lax.psum_scatter(
+        outer_sum(mixed_rows, grad_low).astype(low), "tensor", scatter_dimension=0, tiled=True
+    )
 
     cots = swap_seq(state_cot.reshape(4, 64, D))
-    w_back_own = jnp.concatenate(
-        [w.T.reshape(2, 128, D) for w in (w_squery, w_key, w_value)], axis=1
-    )
-    w_back = lax.all_gather(w_back_own, "tensor", axis=0, tiled=True)
     start_half = lax.dynamic_slice_in_dim(to_low(init_state).astype(wide), half * 64, 64, 0)
     states = jnp.concatenate(
         [start_half[None], lax.dynamic_slice_in_dim(state_rows, half * 64, 64, 1)], axis=0
@@ -1094,7 +1442,7 @@
         outer_sum(os_rows, du_rows).astype(low), "tensor", scatter_dimension=0, tiled=True
     )
     state_part = own_half(d_start, half, 0)
-    gains = lax.psum(jnp.stack([attn_gain_grad, sums[1], mlp_gain_grad, sums[0]]), "tensor")
+    gains = lax.psum(jnp.stack([attn_gain_grad, sums[1], mlp_sums[0], sums[0]]), "tensor")
 
     def total(part):
         return lax.psum(part.astype(low), ("dp", "seq")).astype(wide)
@@ -1111,11 +1459,11 @@
         total(query_grad),
         total(key_grad),
         total(value_grad),
-        total(out_grad),
+        total(out_part),
         total(squery_grad),
         total(sout_part),
-        total(up_grad),
-        total(down_grad),
+        up_grad,
+        down_grad,
         total(bias_grad),
         gain_total[3],
     )

time: 986 us -> 892 us (0.905)
  waiting for transfers between devices: 530 us -> 310 us
  Pallas kernels: 192 us -> 363 us
  blocking collectives: 87.6 us -> 54 us
    all_gather x4 -> x1, waiting for transfers between devices: 160 us -> 39.6 us  [gather_rows(): return lax.all_gather(values, 'tensor', axis=1, tiled=True)]
    pallas_call x0 -> x2, Pallas kernels: none -> 119 us  [the longest x1 60.5 us: middle_forward(): pl.pallas_call(middle_forward_kernel, out_shape=[jax.ShapeDtypeStruct(*on...]
    psum x1, waiting for transfers between devices: 123 us -> 43 us  [total(): return lax.psum(part.astype(low), ('dp', 'seq')).astype(wide)]
    all_gather x1, waiting for transfers between devices: 105 us -> 41.5 us  [line_body(): w_back = lax.all_gather(w_back_own, 'tensor', axis=0, tiled=True)]
    reduce_scatter x0 -> x3, waiting for transfers between devices: none -> 62.3 us  [the longest x1 33.5 us: line_body(): lax.psum_scatter(mlp_part, plane, scatter_dimension=0, tiled=True)]
    reduce_scatter x4 -> x1, waiting for transfers between devices: 104 us -> 44.6 us  [sum_rows(): lax.psum_scatter(terms.astype(jnp.bfloat16), 'tensor', scatter_dimension=...]
    pallas_call x1, Pallas kernels: 86.2 us -> 122 us  [forward_chain(): pl.pallas_call(forward_kernel, out_shape=[jax.ShapeDtypeStruct(*one) for...]
    all_gather x0 -> x4, waiting for transfers between devices: none -> 28.4 us  [the longest x1 28.3 us: line_body(): lax.all_gather(ff_sum, plane, axis=0, tiled=True).reshape(8, 2, ff_own, D)]
  transfers between devices with their start and end apart: 17 -> 18, of which waited for: 12 -> 10; matrix products, arithmetic and copies ran while one was open for 9% -> 13% of each run, Pallas kernels for 2% -> 41%
where the time goes in v2:
time: 892 us; the launch traced here: 885 us
  Pallas kernels  363 us (41%)
  waiting for transfers between devices  310 us (35%)
  blocking collectives  54 us (6%)
  matrix products  50.8 us (6%)
  other arithmetic  44.8 us (5%)
  local copies, waits for them, and re-layouts  33.6 us (4%)
  between operations  14.9 us (2%)
  starting transfers between devices  13.8 us (2%)
    pallas_call x1, Pallas kernels, forward_chain(): pl.pallas_call(forward_kernel, out_shape=[jax.ShapeDtypeStruct(*one) for...  122 us
    pallas_call x1, Pallas kernels, backward_chain(): pl.pallas_call(backward_kernel, out_shape=[jax.ShapeDtypeStruct(*one) for...  106 us
    pallas_call x1, Pallas kernels, middle_forward(): pl.pallas_call(middle_forward_kernel, out_shape=[jax.ShapeDtypeStruct(*on...  60.5 us
    pallas_call x1, Pallas kernels, middle_backward(): pl.pallas_call(middle_backward_kernel, out_shape=[jax.ShapeDtypeStruct(*o...  58.1 us
    reduce_scatter x1, waiting for transfers between devices, sum_rows(): lax.psum_scatter(terms.astype(jnp.bfloat16), 'tensor', scatter_dimension=...  44.6 us
    psum x1, waiting for transfers between devices, total(): return lax.psum(part.astype(low), ('dp', 'seq')).astype(wide)  43 us
    all_gather x1, waiting for transfers between devices, line_body(): w_back = lax.all_gather(w_back_own, 'tensor', axis=0, tiled=True)  41.5 us
    all_gather x1, waiting for transfers between devices, gather_rows(): return lax.all_gather(values, 'tensor', axis=1, tiled=True)  39.6 us
  transfers between devices with their start and end apart: 18, of which 10 were waited for; matrix products, arithmetic and copies ran while one was open for 13% of the time, Pallas kernels for 41%

profile of v2, /device:TPU:0, one launch (start us, length us, event | category | flops | bytes accessed | tf_op | source)
XLA Modules:
  0.0 885.2 jit_solution(3126657390684483973)
XLA Ops:
  8.0 1.3 convert_reduce_fusion
  9.3 1.3 fusion.27
  11.8 2.1 fusion.26
  14.0 1.8 convert_element_type.199
  16.6 1.2 copy.111
  19.7 1.3 pad_maximum_fusion.2
  21.0 37.3 %all-gather.13.cloned.1.call-done.w_sout = bf16[1024,1024]{1,0:T(8,128)(2,1)} async-done(((bf16[256,1024]{1,0:T(8,128)(2,1)}), bf16[1024,1024]{1,0:T(8,128)(2,1)}) %all-gather.13.cloned.1.call-update) | async-done | bytes 2097168 | tf_op jit(solution)/shard_map/all_gather | solution.py:1352
  60.3 3.2 all-to-all-start
  64.2 1.3 pad_maximum_fusion.1
  65.5 39.6 %all-gather.9.cloned.1.call-done = bf16[2,512,1024]{2,1,0:T(8,128)(2,1)} async-done(((bf16[2,128,1024]{2,1,0:T(8,128)(2,1)}), bf16[2,512,1024]{2,1,0:T(8,128)(2,1)}) %all-gather.9.cloned.1.call-update) | async-done | bytes 2097168 | tf_op jit(solution)/shard_map/all_gather | solution.py:91
  105.1 3.9 fusion.17
  109.0 1.6 copy.109
  110.6 3.7 all-to-all-start.1
  115.3 8.1 bias_table.1.bias
  126.8 1.2 pad_add_fusion.scal
  128.1 6.3 all-to-all-done.1.qkv
  134.4 4.2 all-to-all-start.2
  138.8 121.6 %forward_chain.1 = (bf16[4,512,128]{2,1,0:T(8,128)(2,1)}, f32[4,512,1]{2,1,0:T(8,128)}, f32[4,128,1024]{2,1,0:T(8,128)}, bf16[4,512,1024]{2,1,0:T(8,128)(2,1)}, ...) custom-call(s32[5]{0:T(128)} %pad_add_fusion.scal, ...), custom_call_target="tpu_custom_call" | custom-call | flops 20000000000 | bytes 20000000 | tf_op jit(solution)/shard_map/forward_chain/pallas_call | solution.py:692
  260.4 1.3 constant_dynamic-slice_fusion
  261.8 2.8 fusion.49
  264.5 60.5 %middle_forward.1 = (f32[2,128,1024]{2,1,0:T(8,128)}, bf16[2,128,1024]{2,1,0:T(8,128)(2,1)}, bf16[8,256,1024]{2,1,0:T(8,128)(2,1)}) custom-call(bf16[4,512,128]{2,1,0:T(8,128)(2,1)} %get-tuple-element.43.mixed, bf16[2,128,1024]{2,1,0:T(8,128)(2,1)} %tokens.1, bf16[1024,1024]{1,0:T(8,128)(2,1)} %all-gather.15.cloned.1.call-done.w_out, f32[8,1024]{1,0:T(8,128)} %stack.46.vecs), custom_call_target="tpu_custom_call" | custom-call | flops 30000001024 | bytes 30000000 | tf_op jit(solution)/shard_map/middle_forward/pallas_call | solution.py:1124
  325.1 5.3 fusion.53
  330.4 6.1 fusion.6
  336.5 4.4 convolution_convert_fusion
  340.9 58.1 %middle_backward.1 = (f32[2,128,1024]{2,1,0:T(8,128)}, bf16[2,128,1024]{2,1,0:T(8,128)(2,1)}, bf16[4,512,128]{2,1,0:T(8,128)(2,1)}, f32[8,1024]{1,0:T(8,128)}) custom-call(bf16[8,256,1024]{2,1,0:T(8,128)(2,1)} %bitcast.159, f32[2,128,1024]{2,1,0:T(8,128)} %get-tuple-element.45.hidden, bf16[2,128,1024]{2,1,0:T(8,128)(2,1)} %cots.1, ...), custom_call_target="tpu_custom_call" | custom-call | flops 30000001024 | bytes 30000000 | tf_op jit(solution)/shard_map/middle_backward/pallas_call | solution.py:1207
  399.0 3.2 bitcast_convert_fusion.1
  402.3 1.2 pad_maximum_fusion.3.states
  403.5 41.5 %all-gather.21.cloned.1.call-done.w_back = bf16[8,384,1024]{2,1,0:T(8,128)(2,1)} async-done(((bf16[2,384,1024]{2,1,0:T(8,128)(2,1)}), bf16[8,384,1024]{2,1,0:T(8,128)(2,1)}) %all-gather.21.cloned.1.call-update) | async-done | bytes 6291472 | tf_op jit(solution)/shard_map/all_gather | solution.py:1374
  445.0 106.2 %backward_chain.1 = (bf16[4,512,384]{2,1,0:T(8,128)(2,1)}, bf16[4,512,384]{2,1,0:T(8,128)(2,1)}, bf16[4,64,1024]{2,1,0:T(8,128)(2,1)}, f32[64,1024]{1,0:T(8,128)...) custom-call(s32[5]{0:T(128)} %pad_add_fusion.scal, bf16[4,512,384]{2,1,0:T(8,128)(2,1)} %copy-done.8, ...), custom_call_target="tpu_custom_call" | custom-call | flops 40000000000 | bytes 40000000 | tf_op jit(solution)/shard_map/backward_chain/pallas_call | solution.py:879
  551.3 3.1 bitcast_convert_fusion
  554.4 5.3 convolution_convert_fusion.3
  559.8 2.5 convolution_convert_fusion.2
  562.3 1.5 pad_maximum_fusion
  564.3 7.0 convolution_convert_fusion.1
  571.3 23.9 %all_to_all.20 = bf16[4,512,384]{2,1,0:T(8,128)(2,1)S(1)} all-to-all(bf16[4,512,384]{2,1,0:T(8,128)(2,1)} %get-tuple-element.56), channel_id=1, replica_groups=mesh['dp'=2,'seq'=4,'tensor'=4] {'seq'}, dimensions={0} | all-to-all | bytes 3145728 | tf_op jit(solution)/shard_map/all_to_all | solution.py:1300
  595.3 1.2 copy-done.9
  596.4 3.1 bitcast_convert_fusion.2
  599.6 5.1 convolution_bitcast_fusion
  607.5 1.9 fusion.11
  611.1 2.1 copy.116
  613.2 2.2 add_convert_fusion
  616.4 28.8 %reduce-scatter.14.cloned.1.call-done = bf16[256,1024]{1,0:T(8,128)(2,1)} async-done(((bf16[1024,1024]{1,0:T(8,128)(2,1)}), bf16[256,1024]{1,0:T(8,128)(2,1)}) %reduce-scatter.14.cloned.1.call-update) | async-done | bytes 524304 | tf_op jit(solution)/shard_map/reduce_scatter | solution.py:1407
  646.3 1.5 collective-permute-start
  648.9 5.3 collective-permute-done
  654.3 1.1 maximum_select_fusion
  656.2 8.6 diagonal_sums.1
  666.7 33.5 %reduce-scatter.6.cloned.1.call-done = bf16[256,1024]{1,0:T(8,128)(2,1)} async-done(((bf16[2048,1024]{1,0:T(8,128)(2,1)}), bf16[256,1024]{1,0:T(8,128)(2,1)}) %reduce-scatter.6.cloned.1.call-update) | async-done | bytes 524304 | tf_op jit(solution)/shard_map/reduce_scatter | solution.py:1398
  700.1 2.0 fusion.32
  702.1 44.6 %reduce-scatter.8.cloned.1.call-done = bf16[2,128,1024]{2,1,0:T(8,128)(2,1)} async-done(((bf16[2,512,1024]{2,1,0:T(8,128)(2,1)}), bf16[2,128,1024]{2,1,0:T(8,128)(2,1)}) %reduce-scatter.8.cloned.1.call-update) | async-done | bytes 524304 | tf_op jit(solution)/shard_map/reduce_scatter | solution.py:95
  746.7 1.4 fusion.28
  748.1 1.7 fusion.29
  749.8 16.9 %psum.71 = bf16[4,1024]{1,0:T(4,128)(2,1)S(1)} all-reduce(f32[4,1024]{1,0:T(4,128)S(1)} %pad_maximum_fusion.6), channel_id=1, replica_groups=mesh['dp'=2,'seq'=4,'tensor'=4] {'tensor'}, use_global_device_ids=true, to_apply=%region_9.10 | all-reduce | flops 4096 | bytes 24576 | tf_op jit(solution)/shard_map/psum | solution.py:1445
  766.7 13.2 %all-reduce.9 = (bf16[4,1024]{1,0:T(4,128)(2,1)S(1)}, bf16[32,2]{0,1:T(2,128)(2,1)S(1)}) all-reduce(bf16[4,1024]{1,0:T(4,128)(2,1)S(1)} %psum.71, bf16[32,2]{0,1:T(2,128)(2,1)S(1)} %select_convert_fusion.1), channel_id=1, replica_groups=mesh['dp'=2,'seq'=4,'tensor'=4] {'dp','seq'}, use_global_device_ids=true, to_apply=%region_10.11 | all-reduce | flops 4160 | bytes 16640 | tf_op jit(solution)/shard_map/psum | solution.py:1448
  781.1 2.4 add_add_fusion.1
  783.5 43.0 %all-reduce.13.cloned.1.call-done = (bf16[128,1024]{1,0:T(8,128)(2,1)}, bf16[1024,256]{1,0:T(8,128)(2,1)}, bf16[1024,256]{1,0:T(8,128)(2,1)}, bf16[1024,256]{1,0...) async-done(((bf16[128,1024]{1,0:T(8,128)(2,1)}, bf16[1024,256]{1,0:T(8,128)(2,1)}, bf16[1024,256]{1,0:T(8,128)(2,1)}, ...) | async-done | bytes 3407888 | tf_op jit(solution)/shard_map/psum | solution.py:1448
  826.5 1.9 convert_element_type.220
  828.4 2.1 convert_element_type.224
  830.5 2.1 convert_element_type.226
  833.7 1.1 convert_element_type.230
  836.9 28.3 %all-gather.23.cloned.1.call-done = bf16[2048,1024]{1,0:T(8,128)(2,1)} async-done(((bf16[256,1024]{1,0:T(8,128)(2,1)}), bf16[2048,1024]{1,0:T(8,128)(2,1)}) %all-gather.23.cloned.1.call-update) | async-done | bytes 4194320 | tf_op jit(solution)/shard_map/all_gather | solution.py:1410
  865.2 2.7 fusion.47
  867.9 2.6 bitcast_convert_fusion.3
  870.5 2.6 bitcast_convert_fusion.4
  873.1 5.3 copy.123
  (174 shorter events, 27.1 us)
Async XLA Ops:
  7.2 8.7 copy-start
  7.2 8.9 %copy-start.3 = (bf16[1024,256]{1,0:T(8,128)(2,1)S(1)}, bf16[1024,256]{1,0:T(8,128)(2,1)}, u32[]{:S(2)}) copy-start(bf16[1024,256]{1,0:T(8,128)(2,1)} %param.28) | copy-start | bytes 1572868
  7.2 9.1 %copy-start.4 = (bf16[1024,256]{1,0:T(8,128)(2,1)S(1)}, bf16[1024,256]{1,0:T(8,128)(2,1)}, u32[]{:S(2)}) copy-start(bf16[1024,256]{1,0:T(8,128)(2,1)} %param.27) | copy-start | bytes 1572868
  7.2 51.1 %all-gather.13.cloned.1.call-start = ((), (), s32[]{:S(2)}) async-start(), calls=%async_computation.11 | async-start | bytes 2621440 | tf_op jit(solution)/shard_map/all_gather | solution.py:1352
  8.0 97.2 %all-gather.9.cloned.1.call-start = ((), (), s32[]{:S(2)}) async-start(), calls=%async_computation.9 | async-start | bytes 2621440 | tf_op jit(solution)/shard_map/all_gather | solution.py:91
  9.3 1.9 copy-start.24
  10.7 0.6 copy-start.28
  11.2 0.6 copy-start.26
  14.0 124.8 %all-gather.11.cloned.1.call-start = ((), (), s32[]{:S(2)}) async-start(), calls=%async_computation.10 | async-start | bytes 1310720 | tf_op jit(solution)/shard_map/all_gather | solution.py:1351
  15.8 245.9 %all-gather.17.cloned.1.call-start = ((), (), s32[]{:S(2)}) async-start(), calls=%async_computation.13 | async-start | bytes 2621440 | tf_op jit(solution)/shard_map/all_gather | solution.py:1370
  17.8 41.7 %copy-start.37 = (s32[2,1]{0,1:T(1,128)S(1)}, s32[2,1]{0,1:T(1,128)}, u32[]{:S(2)}) copy-start(s32[2,1]{0,1:T(1,128)} %param.20) | copy-start | bytes 28
  19.7 44.3 %copy-start.18 = (bf16[1024,256]{1,0:T(8,128)(2,1)S(1)}, bf16[1024,256]{1,0:T(8,128)(2,1)}, u32[]{:S(2)}) copy-start(bf16[1024,256]{1,0:T(8,128)(2,1)} %param.26) | copy-start | bytes 1572868
  58.3 206.2 %all-gather.15.cloned.1.call-start = ((), (), s32[]{:S(2)}) async-start(), calls=%async_computation.12 | async-start | bytes 2621440 | tf_op jit(solution)/shard_map/all_gather | solution.py:1369
  58.9 266.2 %all-gather.19.cloned.1.call-start = ((), (), s32[]{:S(2)}) async-start(), calls=%async_computation.15 | async-start | bytes 4718592 | tf_op jit(solution)/shard_map/all_gather | solution.py:1373
  60.3 50.3 %all-to-all-start = ((s32[4,1,128]{2,1,0:T(1,128)}), s32[4,1,128]{2,1,0:T(1,128)S(1)}, u32[]{:S(2)}, u32[]{:S(2)}) async-start(s32[4,1,128]{2,1,0:T(1,128)} %broadcast_in_dim.18), calls=%async_computation | async-start | bytes 4096 | tf_op jit(solution)/shard_map/all_to_all | solution.py:1300
  109.0 5.4 copy-start.33
  110.6 12.7 %copy-start.38 = (s32[2]{0:T(128)S(1)}, s32[2]{0:T(128)}, u32[]{:S(2)}) copy-start(s32[2]{0:T(128)} %param.21) | copy-start | bytes 28
  110.6 13.3 %copy-start.32 = (f32[1024]{0:T(1024)S(1)}, f32[1024]{0:T(1024)}, u32[]{:S(2)}) copy-start(f32[1024]{0:T(1024)} %param.35) | copy-start | bytes 12292
  110.6 13.3 %copy-start.30 = (f32[1024]{0:T(1024)S(1)}, f32[1024]{0:T(1024)}, u32[]{:S(2)}) copy-start(f32[1024]{0:T(1024)} %param.24) | copy-start | bytes 12292
  110.6 13.3 %copy-start.31 = (f32[1024]{0:T(1024)S(1)}, f32[1024]{0:T(1024)}, u32[]{:S(2)}) copy-start(f32[1024]{0:T(1024)} %param.25) | copy-start | bytes 12292
  110.6 14.0 %copy-start.6 = (bf16[128,1024]{1,0:T(8,128)(2,1)S(1)}, bf16[128,1024]{1,0:T(8,128)(2,1)}, u32[]{:S(2)}) copy-start(bf16[128,1024]{1,0:T(8,128)(2,1)} %convert_element_type.199) | copy-start | bytes 786436
  110.6 23.8 %all-to-all-start.1 = ((bf16[4,512,384]{2,1,0:T(8,128)(2,1)}), bf16[4,512,384]{2,1,0:T(8,128)(2,1)S(1)}, u32[]{:S(2)}, u32[]{:S(2)}) async-start(bf16[4,512,384]{2,1,0:T(8,128)(2,1)} %bitcast.9), calls=%async_computation.1 | async-start | bytes 3145728 | tf_op jit(solution)/shard_map/all_to_all | solution.py:1300
  114.4 330.7 %all-gather.21.cloned.1.call-start = ((), (), s32[]{:S(2)}) async-start(), calls=%async_computation.16 | async-start | bytes 7864320 | tf_op jit(solution)/shard_map/all_gather | solution.py:1374
  114.5 9.4 %copy-start.21 = (s32[2048]{0:T(1024)}, s32[2048]{0:T(1024)S(1)}, u32[]{:S(2)}) copy-start(s32[2048]{0:T(1024)S(1)} %fusion.44) | copy-start | bytes 24580
  134.4 4.4 copy-start.8
  134.4 269.1 %all-to-all-start.2 = ((bf16[4,64,1024]{2,1,0:T(8,128)(2,1)}), bf16[4,64,1024]{2,1,0:T(8,128)(2,1)}, u32[]{:S(2)}, u32[]{:S(2)}) async-start(bf16[4,64,1024]{2,1,0:T(8,128)(2,1)} %bitcast.144), calls=%async_computation.3 | async-start | bytes 1048576 | tf_op jit(solution)/shard_map/all_to_all | solution.py:1300
  138.6 477.7 %reduce-scatter.10.cloned.1.call-start = ((), (), s32[]{:S(2)}) async-start(), calls=%async_computation.18 | async-start | bytes 2621440 | tf_op jit(solution)/shard_map/reduce_scatter | solution.py:1413
  325.1 5.3 copy-start.13
  325.1 5.3 copy-start.39
  336.5 4.4 copy-start.40
  340.9 58.1 %copy-start.19 = (bf16[2,128,1024]{2,1,0:T(8,128)(2,1)S(1)}, bf16[2,128,1024]{2,1,0:T(8,128)(2,1)}, u32[]{:S(2)}) copy-start(bf16[2,128,1024]{2,1,0:T(8,128)(2,1)} %get-tuple-element.62) | copy-start | bytes 1572868
  402.2 214.0 %reduce-scatter.12.cloned.1.call-start = ((), (), s32[]{:S(2)}) async-start(), calls=%async_computation.19 | async-start | bytes 2621440 | tf_op jit(solution)/shard_map/reduce_scatter | solution.py:1441
  445.0 106.2 %copy-start.41 = (bf16[4,64,1024]{2,1,0:T(8,128)(2,1)S(1)}, bf16[4,64,1024]{2,1,0:T(8,128)(2,1)}, u32[]{:S(2)}) copy-start(bf16[4,64,1024]{2,1,0:T(8,128)(2,1)} %get-tuple-element.64) | copy-start | bytes 1572868
  554.4 90.8 %reduce-scatter.14.cloned.1.call-start = ((), (), s32[]{:S(2)}) async-start(), calls=%async_computation.20 | async-start | bytes 2621440 | tf_op jit(solution)/shard_map/reduce_scatter | solution.py:1407
  554.4 5.3 copy-start.35
  554.4 5.3 copy-start.42
  563.8 136.3 %reduce-scatter.6.cloned.1.call-start = ((), (), s32[]{:S(2)}) async-start(), calls=%async_computation.14 | async-start | bytes 4718592 | tf_op jit(solution)/shard_map/reduce_scatter | solution.py:1398
  571.3 25.2 %copy-start.7 = (bf16[1024,2,3,128]{0,3,2,1:T(8,128)(2,1)S(1)}, bf16[1024,2,3,128]{0,3,2,1:T(8,128)(2,1)}, u32[]{:S(2)}) copy-start(bf16[1024,2,3,128]{0,3,2,1:T(8,128)(2,1)} %pad_maximum_fusion.1) | copy-start | bytes 4718596
  571.3 175.5 %reduce-scatter.8.cloned.1.call-start = ((), (), s32[]{:S(2)}) async-start(), calls=%async_computation.17 | async-start | bytes 2621440 | tf_op jit(solution)/shard_map/reduce_scatter | solution.py:95
  595.3 1.2 copy-start.9
  599.6 226.9 %all-reduce.13.cloned.1.call-start = ((), (), s32[]{:S(2)}) async-start(), calls=%async_computation.22 | async-start | bytes 6815744 | tf_op jit(solution)/shard_map/psum | solution.py:1448
  599.6 5.2 copy-start.20
  604.7 1.9 copy-start.34
  604.7 2.8 copy-start.10
  604.7 2.8 copy-start.36
  611.1 4.3 copy-start.5
  616.3 248.9 %all-gather.23.cloned.1.call-start = ((), (), s32[]{:S(2)}) async-start(), calls=%async_computation.21 | async-start | bytes 4718592 | tf_op jit(solution)/shard_map/all_gather | solution.py:1410
  646.3 19.4 %copy-start.22 = (s32[2048]{0:T(1024)S(1)}, s32[2048]{0:T(1024)}, u32[]{:S(2)}) copy-start(s32[2048]{0:T(1024)} %copy-done.21) | copy-start | bytes 24580
  646.3 53.8 %copy-start.12 = (f32[2,128,1024]{2,1,0:T(8,128)S(1)}, f32[2,128,1024]{2,1,0:T(8,128)}, u32[]{:S(2)}) copy-start(f32[2,128,1024]{2,1,0:T(8,128)} %get-tuple-element.45.hidden) | copy-start | bytes 3145732
  646.3 7.9 collective-permute-start
  654.3 92.4 %copy-start.2 = (bf16[2,128,1024]{2,1,0:T(8,128)(2,1)S(1)}, bf16[2,128,1024]{2,1,0:T(8,128)(2,1)}, u32[]{:S(2)}) copy-start(bf16[2,128,1024]{2,1,0:T(8,128)(2,1)} %tokens.1) | copy-start | bytes 1572868
  654.3 92.4 %copy-start.23 = (f32[1024]{0:T(1024)S(1)}, f32[1024]{0:T(1024)}, u32[]{:S(2)}) copy-start(f32[1024]{0:T(1024)} %param.23) | copy-start | bytes 12292
  654.3 92.4 %copy-start.25 = (f32[2,128]{1,0:T(2,128)S(1)}, f32[2,128]{1,0:T(2,128)}, u32[]{:S(2)}) copy-start(f32[2,128]{1,0:T(2,128)} %copy-done.24) | copy-start | bytes 3076
  655.4 92.7 %copy-start.29 = (f32[2,128]{1,0:T(2,128)S(1)}, f32[2,128]{1,0:T(2,128)}, u32[]{:S(2)}) copy-start(f32[2,128]{1,0:T(2,128)} %copy-done.28) | copy-start | bytes 3076
  655.4 92.7 %copy-start.27 = (f32[2,128]{1,0:T(2,128)S(1)}, f32[2,128]{1,0:T(2,128)}, u32[]{:S(2)}) copy-start(f32[2,128]{1,0:T(2,128)} %copy-done.26) | copy-start | bytes 3076
  656.2 124.9 %copy-start.11 = (f32[2,128,1024]{2,1,0:T(8,128)S(1)}, f32[2,128,1024]{2,1,0:T(8,128)}, u32[]{:S(2)}) copy-start(f32[2,128,1024]{2,1,0:T(8,128)} %get-tuple-element.50) | copy-start | bytes 3145732
  826.5 6.2 copy-start.17
  826.5 7.2 copy-start.16
  828.3 6.4 copy-start.15
  830.5 5.3 copy-start.14
  870.5 7.9 copy-start.1
Sparse Core Ops, SparseCore 0:
  9.6 48.6 all-gather.12
  60.4 44.6 all-gather.8
  107.3 26.6 all-gather.10
  136.0 67.7 all-gather.16
  205.2 59.1 all-gather.14
  266.1 50.4 all-gather.18
  318.1 126.8 all-gather.20
  447.3 53.3 reduce-scatter.9
  554.5 45.2 reduce-scatter.11
  601.9 43.1 reduce-scatter.13
  649.5 50.6 reduce-scatter.5
  702.8 43.8 reduce-scatter.7
  752.6 73.7 all-reduce.12
  828.4 36.8 all-gather.22

commit v3 on v2

--- a/solution.py
+++ b/solution.py
@@ -950,20 +950,24 @@
     send(me, 0, to_y)
     send(me, 0, to_c)
     send(me, 1, to_c)
+    yield
     arrived(at_x, 0)
     send(at_x, 0, to_y)
     arrived(at_y, 1)
     send(at_y, 1, to_x)
     send(at_x, 0, to_c)
     send(at_y, 1, to_c)
+    yield
     arrived(at_x, 1)
     send(at_x, 1, to_c)
     arrived(at_y, 0)
     send(at_y, 0, to_c)
+    yield
     arrived(at_d, 0)
     send(at_d, 0, to_c)
     arrived(at_d, 1)
     send(at_d, 1, to_c)
+    yield
     for owner in (
         plane_index(side, core),
         plane_index(across, core),
@@ -974,6 +978,16 @@
         arrived(owner, 1)
     for one in sent:
         one.wait_send()
+
+
+def run_all(*steps):
+    waiting = list(steps)
+    while waiting:
+        for one in list(waiting):
+            try:
+                next(one)
+            except StopIteration:
+                waiting.remove(one)
 
 
 def plane_scatter(part, core_got, near_got, far_got, total, rows, send_sem, recv_sem):
@@ -1032,6 +1046,7 @@
             near[2].start()
         if slot == 2:
             near[3].start()
+    yield
     near[0].wait_recv()
     add_into(at_y, halves[0], near_got[0])
     far = [
@@ -1042,10 +1057,12 @@
     near[1].wait_recv()
     add_into(at_x, halves[1], near_got[1])
     far[1].start()
+    yield
     near[2].wait_recv()
     add_into(me, halves[0], near_got[2])
     near[3].wait_recv()
     add_into(me, halves[1], near_got[3])
+    yield
     for slot, view in enumerate(halves):
         far[slot].wait_recv()
         total[view, :] = part[me, view, :].astype(jnp.float32) + far_got[slot].astype(jnp.float32)
@@ -1113,7 +1130,7 @@
         return 0
 
     lax.fori_loop(0, 2, one, 0)
-    plane_gather(mid_all, 256, ring_send, ring_recv)
+    run_all(plane_gather(mid_all, 256, ring_send, ring_recv))
     for slot, (_, seq_to, rank_to) in enumerate(peers):
         rows_copy(slot, here, place, rank, seq_to, rank_to).wait_send()
 
@@ -1159,7 +1176,7 @@
 
     lax.fori_loop(0, 8, keep, 0)
     greet(peers)
-    plane_scatter(work, core_got, near_got, far_got, total, 256, ring_send, ring_recv)
+    run_all(plane_scatter(work, core_got, near_got, far_got, total, 256, ring_send, ring_recv))
     gain = vecs[2:3, :]
     sums[...] = jnp.zeros_like(sums)
 
@@ -1234,65 +1251,638 @@
 WIDE = 2048
 
 
-def bias_kernel(line, table):
-    first = line[...]
-    row = lax.broadcasted_iota(jnp.int32, (8, WIDE), 0)
-    for step in (1, 2, 4):
-        first = jnp.where(row // step % 2 == 1, pltpu.roll(first, step, 1), first)
-
-    def one(group, _):
-        table[span(group, 8), :] = pltpu.roll(first, 8 * group, 1)[:, 0 : 2 * BLOCK]
-        return 0
-
-    lax.fori_loop(0, BLOCK // 8, one, 0)
-
-
-def bias_table(line):
+def opening_kernel(
+    tokens, w_qkv, piece, vecs, line,
+    rows_all, qkv, kept, table,
+    stage, send_sem, core_sem, recv_sem, piece_send, piece_recv, ring_send, ring_recv,
+):
+    side, place, half, rank = plane_place()
+    mine = place // 2
+    core = place + 1 - 2 * half
+    other = lax.rem(place + 2, 4)
+    me = plane_index(side, place)
+    extra = piece.shape[0]
+    barrier = pltpu.get_barrier_semaphore()
+    greeted = [{"tensor": lax.rem(rank + step, 4)} for step in (1, 2, 3)]
+    greeted += [{"seq": core}, {"seq": other}, {"dp": 1 - side}]
+    for target in greeted:
+        pl.semaphore_signal(barrier, inc=1, device_id=target, device_id_type=MESH_ID)
+    gain = vecs[3:4, :]
+
+    def normed(which):
+        centered, scale = norm_parts(tokens[which].astype(jnp.float32))
+        return to_low(centered * scale * gain)
+
+    def moved(block_id, origin, sem, target):
+        view = rows_all.at[block_id, span(origin, 128), :]
+        return pltpu.make_async_remote_copy(
+            src_ref=view,
+            dst_ref=view,
+            send_sem=sem,
+            recv_sem=recv_sem.at[block_id, origin],
+            device_id=target,
+            device_id_type=MESH_ID,
+        )
+
+    stage[...] = normed(1 - mine)
+    kept[me, span(rank, extra), :] = piece[...]
+    pl.semaphore_wait(barrier, 6)
+    aside = pltpu.make_async_remote_copy(
+        src_ref=stage,
+        dst_ref=rows_all.at[place, span(rank, 128), :],
+        send_sem=send_sem.at[0, 0, 3],
+        recv_sem=recv_sem.at[place, rank],
+        device_id={"seq": other},
+        device_id_type=MESH_ID,
+    )
+    aside.start()
+    rows_all[place, span(rank, 128), :] = normed(mine)
+    right, left = {"tensor": lax.rem(rank + 1, 4)}, {"tensor": lax.rem(rank + 3, 4)}
+    blocks = (place, other)
+
+    def pass_on(which, distance):
+        block_id = blocks[which]
+
+        @pl.when((rank < 3) & (rank >= distance))
+        def _():
+            moved(block_id, jnp.maximum(rank - distance, 0), send_sem.at[which, distance, 0], right).start()
+
+        @pl.when((rank > 0) & (rank + distance <= 3))
+        def _():
+            moved(block_id, jnp.minimum(rank + distance, 3), send_sem.at[which, distance, 1], left).start()
+
+    def pass_done(which, distance):
+        block_id = blocks[which]
+
+        @pl.when((rank < 3) & (rank >= distance))
+        def _():
+            moved(block_id, jnp.maximum(rank - distance, 0), send_sem.at[which, distance, 0], right).wait_send()
+
+        @pl.when((rank > 0) & (rank + distance <= 3))
+        def _():
+            moved(block_id, jnp.minimum(rank + distance, 3), send_sem.at[which, distance, 1], left).wait_send()
+
+    def project(block_id, origin):
+        view = span(origin, 128)
+        qkv[block_id, view, :] = to_low(dot_nn(rows_all[block_id, view, :], w_qkv[...]))
+
+    def rows_steps():
+        pass_on(0, 0)
+        moved(place, rank, core_sem.at[0, rank], {"seq": core}).start()
+        project(place, rank)
+        moved(other, rank, send_sem.at[0, 0, 3], {"seq": other}).wait_recv()
+        pass_on(1, 0)
+        moved(other, rank, core_sem.at[1, rank], {"seq": core}).start()
+        project(other, rank)
+        yield
+        for distance in (1, 2, 3):
+            for which in (0, 1):
+                block_id = blocks[which]
+                for way, ok, origin in (
+                    (0, rank >= distance, jnp.maximum(rank - distance, 0)),
+                    (1, rank + distance <= 3, jnp.minimum(rank + distance, 3)),
+                ):
+
+                    @pl.when(ok)
+                    def _():
+                        moved(block_id, origin, send_sem.at[which, distance, way], right).wait_recv()
+                        if distance < 3:
+                            if way == 0:
+
+                                @pl.when(rank < 3)
+                                def _():
+                                    moved(
+                                        block_id, origin, send_sem.at[which, distance, 0], right
+                                    ).start()
+
+                            else:
+
+                                @pl.when(rank > 0)
+                                def _():
+                                    moved(
+                                        block_id, origin, send_sem.at[which, distance, 1], left
+                                    ).start()
+
+                        moved(block_id, origin, core_sem.at[which, origin], {"seq": core}).start()
+                        project(block_id, origin)
+
+                yield
+        for which, block_id in enumerate((core, lax.rem(core + 2, 4))):
+            for origin in range(4):
+                moved(block_id, origin, core_sem.at[which, origin], {"seq": core}).wait_recv()
+                project(block_id, origin)
+        for which in (0, 1):
+            for distance in (0, 1, 2):
+                pass_done(which, distance)
+            for origin in range(4):
+                moved(blocks[which], origin, core_sem.at[which, origin], {"seq": core}).wait_send()
+
+    def piece_move(slot, origin, target):
+        view = kept.at[me, span(origin, extra), :]
+        return pltpu.make_async_remote_copy(
+            src_ref=view,
+            dst_ref=view,
+            send_sem=piece_send.at[slot],
+            recv_sem=piece_recv.at[origin],
+            device_id=target,
+            device_id_type=MESH_ID,
+        )
+
+    def piece_steps():
+        for slot in range(3):
+            piece_move(slot, rank, greeted[slot]).start()
+        first = line[...]
+        row = lax.broadcasted_iota(jnp.int32, (8, WIDE), 0)
+        for step in (1, 2, 4):
+            first = jnp.where(row // step % 2 == 1, pltpu.roll(first, step, 1), first)
+
+        def one(group, _):
+            table[span(group, 8), :] = pltpu.roll(first, 8 * group, 1)[:, 0 : 2 * BLOCK]
+            return 0
+
+        lax.fori_loop(0, BLOCK // 8, one, 0)
+        yield
+        for slot in range(3):
+            piece_move(slot, lax.rem(rank + slot + 1, 4), greeted[slot]).wait_recv()
+        for _ in plane_gather(kept, 4 * extra, ring_send, ring_recv):
+            yield
+        for slot in range(3):
+            piece_move(slot, rank, greeted[slot]).wait_send()
+
+    run_all(rows_steps(), piece_steps())
+    aside.wait_send()
+
+
+def opening(tokens, w_qkv, piece, vecs, line):
+    low, wide = jnp.bfloat16, jnp.float32
+    extra = piece.shape[0]
+    shapes = (
+        ((4, BLOCK, D), low),
+        ((4, BLOCK, 384), low),
+        ((8, 4 * extra, D), low),
+        ((BLOCK, 2 * BLOCK), wide),
+    )
     return pl.pallas_call(
-        bias_kernel,
-        out_shape=jax.ShapeDtypeStruct((BLOCK, 2 * BLOCK), jnp.float32),
-        in_specs=vmem_specs(1),
-        out_specs=pl.BlockSpec(memory_space=pltpu.VMEM),
-        compiler_params=pltpu.CompilerParams(vmem_limit_bytes=VMEM_LIMIT),
-        name="bias_table",
-    )(line)
-
-
-def diagonal_kernel(table, out, acc):
-    acc[...] = jnp.zeros_like(acc)
-
-    def one(group, _):
-        rows = table[span(group, 8), :]
-        wide = jnp.concatenate([rows, jnp.zeros((8, WIDE - 2 * BLOCK), jnp.float32)], axis=1)
-        acc[...] += pltpu.roll(wide, lax.rem(WIDE - 8 * group, WIDE), 1)
-        return 0
-
-    lax.fori_loop(0, BLOCK // 8, one, 0)
-    total = acc[...]
-    row = lax.broadcasted_iota(jnp.int32, (8, WIDE), 0)
-    for step in (1, 2, 4):
-        total = jnp.where(row // step % 2 == 1, pltpu.roll(total, WIDE - step, 1), total)
-    out[...] = jnp.broadcast_to(jnp.sum(total, axis=0, keepdims=True), (8, WIDE))
-
-
-def diagonal_sums(table):
+        opening_kernel,
+        out_shape=[jax.ShapeDtypeStruct(*one) for one in shapes],
+        in_specs=vmem_specs(5),
+        out_specs=vmem_specs(4),
+        scratch_shapes=[
+            pltpu.VMEM((128, D), low),
+            pltpu.SemaphoreType.DMA((2, 4, 4)),
+            pltpu.SemaphoreType.DMA((2, 4)),
+            pltpu.SemaphoreType.DMA((4, 4)),
+            pltpu.SemaphoreType.DMA((3,)),
+            pltpu.SemaphoreType.DMA((4,)),
+            pltpu.SemaphoreType.DMA((16,)),
+            pltpu.SemaphoreType.DMA((8, 2)),
+        ],
+        compiler_params=pltpu.CompilerParams(
+            collective_id=5, has_side_effects=True, vmem_limit_bytes=VMEM_LIMIT
+        ),
+        cost_estimate=pl.CostEstimate(
+            flops=30000000000, bytes_accessed=30000000, transcendentals=0
+        ),
+        name="opening",
+    )(tokens, w_qkv, piece, vecs, line)
+
+
+def pair_sum(part, near_got, far_got, result, rows, send_sem, recv_sem):
+    side, place, half, rank = plane_place()
+    mine = place // 2
+    across, beside = 1 - side, 1 - mine
+    me = 2 * side + mine
+    at_x, at_y, at_d = 2 * across + mine, 2 * side + beside, 2 * across + beside
+    to_x, to_y = {"dp": across}, {"seq": lax.rem(place + 2, 4)}
+    size = rows // 2
+    views = (pl.ds(0, size), pl.ds(size, size))
+
+    def moved(source, target_ref, slot, target):
+        return pltpu.make_async_remote_copy(
+            src_ref=source,
+            dst_ref=target_ref,
+            send_sem=send_sem.at[slot],
+            recv_sem=recv_sem.at[slot],
+            device_id=target,
+            device_id_type=MESH_ID,
+        )
+
+    def add_into(owner, view, other):
+        part[owner, view, :] = to_low(
+            part[owner, view, :].astype(jnp.float32) + other.astype(jnp.float32)
+        )
+
+    near = [
+        moved(part.at[at_d, views[0], :], near_got.at[0], 0, to_x),
+        moved(part.at[at_d, views[1], :], near_got.at[1], 1, to_y),
+        moved(part.at[at_x, views[0], :], near_got.at[2], 2, to_x),
+        moved(part.at[at_y, views[1], :], near_got.at[3], 3, to_y),
+    ]
+    for one in near:
+        one.start()
+    yield
+    near[0].wait_recv()
+    add_into(at_y, views[0], near_got[0])
+    far = [
+        moved(part.at[at_y, views[0], :], far_got.at[0], 4, to_y),
+        moved(part.at[at_x, views[1], :], far_got.at[1], 5, to_x),
+    ]
+    far[0].start()
+    near[1].wait_recv()
+    add_into(at_x, views[1], near_got[1])
+    far[1].start()
+    yield
+    near[2].wait_recv()
+    add_into(me, views[0], near_got[2])
+    near[3].wait_recv()
+    add_into(me, views[1], near_got[3])
+    for slot, view in enumerate(views):
+        far[slot].wait_recv()
+        result[me, view, :] = to_low(
+            part[me, view, :].astype(jnp.float32) + far_got[slot].astype(jnp.float32)
+        )
+
+    def given(owner, which, slot, target):
+        view = result.at[owner, views[which], :]
+        return moved(view, view, slot, target)
+
+    own = [
+        given(me, 0, 6, to_x),
+        given(me, 1, 7, to_y),
+        given(me, 1, 8, to_x),
+        given(me, 0, 9, to_y),
+    ]
+    for one in own:
+        one.start()
+    yield
+    given(at_x, 0, 6, to_x).wait_recv()
+    last = [given(at_x, 0, 10, to_y), given(at_y, 1, 11, to_x)]
+    last[0].start()
+    given(at_y, 1, 7, to_y).wait_recv()
+    last[1].start()
+    yield
+    given(at_x, 1, 8, to_x).wait_recv()
+    given(at_y, 0, 9, to_y).wait_recv()
+    given(at_d, 0, 10, to_y).wait_recv()
+    given(at_d, 1, 11, to_x).wait_recv()
+    for one in near + far + own + last:
+        one.wait_send()
+
+
+PAIR_ROWS = 640
+
+
+def closing_kernel(
+    d_qkv, w_qkv, tokens, d_hidden, vecs, rows_all, state_low, d_qkvst, os_rows, du_rows,
+    d_start, dz_sum, spots, small, out_part,
+    inputs_grad, pair_out, sout_out, small_out,
+    leave, came, sums, got_r, got_l, final, cross, cross_got,
+    pair_part, pair_near, pair_far,
+    work, core_got, near_got, far_got, total, z_part, z_got,
+    diag, small_z, small_p,
+    line_send, line_recv, way_send, way_recv, pair_send, pair_recv, core_sem,
+    ring_send, ring_recv, zs_send, zs_recv, gather_send, gather_recv, small_send, small_recv,
+):
+    side, place, half, rank = plane_place()
+    mine = place // 2
+    core = place + 1 - 2 * half
+    other = lax.rem(place + 2, 4)
+    me = plane_index(side, place)
+    ranks = [lax.rem(rank + step, 4) for step in (1, 2, 3)]
+    spots_of = [lax.rem(me + step, 8) for step in range(1, 8)]
+    barrier = pltpu.get_barrier_semaphore()
+    for target in ranks:
+        pl.semaphore_signal(barrier, inc=1, device_id={"tensor": target}, device_id_type=MESH_ID)
+    for target in spots_of:
+        pl.semaphore_signal(
+            barrier,
+            inc=1,
+            device_id={"dp": target // 4, "seq": lax.rem(target, 4)},
+            device_id_type=MESH_ID,
+        )
+    gain = vecs[3:4, :]
+    right, left = {"tensor": lax.rem(rank + 1, 4)}, {"tensor": lax.rem(rank + 3, 4)}
+
+    def moved(source, target_ref, send, recv, target):
+        return pltpu.make_async_remote_copy(
+            src_ref=source,
+            dst_ref=target_ref,
+            send_sem=send,
+            recv_sem=recv,
+            device_id=target,
+            device_id_type=MESH_ID,
+        )
+
+    def to_core(which):
+        return moved(
+            leave.at[which], came.at[which], line_send.at[which], line_recv.at[which], {"seq": core}
+        )
+
+    def crossing():
+        return moved(cross, cross_got, line_send.at[2], line_recv.at[2], {"seq": other})
+
+    def step_right(which, target):
+        return moved(
+            sums.at[which, target], got_r.at[which, target],
+            way_send.at[which, target], way_recv.at[0, which, target], right,
+        )
+
+    def step_left(which, target):
+        return moved(
+            sums.at[which, target], got_l.at[which, target],
+            way_send.at[which, target], way_recv.at[1, which, target], left,
+        )
+
+    def add_sum(which, target, got):
+        sums[which, target] = to_low(
+            sums[which, target].astype(jnp.float32) + got[which, target].astype(jnp.float32)
+        )
+
+    def line_steps():
+        for which, block_id in enumerate((lax.rem(core + 2, 4), core)):
+
+            def partner(chunk, _):
+                rows = span(chunk, ROWS)
+                leave[which, rows, :] = to_low(dot_nt(d_qkv[block_id, rows, :], w_qkv[...]))
+                return 0
+
+            lax.fori_loop(0, CHUNKS, partner, 0)
+            if which == 0:
+                pl.semaphore_wait(barrier, 10)
+            to_core(which).start()
+        for which, block_id in enumerate((other, place)):
+            to_core(which).wait_recv()
+
+            def own(chunk, _):
+                rows = span(chunk, ROWS)
+                sums[which, chunk] = to_low(
+                    dot_nt(d_qkv[block_id, rows, :], w_qkv[...])
+                    + came[which, rows, :].astype(jnp.float32)
+                )
+                return 0
+
+            lax.fori_loop(0, CHUNKS, own, 0)
+        for which in (0, 1):
+            for to_right, to_left in ((3, 0), (2, 1), (1, 2)):
+
+                @pl.when(rank < to_right)
+                def _():
+                    @pl.when(rank > 0)
+                    def _():
+                        step_right(which, to_right).wait_recv()
+                        add_sum(which, to_right, got_r)
+
+                    step_right(which, to_right).start()
+
+                @pl.when(rank > to_left)
+                def _():
+                    @pl.when(rank < 3)
+                    def _():
+                        step_left(which, to_left).wait_recv()
+                        add_sum(which, to_left, got_l)
+
+                    step_left(which, to_left).start()
+
+                yield
+            final[which] = sums[which, rank].astype(jnp.float32)
+
+            @pl.when(rank > 0)
+            def _():
+                step_right(which, rank).wait_recv()
+                final[which] += got_r[which, rank].astype(jnp.float32)
+
+            @pl.when(rank < 3)
+            def _():
+                step_left(which, rank).wait_recv()
+                final[which] += got_l[which, rank].astype(jnp.float32)
+
+            if which == 0:
+                cross[...] = to_low(final[0])
+                crossing().start()
+            yield
+        crossing().wait_recv()
+        final[0] = cross_got[...].astype(jnp.float32)
+        small_z[rank] = small[...]
+        for which, row_set in ((1, mine), (0, 1 - mine)):
+            grad = final[which]
+            centered, scale = norm_parts(tokens[row_set].astype(jnp.float32))
+            normed = centered * scale
+            small_z[rank, 0:1, :] += jnp.sum(grad * normed, axis=0, keepdims=True)
+            lifted = grad * gain
+            inputs_grad[row_set] = d_hidden[row_set] + scale * (
+                lifted
+                - jnp.mean(lifted, axis=-1, keepdims=True)
+                - normed * jnp.mean(lifted * normed, axis=-1, keepdims=True)
+            )
+        crossing().wait_send()
+        for which in (0, 1):
+            to_core(which).wait_send()
+            for target in range(4):
+
+                @pl.when(rank < target)
+                def _():
+                    step_right(which, target).wait_send()
+
+                @pl.when(rank > target)
+                def _():
+                    step_left(which, target).wait_send()
+
+    def pair_steps():
+        for chunk in range(4):
+            if chunk < 3:
+                first = 128 * chunk
+
+                def one(block_id, acc):
+                    acc = acc + dot_tn(d_qkv[block_id, :, first : first + 128], rows_all[block_id])
+                    if chunk > 0:
+                        acc = acc + dot_tn(
+                            d_qkvst[block_id, :, first : first + 128], state_low[block_id]
+                        )
+                    return acc
+
+            else:
+
+                def one(block_id, acc):
+                    return acc + dot_tn(d_qkvst[block_id, :, 0:128], state_low[block_id])
+
+            acc = lax.fori_loop(0, 4, one, jnp.zeros((128, D), jnp.float32))
+            low = to_low(acc)
+            first = 128 * chunk
+            while first < 128 * (chunk + 1):
+                owner, inside = first // 160, first % 160
+                size = min(160 - inside, 128 * (chunk + 1) - first)
+                begin = first - 128 * chunk
+                pair_part[owner, inside : inside + size, :] = low[begin : begin + size, :]
+                first += size
+        pair_part[3, 32:96, :] = to_low(d_start[...])
+        pair_part[3, 96:160, :] = jnp.zeros((64, D), jnp.bfloat16)
+        for _ in pair_sum(
+            pair_part, pair_near, pair_far, pair_out.at[half], 160, pair_send, pair_recv
+        ):
+            yield
+        full = moved(
+            pair_out.at[half], pair_out.at[half], core_sem.at[0], core_sem.at[1], {"seq": core}
+        )
+        full.start()
+        yield
+        moved(
+            pair_out.at[1 - half], pair_out.at[1 - half], core_sem.at[0], core_sem.at[1],
+            {"seq": core},
+        ).wait_recv()
+        full.wait_send()
+
+    def sout_steps():
+        for head in range(LINE):
+            low = to_low(dot_tn(os_rows[:, 128 * head : 128 * head + 128], du_rows[...]))
+            for piece in range(4):
+                work[
+                    4 * (head % 2) + piece, 32 * (head // 2) : 32 * (head // 2) + 32, :
+                ] = low[32 * piece : 32 * piece + 32, :]
+        for _ in plane_scatter(
+            work, core_got, near_got, far_got, total, 128, ring_send, ring_recv
+        ):
+            yield
+        z_part[:, 0:32, :] = to_low(total[...]).reshape(4, 32, D)
+        z_part[:, 32:64, :] = out_part[...].reshape(4, 32, D)
+        out = [
+            moved(
+                z_part.at[target], z_got.at[rank], zs_send.at[slot], zs_recv.at[rank],
+                {"tensor": target},
+            )
+            for slot, target in enumerate(ranks)
+        ]
+        for one in out:
+            one.start()
+        z_got[rank] = z_part[rank]
+        yield
+        for slot, target in enumerate(ranks):
+            moved(
+                z_part.at[target], z_got.at[target], zs_send.at[slot], zs_recv.at[target],
+                {"tensor": target},
+            ).wait_recv()
+        acc = z_got[0].astype(jnp.float32)
+        for target in range(1, 4):
+            acc = acc + z_got[target].astype(jnp.float32)
+        sout_out[me] = to_low(acc)
+        for _ in plane_gather(sout_out, 64, gather_send, gather_recv):
+            yield
+        for one in out:
+            one.wait_send()
+
+    def diag_steps():
+        diag[...] = jnp.zeros_like(diag)
+        for part in range(4):
+
+            def one(group, _):
+                rows = dz_sum[span(group, 8), :]
+                wide = jnp.concatenate(
+                    [rows, jnp.zeros((8, WIDE - 2 * BLOCK), jnp.float32)], axis=1
+                )
+                diag[...] += pltpu.roll(wide, lax.rem(WIDE - 8 * group, WIDE), 1)
+                return 0
+
+            lax.fori_loop(16 * part, 16 * part + 16, one, 0)
+            yield
+        total_line = diag[...]
+        row = lax.broadcasted_iota(jnp.int32, (8, WIDE), 0)
+        for step in (1, 2, 4):
+            total_line = jnp.where(
+                row // step % 2 == 1, pltpu.roll(total_line, WIDE - step, 1), total_line
+            )
+        line_sum = jnp.broadcast_to(jnp.sum(total_line, axis=0, keepdims=True), (8, WIDE))
+        high = to_low(line_sum)
+        rest = to_low(line_sum - high.astype(jnp.float32))
+        diag[:, 0:256] = dot_nn(high, spots[...]) + dot_nn(rest, spots[...])
+
+    run_all(line_steps(), pair_steps(), sout_steps(), diag_steps())
+    small_z[rank, 4:5, 0:256] = diag[0:1, 0:256]
+
+    def small_over_z(slot, sender, target):
+        return moved(
+            small_z.at[sender], small_z.at[sender], small_send.at[slot], small_recv.at[sender],
+            {"tensor": target},
+        )
+
+    for slot, target in enumerate(ranks):
+        small_over_z(slot, rank, target).start()
+    for slot, target in enumerate(ranks):
+        small_over_z(slot, target, target).wait_recv()
+    small_p[me] = small_z[0] + small_z[1] + small_z[2] + small_z[3]
+
+    def small_over_plane(slot, sender, target):
+        return moved(
+            small_p.at[sender], small_p.at[sender], small_send.at[3 + slot],
+            small_recv.at[4 + sender],
+            {"dp": target // 4, "seq": lax.rem(target, 4)},
+        )
+
+    for slot, target in enumerate(spots_of):
+        small_over_plane(slot, me, target).start()
+    for slot, target in enumerate(spots_of):
+        small_over_plane(slot, target, target).wait_recv()
+    acc = small_p[0]
+    for target in range(1, 8):
+        acc = acc + small_p[target]
+    small_out[...] = acc
+    for slot, target in enumerate(ranks):
+        small_over_z(slot, rank, target).wait_send()
+    for slot, target in enumerate(spots_of):
+        small_over_plane(slot, me, target).wait_send()
+
+
+def closing(
+    d_qkv, w_qkv, tokens, d_hidden, vecs, rows_all, state_low, d_qkvst, os_rows, du_rows,
+    d_start, dz_sum, spots, small, out_part,
+):
+    low, wide = jnp.bfloat16, jnp.float32
+    shapes = (
+        ((2, 128, D), wide),
+        ((2, 4, PAIR_ROWS // 4, D), low),
+        ((8, 64, D), low),
+        ((8, D), wide),
+    )
+    dma = pltpu.SemaphoreType.DMA
     return pl.pallas_call(
-        diagonal_kernel,
-        out_shape=jax.ShapeDtypeStruct((8, WIDE), jnp.float32),
-        in_specs=vmem_specs(1),
-        out_specs=pl.BlockSpec(memory_space=pltpu.VMEM),
-        scratch_shapes=[pltpu.VMEM((8, WIDE), jnp.float32)],
-        compiler_params=pltpu.CompilerParams(vmem_limit_bytes=VMEM_LIMIT),
-        name="diagonal_sums",
-    )(table)
-
-
-def own_half(part, half, axis):
-    empty = jnp.zeros_like(part)
-    return jnp.where(
-        half == 0,
-        jnp.concatenate([part, empty], axis=axis),
-        jnp.concatenate([empty, part], axis=axis),
+        closing_kernel,
+        out_shape=[jax.ShapeDtypeStruct(*one) for one in shapes],
+        in_specs=vmem_specs(15),
+        out_specs=vmem_specs(4),
+        scratch_shapes=[
+            pltpu.VMEM((2, BLOCK, D), low),
+            pltpu.VMEM((2, BLOCK, D), low),
+            pltpu.VMEM((2, 4, 128, D), low),
+            pltpu.VMEM((2, 4, 128, D), low),
+            pltpu.VMEM((2, 4, 128, D), low),
+            pltpu.VMEM((2, 128, D), wide),
+            pltpu.VMEM((128, D), low),
+            pltpu.VMEM((128, D), low),
+            pltpu.VMEM((4, PAIR_ROWS // 4, D), low),
+            pltpu.VMEM((4, PAIR_ROWS // 8, D), low),
+            pltpu.VMEM((2, PAIR_ROWS // 8, D), low),
+            pltpu.VMEM((8, 128, D), low),
+            pltpu.VMEM((4, 128, D), low),
+            pltpu.VMEM((4, 64, D), low),
+            pltpu.VMEM((2, 64, D), low),
+            pltpu.VMEM((128, D), wide),
+            pltpu.VMEM((4, 64, D), low),
+            pltpu.VMEM((4, 64, D), low),
+            pltpu.VMEM((8, WIDE), wide),
+            pltpu.VMEM((4, 8, D), wide),
+            pltpu.VMEM((8, 8, D), wide),
+            dma((3,)), dma((3,)), dma((2, 4)), dma((2, 2, 4)), dma((12,)), dma((12,)), dma((2,)),
+            dma((10,)), dma((10,)), dma((3,)), dma((4,)), dma((16,)), dma((8, 2)), dma((10,)),
+            dma((12,)),
+        ],
+        compiler_params=pltpu.CompilerParams(
+            collective_id=6, has_side_effects=True, vmem_limit_bytes=VMEM_LIMIT
+        ),
+        cost_estimate=pl.CostEstimate(
+            flops=30000000000, bytes_accessed=30000000, transcendentals=0
+        ),
+        name="closing",
+    )(
+        d_qkv, w_qkv, tokens, d_hidden, vecs, rows_all, state_low, d_qkvst, os_rows, du_rows,
+        d_start, dz_sum, spots, small, out_part,
     )
 
 
@@ -1325,78 +1915,97 @@
     place = lax.axis_index("seq")
     half = lax.rem(place, 2)
     mine = place // 2
+    plane = ("dp", "seq")
+    spot = 4 * lax.axis_index("dp") + place
+    head = 2 * lax.axis_index("tensor") + half
     head_of = lambda weight: lax.dynamic_slice_in_dim(weight, half * 128, 128, 1)
     gate_value = jax.nn.sigmoid(gate_bias)
-    vecs = jnp.stack([state_gain, gate_value, mlp_gain] + [jnp.zeros_like(gate_value)] * 5)
+    vecs = jnp.stack(
+        [state_gain, gate_value, mlp_gain, attn_gain] + [jnp.zeros_like(gate_value)] * 4
+    )
     offsets = jnp.arange(WIDE) - BLOCK
     offsets = jnp.where(offsets >= WIDE - 2 * BLOCK, offsets - WIDE, offsets)
     bucket_ids = bucket_of(offsets)
-    one_hot = (bucket_ids[:, None] == jnp.arange(BUCKETS)[None, :]).astype(wide)
+    one_hot = bucket_ids[:, None] == jnp.arange(BUCKETS)[None, :]
     my_bias = jnp.where(half == 0, rel_bias[:, 0], rel_bias[:, 1])
-    bias_line = jnp.sum(one_hot * my_bias[None, :], axis=1)
-    bias = bias_table(jnp.broadcast_to(bias_line[None, :], (8, WIDE)))
+    bias_line = jnp.sum(jnp.where(one_hot, my_bias[None, :], 0.0), axis=1)
+    lane = jnp.arange(LINE * BUCKETS)
+    spots = (
+        (bucket_ids[:, None] == lax.rem(lane, BUCKETS)[None, :]) & (lane // BUCKETS == head)[None, :]
+    ).astype(low)
     segs = jnp.broadcast_to(jnp.repeat(seg_starts[:, 0], 2)[:, None, None], (4, 1, 128))
     segs = swap_seq(segs)[:, 0, 0]
-    scal = jnp.concatenate([lax.dynamic_slice_in_dim(lengths, mine, 1, 0), segs])
-
-    inputs_wide = inputs.astype(wide)
-    tokens_low = gather_rows(to_low(layer_norm(inputs_wide, attn_gain)))
-    w_qkv = jnp.stack(
-        [w.reshape(D, 2, 128) for w in (w_query, w_key, w_value)], axis=2
-    ).reshape(D, 2, 384)
-    qkv_native = to_low(
-        jnp.einsum("sqd,dhe->shqe", tokens_low, w_qkv, preferred_element_type=wide)
-    )
-    qkv = swap_seq(qkv_native.reshape(4, BLOCK, 384))
-    start_all = lax.all_gather(to_low(init_state), "tensor", axis=0, tiled=True)
-    w_sout_all = lax.all_gather(w_sout, "tensor", axis=0, tiled=True)
-    plane = ("dp", "seq")
-    spot = 4 * lax.axis_index("dp") + place
+    cots = swap_seq(state_cot.reshape(4, 64, D))
+    cot_used = lax.all_gather(out_cot.reshape(256, D), plane, axis=0, tiled=True)
+
+    w_qkv = jnp.concatenate([head_of(w_query), head_of(w_key), head_of(w_value)], axis=1)
+    w_state = jnp.concatenate([head_of(w_squery), w_qkv[:, 128:]], axis=1)
+    piece = jnp.concatenate(
+        [
+            lax.dynamic_slice_in_dim(w_sout, spot * 32, 32, 0),
+            to_low(lax.dynamic_slice_in_dim(init_state, spot * 16, 16, 0)),
+            lax.dynamic_slice_in_dim(w_out, spot * 32, 32, 0),
+        ],
+        axis=0,
+    )
+    rows_all, qkv, kept, bias = opening(
+        inputs, w_qkv, piece, vecs, jnp.broadcast_to(bias_line[None, :], (8, WIDE))
+    )
+    kept = kept.reshape(8, 4, 80, D).transpose(1, 0, 2, 3)
+    w_sout_all = kept[:, :, :32].reshape(D, D)
+    start_all = kept[:, :, 32:48].reshape(STATES, D)
+    w_out_all = kept[:, :, 48:].reshape(D, D)
+
     ff_own = w_up.shape[1] // 8
-    ff_slices = jnp.concatenate(
+    piece_of = lambda weight: lax.dynamic_slice_in_dim(weight, spot * 32, 32, 1).T
+    pieces = jnp.concatenate(
         [
+            piece_of(w_squery),
+            piece_of(w_key),
+            piece_of(w_value),
             lax.dynamic_slice_in_dim(w_up, spot * ff_own, ff_own, 1).T,
             lax.dynamic_slice_in_dim(w_down, spot * ff_own, ff_own, 0),
         ],
         axis=0,
     )
-    w_back_own = jnp.concatenate(
-        [w.T.reshape(2, 128, D) for w in (w_squery, w_key, w_value)], axis=1
-    )
-    w_sout_all, w_out_own, ff_slices, cot_own, w_back_own = lax.optimization_barrier(
-        (w_sout_all, w_out, ff_slices, out_cot, w_back_own)
-    )
-    w_out_all = lax.all_gather(w_out_own, "tensor", axis=0, tiled=True)
-    ff_all = lax.all_gather(ff_slices, "tensor", axis=0, tiled=True).reshape(4, 2, ff_own, D)
-    up_rows = ff_all[:, 0].reshape(4 * ff_own, D)
-    down_rows = ff_all[:, 1].reshape(4 * ff_own, D)
-    cot_used = lax.all_gather(cot_own.reshape(256, D), plane, axis=0, tiled=True)
-    w_back = lax.all_gather(w_back_own, "tensor", axis=0, tiled=True)
-    w_state = jnp.concatenate([head_of(w_squery), head_of(w_key), head_of(w_value)], axis=1)
+    qkv, pieces, segs = lax.optimization_barrier((qkv, pieces, segs))
+    scal = jnp.concatenate([lax.dynamic_slice_in_dim(lengths, mine, 1, 0), segs])
+    spread = lax.all_gather(pieces, "tensor", axis=0, tiled=True).reshape(4, 96 + 2 * ff_own, D)
+    up_rows = spread[:, 96 : 96 + ff_own].reshape(4 * ff_own, D)
+    down_rows = spread[:, 96 + ff_own :].reshape(4 * ff_own, D)
+
     mixed, lse_tok, state_rows, state_low, qkvst, lse_st, os_rows = forward_chain(
         scal, qkv, start_all, w_state, w_sout_all, vecs, bias
     )
     other_block = lax.rem(place + 2, 4)
     sent = lax.dynamic_slice_in_dim(state_rows, other_block, 1, 0)[0].astype(low)
     came = lax.ppermute(sent, "seq", [(source, (source + 2) % 4) for source in range(4)])
-    kept = lax.dynamic_slice_in_dim(state_rows, place, 1, 0)[0]
+    kept_rows = lax.dynamic_slice_in_dim(state_rows, place, 1, 0)[0]
     state_out = jnp.where(
-        mine == 0, jnp.stack([kept, came.astype(wide)]), jnp.stack([came.astype(wide), kept])
-    )
-
+        mine == 0,
+        jnp.stack([kept_rows, came.astype(wide)]),
+        jnp.stack([came.astype(wide), kept_rows]),
+    )
+
+    mixed, back_piece, cots = lax.optimization_barrier(
+        (mixed, spread[:, 0:96].reshape(384, D), cots)
+    )
+    w_back = lax.all_gather(back_piece, plane, axis=0, tiled=True)
     hidden_in, mixed_rows, mid_all = middle_forward(mixed, inputs, w_out_all, vecs)
     mid_low = mid_all.reshape(2048, D)
     pre_act = matmul_t(mid_low, up_rows)
     hidden_low = to_low(jax.nn.gelu(pre_act))
-    mlp_part = to_low(matmul(hidden_low, down_rows))
     grad_hidden_act = matmul_t(cot_used, down_rows)
     grad_pre = to_low(gelu_back(pre_act, grad_hidden_act))
     d_mid_part = to_low(matmul(grad_pre, up_rows))
+    d_mid_part, w_back = lax.optimization_barrier((d_mid_part, w_back))
+    w_back = (
+        w_back.reshape(2, 4, 4, 3, 32, D).transpose(2, 0, 3, 1, 4, 5).reshape(LINE, 384, D)
+    )
     grad_hidden, grad_low, d_mixed, mlp_sums = middle_backward(
         d_mid_part.reshape(8, 256, D), hidden_in, out_cot, w_out_all, vecs
     )
-    mlp_rows = lax.psum_scatter(mlp_part, plane, scatter_dimension=0, tiled=True)
-    tokens_out = (hidden_in + mlp_rows.reshape(2, 128, D).astype(wide)).astype(low)
+    mlp_part = to_low(matmul(hidden_low, down_rows))
     ff_grads = jnp.stack(
         [
             outer_sum(grad_pre, mid_low).astype(low).reshape(4, ff_own, D),
@@ -1404,68 +2013,64 @@
         ],
         axis=1,
     )
+    out_part = outer_sum(mixed_rows, grad_low).astype(low)
+    out_part = out_part.reshape(4, 8, 32, D).transpose(1, 0, 2, 3).reshape(D, D)
+    d_mixed, mlp_part, ff_grads, out_part = lax.optimization_barrier(
+        (d_mixed, mlp_part, ff_grads, out_part)
+    )
+    mlp_rows = lax.psum_scatter(mlp_part, plane, scatter_dimension=0, tiled=True)
     ff_sum = lax.psum_scatter(
         ff_grads.reshape(8 * ff_own, D), "tensor", scatter_dimension=0, tiled=True
     )
+    out_part = lax.psum_scatter(out_part, plane, scatter_dimension=0, tiled=True)
+
+    start_half = lax.dynamic_slice_in_dim(to_low(init_state).astype(wide), half * 64, 64, 0)
+    states = jnp.concatenate(
+        [start_half[None], lax.dynamic_slice_in_dim(state_rows, half * 64, 64, 1)], axis=0
+    )
+    d_qkv, d_qkvst, du_rows, d_start, sums, dz_sum = backward_chain(
+        scal, qkv, d_mixed, lse_tok, qkvst, lse_st, states, cots, w_back, w_sout_all, vecs, bias
+    )
+    d_qkv, ff_sum, out_part = lax.optimization_barrier((d_qkv, ff_sum, out_part))
+    tokens_out = (hidden_in + mlp_rows.reshape(2, 128, D).astype(wide)).astype(low)
     ff_total = lax.all_gather(ff_sum, plane, axis=0, tiled=True).reshape(8, 2, ff_own, D)
     up_grad = ff_total[:, 0].reshape(8 * ff_own, D).T.astype(wide)
     down_grad = ff_total[:, 1].reshape(8 * ff_own, D).astype(wide)
-    out_part = lax.psum_scatter(
-        outer_sum(mixed_rows, grad_low).astype(low), "tensor", scatter_dimension=0, tiled=True
-    )
-
-    cots = swap_seq(state_cot.reshape(4, 64, D))
-    start_half = lax.dynamic_slice_in_dim(to_low(init_state).astype(wide), half * 64, 64, 0)
-    states = jnp.concatenate(
-        [start_half[None], lax.dynamic_slice_in_dim(state_rows, half * 64, 64, 1)], axis=0
-    )
-    d_qkv, d_qkvst, du_rows, d_start, sums, dz_sum = backward_chain(
-        scal, qkv, d_mixed, lse_tok, qkvst, lse_st, states, cots, w_back, w_sout_all, vecs, bias
-    )
-    diag = diagonal_sums(dz_sum)[0]
-    bias_grad = own_half(
-        jnp.sum(one_hot * diag[:, None], axis=0)[:, None], half, 1
-    )
-    d_native = swap_seq(d_qkv).reshape(2, 2, BLOCK, 384)
-    grad_tokens = sum_rows(
-        jnp.einsum("shqe,dhe->sqd", d_native, w_qkv, preferred_element_type=wide)
-    )
-    grad_in_norm, attn_gain_grad = norm_back(inputs_wide, attn_gain, grad_tokens)
-    inputs_grad = grad_hidden + grad_in_norm
-    tok_grads = jnp.einsum("sqd,shqe->dhe", tokens_low, d_native, preferred_element_type=wide)
-    st_grads = outer_sum(state_low, d_qkvst)
-    query_grad = tok_grads[:, :, 0:128].reshape(D, 256)
-    key_grad = tok_grads[:, :, 128:256].reshape(D, 256) + own_half(st_grads[:, 128:256], half, 1)
-    value_grad = tok_grads[:, :, 256:384].reshape(D, 256) + own_half(st_grads[:, 256:384], half, 1)
-    squery_grad = own_half(st_grads[:, 0:128], half, 1)
-    sout_part = lax.psum_scatter(
-        outer_sum(os_rows, du_rows).astype(low), "tensor", scatter_dimension=0, tiled=True
-    )
-    state_part = own_half(d_start, half, 0)
-    gains = lax.psum(jnp.stack([attn_gain_grad, sums[1], mlp_sums[0], sums[0]]), "tensor")
-
-    def total(part):
-        return lax.psum(part.astype(low), ("dp", "seq")).astype(wide)
-
-    gain_total = total(gains)
+    small = jnp.concatenate(
+        [jnp.zeros((1, D), wide), sums[1:2], mlp_sums[0:1], sums[0:1], jnp.zeros((4, D), wide)]
+    )
+    inputs_grad, pair, two_grads, small = closing(
+        d_qkv, w_qkv, inputs, grad_hidden, vecs, rows_all, state_low, d_qkvst,
+        os_rows.reshape(256, D), du_rows.reshape(256, D), d_start, dz_sum, spots, small, out_part,
+    )
+    pair = pair.reshape(2, PAIR_ROWS, D)
+    out_grad = two_grads[:, 32:].reshape(256, D).astype(wide)
+    sout_grad = two_grads[:, :32].reshape(256, D).astype(wide)
+
+    def turned(first):
+        return pair[:, first : first + 128].reshape(256, D).T.astype(wide)
+
+    bias_grad = lax.dynamic_slice_in_dim(
+        small[4, : LINE * BUCKETS].reshape(4, 2, BUCKETS), lax.axis_index("tensor"), 1, 0
+    )[0].T
     return (
         tokens_out,
         state_out[:, None],
         inputs_grad,
-        total(state_part),
-        gain_total[0],
-        gain_total[1],
-        gain_total[2],
-        total(query_grad),
-        total(key_grad),
-        total(value_grad),
-        total(out_part),
-        total(squery_grad),
-        total(sout_part),
+        pair[:, 512:576].reshape(128, D).astype(wide),
+        small[0],
+        small[1],
+        small[2],
+        turned(0),
+        turned(128),
+        turned(256),
+        out_grad,
+        turned(384),
+        sout_grad,
         up_grad,
         down_grad,
-        total(bias_grad),
-        gain_total[3],
+        bias_grad,
+        small[3],
     )
 
 

time: 892 us -> 656 us (0.74)
  waiting for transfers between devices: 310 us -> 7.16 us
  Pallas kernels: 363 us -> 501 us
  blocking collectives: 54 us -> 0 us
  local copies, waits for them, and re-layouts: 33.6 us -> 65.1 us
  other arithmetic: 44.8 us -> 21 us
  matrix products: 50.8 us -> 28.6 us
    pallas_call x2, Pallas kernels: 16.7 us -> 186 us  [the longest x1 120 us: closing(): pl.pallas_call(closing_kernel, out_shape=[jax.ShapeDtypeStruct(*one) for...]
    all_gather x7 -> x3, waiting for transfers between devices: 119 us -> 0.02 us  [the longest x1 0.02 us: line_body(): lax.all_gather(pieces, 'tensor', axis=0, tiled=True)]
    reduce_scatter x3 -> x1, waiting for transfers between devices: 44.6 us -> 0.02 us  [line_body(): lax.psum_scatter(out_part, plane, scatter_dimension=0, tiled=True)]
    psum x1 -> x0, waiting for transfers between devices: 43 us -> none  [total(): return lax.psum(part.astype(low), ('dp', 'seq')).astype(wide)]
    reduce_scatter x1, waiting for transfers between devices: 33.5 us -> 0.01 us  [line_body(): lax.psum_scatter(mlp_part, plane, scatter_dimension=0, tiled=True)]
    psum x2 -> x0, blocking collectives: 30.1 us -> none  [the longest x1 16.9 us: line_body(): lax.psum(jnp.stack([attn_gain_grad, sums[1], mlp_sums[0], sums[0]]), 'ten...]
    reduce_scatter x1, waiting for transfers between devices: 28.8 us -> 0.02 us  [line_body(): lax.psum_scatter(ff_grads.reshape(8 * ff_own, D), 'tensor', scatter_dimen...]
    all_gather x1, waiting for transfers between devices: 28.3 us -> 0.01 us  [line_body(): lax.all_gather(ff_sum, plane, axis=0, tiled=True).reshape(8, 2, ff_own, D)]
  transfers between devices with their start and end apart: 18 -> 10, of which waited for: 10 -> 1; matrix products, arithmetic and copies ran while one was open for 13% -> 14% of each run, Pallas kernels for 41% -> 70%
where the time goes in v3:
time: 656 us; the launch traced here: 648 us
  Pallas kernels  501 us (76%)
  local copies, waits for them, and re-layouts  65.1 us (10%)
  matrix products  28.6 us (4%)
  other arithmetic  21 us (3%)
  between operations  15.2 us (2%)
  starting transfers between devices  9.97 us (2%)
  waiting for transfers between devices  7.16 us (1%)
    pallas_call x1, Pallas kernels, closing(): pl.pallas_call(closing_kernel, out_shape=[jax.ShapeDtypeStruct(*one) for...  120 us
    pallas_call x1, Pallas kernels, backward_chain(): pl.pallas_call(backward_kernel, out_shape=[jax.ShapeDtypeStruct(*one) for...  111 us
    pallas_call x1, Pallas kernels, forward_chain(): pl.pallas_call(forward_kernel, out_shape=[jax.ShapeDtypeStruct(*one) for...  105 us
    pallas_call x1, Pallas kernels, opening(): pl.pallas_call(opening_kernel, out_shape=[jax.ShapeDtypeStruct(*one) for...  65.9 us
    pallas_call x1, Pallas kernels, middle_forward(): pl.pallas_call(middle_forward_kernel, out_shape=[jax.ShapeDtypeStruct(*on...  54.3 us
    pallas_call x1, Pallas kernels, middle_backward(): pl.pallas_call(middle_backward_kernel, out_shape=[jax.ShapeDtypeStruct(*o...  45.3 us
  transfers between devices with their start and end apart: 10, of which 1 were waited for; matrix products, arithmetic and copies ran while one was open for 14% of the time, Pallas kernels for 70%

profile of v3, /device:TPU:0, one launch (start us, length us, event | category | flops | bytes accessed | tf_op | source)
XLA Modules:
  0.0 648.2 jit_solution(8183587935109381026)
XLA Ops:
  7.2 0.9 broadcast_in_dim.44
  8.8 4.2 all-to-all-start
  14.1 1.1 constant_dynamic-slice_fusion.6
  15.3 1.2 constant_dynamic-slice_fusion.4
  16.8 1.1 constant_dynamic-slice_fusion.2
  18.1 0.9 dynamic-slice_convert_fusion.2
  18.9 0.9 constant_dynamic-slice_fusion.7
  20.6 1.3 pad_maximum_fusion.2
  23.2 65.9 %opening.1 = (bf16[4,512,1024]{2,1,0:T(8,128)(2,1)}, bf16[4,512,384]{2,1,0:T(8,128)(2,1)}, bf16[8,320,1024]{2,1,0:T(8,128)(2,1)}, f32[512,1024]{1,0:T(8,128)}) custom-call(bf16[2,128,1024]{2,1,0:T(8,128)(2,1)} %tokens.5, bf16[1024,384]{1,0:T(8,128)(2,1)} %get-tuple-element.116.w_qkv, bf16[80,1024]{1,0:T(8,128)(2,1)} %pad_maximum_fusion.6.piece, ...), custom_call_target="tpu_custom_call" | custom-call | flops 30000001024 | bytes 30000000 | tf_op jit(solution)/shard_map/opening/pallas_call | solution.py:1425
  89.1 1.0 dynamic-slice_dynamic-update-slice_fusion
  91.1 0.7 all-gather.7.cloned.1.call-update
  91.8 3.5 all-to-all-start.1
  95.8 3.6 copy.149
  99.4 2.3 copy-done.2
  101.7 1.0 slice.107
  103.3 5.1 fusion.25
  108.4 1.2 pad_add_fusion.scal
  109.7 104.6 %forward_chain.1 = (bf16[4,512,128]{2,1,0:T(8,128)(2,1)}, f32[4,512,1]{2,1,0:T(8,128)}, f32[4,128,1024]{2,1,0:T(8,128)}, bf16[4,512,1024]{2,1,0:T(8,128)(2,1)}, ...) custom-call(s32[5]{0:T(128)} %pad_add_fusion.scal, ...), custom_call_target="tpu_custom_call" | custom-call | flops 20000000000 | bytes 20000000 | tf_op jit(solution)/shard_map/forward_chain/pallas_call | solution.py:692
  214.3 2.1 slice.109
  216.5 1.8 fusion.27
  218.3 54.3 %middle_forward.1 = (f32[2,128,1024]{2,1,0:T(8,128)}, bf16[2,128,1024]{2,1,0:T(8,128)(2,1)}, bf16[8,256,1024]{2,1,0:T(8,128)(2,1)}) custom-call(bf16[4,512,128]{2,1,0:T(8,128)(2,1)} %get-tuple-element.67.mixed, bf16[2,128,1024]{2,1,0:T(8,128)(2,1)} %tokens.5, bf16[1024,1024]{1,0:T(8,128)(2,1)} %bitcast.144, f32[8,1024]{1,0:T(8,128)} %stack.36.vecs), custom_call_target="tpu_custom_call" | custom-call | flops 30000001024 | bytes 30000000 | tf_op jit(solution)/shard_map/middle_forward/pallas_call | solution.py:1141
  272.6 4.6 fusion.32
  277.2 2.0 copy-done.22
  279.2 5.0 convolution_convert_fusion
  284.2 7.8 %fusion.6 = bf16[2048,512]{0,1:T(8,128)(2,1)S(1)} fusion(f32[2048,512]{0,1:T(8,128)} %copy-done.22, bf16[512,1024]{1,0:T(8,128)(2,1)S(1)} %bitcast.154, bf16[2048,1024]{1,0:T(8,128)(2,1)} %all-gather.7.cloned.1.call-done), kind=kOutput, calls=%fused_computation.9 | convolution fusion | flops 2168455168 | bytes 11534336 | tf_op jit(solution)/shard_map/...n,kn->...k/dot_general | solution.py:79
  292.1 2.4 convolution_convert_fusion.3
  294.4 1.1 copy-done.23
  295.5 2.7 convolution_convert_fusion.2
  298.2 1.5 pad_maximum_fusion
  299.8 4.4 convolution_convert_fusion.1
  304.2 45.3 %middle_backward.1 = (f32[2,128,1024]{2,1,0:T(8,128)}, bf16[2,128,1024]{2,1,0:T(8,128)(2,1)}, bf16[4,512,128]{2,1,0:T(8,128)(2,1)}, f32[8,1024]{1,0:T(8,128)}) custom-call(bf16[8,256,1024]{2,1,0:T(8,128)(2,1)} %bitcast.170, f32[2,128,1024]{2,1,0:T(8,128)} %get-tuple-element.68.hidden, bf16[2,128,1024]{2,1,0:T(8,128)(2,1)} %cots.1, ...), custom_call_target="tpu_custom_call" | custom-call | flops 30000001024 | bytes 30000000 | tf_op jit(solution)/shard_map/middle_backward/pallas_call | solution.py:1224
  349.5 1.8 bitcast_convert_fusion
  351.3 1.6 copy.131
  354.1 1.0 convert_bitcast_fusion
  355.1 1.3 constant_dynamic-slice_fusion.1
  356.5 1.2 pad_maximum_fusion.1.states
  357.7 7.2 %copy.132 = bf16[4,2,3,4,32,1024]{5,4,3,2,1,0:T(8,128)(2,1)} copy(bf16[4,2,3,4,32,1024]{5,4,2,0,3,1:T(8,128)(2,1)} %bitcast.132) | data formatting | bytes 12582912 | tf_op jit(solution)/shard_map/transpose | solution.py:2003
  364.9 110.9 %backward_chain.1 = (bf16[4,512,384]{2,1,0:T(8,128)(2,1)}, bf16[4,512,384]{2,1,0:T(8,128)(2,1)}, bf16[4,64,1024]{2,1,0:T(8,128)(2,1)}, f32[64,1024]{1,0:T(8,128)...) custom-call(s32[5]{0:T(128)} %pad_add_fusion.scal, bf16[4,512,384]{2,1,0:T(8,128)(2,1)} %get-tuple-element.62.qkv, ...), custom_call_target="tpu_custom_call" | custom-call | flops 40000000000 | bytes 40000000 | tf_op jit(solution)/shard_map/backward_chain/pallas_call | solution.py:879
  475.9 1.1 fusion.11
  477.0 1.5 collective-permute-start
  478.5 1.2 and_convert_fusion.spots
  479.8 1.1 dynamic-slice_bitcast_fusion
  480.9 5.3 collective-permute-done
  486.2 1.1 maximum_select_fusion
  487.3 0.8 slice.90
  488.0 0.8 fusion.31
  489.6 120.1 %closing.1 = (f32[2,128,1024]{2,1,0:T(8,128)}, bf16[2,4,160,1024]{3,2,1,0:T(8,128)(2,1)}, bf16[8,64,1024]{2,1,0:T(8,128)(2,1)}, f32[8,1024]{1,0:T(8,128)}) custom-call(bf16[4,512,384]{2,1,0:T(8,128)(2,1)} %get-tuple-element.86.d_qkv, bf16[1024,384]{1,0:T(8,128)(2,1)} %get-tuple-element.116.w_qkv, bf16[2,128,1024]{2,1,0:T(8,128)(2,1)} %tokens.5, ...), custom_call_target="tpu_custom_call" | custom-call | flops 30000001024 | bytes 30000000 | tf_op jit(solution)/shard_map/closing/pallas_call | solution.py:1845
  609.7 0.7 slice_reduce_fusion.1
  610.5 1.0 slice.113
  611.5 1.8 fusion.28
  613.4 1.3 copy.143
  614.8 1.3 copy.142
  616.3 1.3 copy.141
  617.8 1.3 copy.140
  620.3 0.9 bitcast_convert_fusion.9
  621.1 1.3 fusion.29
  622.4 1.1 bitcast_convert_fusion.3
  623.5 1.1 bitcast_convert_fusion.5
  624.7 2.0 fusion.10
  626.6 2.7 fusion.26
  629.3 2.6 bitcast_convert_fusion.1
  632.0 2.6 bitcast_convert_fusion.2
  634.5 5.4 copy.137
  639.9 1.0 copy.155
  (101 shorter events, 10.2 us)
Async XLA Ops:
  7.2 6.6 %copy-start = (bf16[1024,1024]{1,0:T(8,128)(2,1)S(1)}, bf16[1024,1024]{1,0:T(8,128)(2,1)}, u32[]{:S(2)}) copy-start(bf16[1024,1024]{1,0:T(8,128)(2,1)} %param.32) | copy-start | bytes 6291460
  7.2 10.7 %copy-start.7 = (bf16[1024,256]{1,0:T(8,128)(2,1)S(1)}, bf16[1024,256]{1,0:T(8,128)(2,1)}, u32[]{:S(2)}) copy-start(bf16[1024,256]{1,0:T(8,128)(2,1)} %param.27) | copy-start | bytes 1572868
  7.2 10.7 %copy-start.11 = (bf16[1024,256]{1,0:T(8,128)(2,1)S(1)}, bf16[1024,256]{1,0:T(8,128)(2,1)}, u32[]{:S(2)}) copy-start(bf16[1024,256]{1,0:T(8,128)(2,1)} %param.26) | copy-start | bytes 1572868
  7.2 10.7 %copy-start.18 = (f32[32,2]{0,1:T(2,128)S(1)}, f32[32,2]{0,1:T(2,128)}, u32[]{:S(2)}) copy-start(f32[32,2]{0,1:T(2,128)} %param.34) | copy-start | bytes 772
  8.8 81.3 %all-to-all-start = ((s32[4,1,128]{2,1,0:T(1,128)}), s32[4,1,128]{2,1,0:T(1,128)S(1)}, u32[]{:S(2)}, u32[]{:S(2)}) async-start(s32[4,1,128]{2,1,0:T(1,128)} %broadcast_in_dim.46), calls=%async_computation | async-start | bytes 4096 | tf_op jit(solution)/shard_map/all_to_all | solution.py:1890
  13.1 201.2 %all-gather.5.cloned.1.call-start = ((), (), s32[]{:S(2)}) async-start(), calls=%async_computation.5 | async-start | bytes 3604480 | tf_op jit(solution)/shard_map/all_gather | solution.py:1973
  13.1 8.8 %copy-start.12 = (s32[2048]{0:T(1024)}, s32[2048]{0:T(1024)S(1)}, u32[]{:S(2)}) copy-start(s32[2048]{0:T(1024)S(1)} %fusion.21) | copy-start | bytes 24580
  15.1 6.7 %copy-start.15 = (f32[1024]{0:T(1024)S(1)}, f32[1024]{0:T(1024)}, u32[]{:S(2)}) copy-start(f32[1024]{0:T(1024)} %param.24) | copy-start | bytes 12292
  15.2 6.7 %copy-start.16 = (f32[1024]{0:T(1024)S(1)}, f32[1024]{0:T(1024)}, u32[]{:S(2)}) copy-start(f32[1024]{0:T(1024)} %param.25) | copy-start | bytes 12292
  15.2 6.7 %copy-start.17 = (f32[1024]{0:T(1024)S(1)}, f32[1024]{0:T(1024)}, u32[]{:S(2)}) copy-start(f32[1024]{0:T(1024)} %param.23) | copy-start | bytes 12292
  21.9 67.2 %copy-start.9 = (f32[4,1024]{1,0:T(4,128)}, f32[4,1024]{1,0:T(4,128)S(1)}, u32[]{:S(2)}) copy-start(f32[4,1024]{1,0:T(4,128)S(1)} %broadcast.144) | copy-start | bytes 49156
  90.1 0.9 copy-start.5
  91.0 193.2 %all-gather.7.cloned.1.call-start = ((), (), s32[]{:S(2)}) async-start(), calls=%async_computation.6 | async-start | bytes 4718592 | tf_op jit(solution)/shard_map/all_gather | solution.py:1939
  91.8 124.6 %all-to-all-start.1 = ((bf16[4,64,1024]{2,1,0:T(8,128)(2,1)}), bf16[4,64,1024]{2,1,0:T(8,128)(2,1)S(1)}, u32[]{:S(2)}, u32[]{:S(2)}) async-start(bf16[4,64,1024]{2,1,0:T(8,128)(2,1)} %bitcast.16), calls=%async_computation.1 | async-start | bytes 1048576 | tf_op jit(solution)/shard_map/all_to_all | solution.py:1890
  95.3 208.9 %all-gather.9.cloned.1.call-start = ((), (), s32[]{:S(2)}) async-start(), calls=%async_computation.7 | async-start | bytes 7077888 | tf_op jit(solution)/shard_map/all_gather | solution.py:1993
  95.8 7.0 %copy-start.20 = (s32[2]{0:T(128)S(1)}, s32[2]{0:T(128)}, u32[]{:S(2)}) copy-start(s32[2]{0:T(128)} %param.21) | copy-start | bytes 28
  99.4 2.3 copy-start.2
  216.4 56.2 %copy-start.6 = (bf16[4,64,1024]{2,1,0:T(8,128)(2,1)}, bf16[4,64,1024]{2,1,0:T(8,128)(2,1)S(1)}, u32[]{:S(2)}) copy-start(bf16[4,64,1024]{2,1,0:T(8,128)(2,1)S(1)} %all-to-all-done.1.cots) | copy-start | bytes 1572868
  216.4 259.4 %reduce-scatter.8.cloned.1.call-start = ((), (), s32[]{:S(2)}) async-start(), calls=%async_computation.10 | async-start | bytes 2359296 | tf_op jit(solution)/shard_map/reduce_scatter | solution.py:2025
  277.2 2.0 copy-start.22
  284.2 7.8 %copy-start.21 = (bf16[8,256,1024]{2,1,0:T(8,128)(2,1)S(1)}, bf16[8,256,1024]{2,1,0:T(8,128)(2,1)}, u32[]{:S(2)}) copy-start(bf16[8,256,1024]{2,1,0:T(8,128)(2,1)} %get-tuple-element.69) | copy-start | bytes 12582916
  292.0 2.4 copy-start.19
  292.1 3.5 copy-start.23
  304.2 45.3 %copy-start.8 = (bf16[2,128,1024]{2,1,0:T(8,128)(2,1)S(1)}, bf16[2,128,1024]{2,1,0:T(8,128)(2,1)}, u32[]{:S(2)}) copy-start(bf16[2,128,1024]{2,1,0:T(8,128)(2,1)} %get-tuple-element.73) | copy-start | bytes 1572868
  352.9 123.0 %reduce-scatter.6.cloned.1.call-start = ((), (), s32[]{:S(2)}) async-start(), calls=%async_computation.9 | async-start | bytes 2621440 | tf_op jit(solution)/shard_map/reduce_scatter | solution.py:2022
  353.5 271.2 %reduce-scatter.4.cloned.1.call-start = ((), (), s32[]{:S(2)}) async-start(), calls=%async_computation.8 | async-start | bytes 4718592 | tf_op jit(solution)/shard_map/reduce_scatter | solution.py:2021
  354.1 272.6 %all-gather.11.cloned.1.call-start = ((), (), s32[]{:S(2)}) async-start(), calls=%async_computation.11 | async-start | bytes 4718592 | tf_op jit(solution)/shard_map/all_gather | solution.py:2036
  364.8 113.7 %copy-start.13 = (s32[2048]{0:T(1024)S(1)}, s32[2048]{0:T(1024)}, u32[]{:S(2)}) copy-start(s32[2048]{0:T(1024)} %copy-done.12) | copy-start | bytes 24580
  475.8 13.1 %copy-start.10 = (f32[4,1024]{1,0:T(4,128)S(1)}, f32[4,1024]{1,0:T(4,128)}, u32[]{:S(2)}) copy-start(f32[4,1024]{1,0:T(4,128)} %copy-done.9) | copy-start | bytes 49156
  477.0 9.1 %collective-permute-start = (bf16[128,1024]{1,0:T(8,128)(2,1)S(1)}, bf16[128,1024]{1,0:T(8,128)(2,1)S(1)}, u32[]{:S(2)}, u32[]{:S(2)}) collective-permute-start(bf16[128,1024]{1,0:T(8,128)(2,1)S(1)} %fusion.11), channel_id=1, source_target_pairs={{0,8},{4,12},{8,0},{12,4},{1,9},{5,13},{9,1},{13,5},{2,10},{6,14},... | collective-permute-start | bytes 786440 | tf_op jit(solution)/shard_map/ppermute | solution.py:1982
  616.2 3.5 copy-start.14
  617.8 6.9 %copy-start.3 = (f32[2,128,1024]{2,1,0:T(8,128)S(1)}, f32[2,128,1024]{2,1,0:T(8,128)}, u32[]{:S(2)}) copy-start(f32[2,128,1024]{2,1,0:T(8,128)} %get-tuple-element.68.hidden) | copy-start | bytes 3145732
  632.0 9.0 %copy-start.1 = (bf16[1024,1024]{1,0:T(8,128)(2,1)S(1)}, bf16[1024,1024]{1,0:T(8,128)(2,1)}, u32[]{:S(2)}) copy-start(bf16[1024,1024]{1,0:T(8,128)(2,1)} %param.32) | copy-start | bytes 6291460
  634.5 5.4 copy-start.4
Sparse Core Ops, SparseCore 0:
  91.1 80.9 all-gather.4
  174.0 34.9 all-gather.6
  216.6 60.4 all-gather.8
  353.0 39.6 reduce-scatter.7
  395.0 58.5 reduce-scatter.5
  457.3 57.4 reduce-scatter.3
  516.8 55.1 all-gather.10
